TPU v7x, 32 devices: a whole 2x2x4 slice. The times are simulated.
32 devices in a mesh: leaf: 16 (over z, y, x), col: 2 (over core).
Axes of the slice: x: 2, y: 2, z: 4, core: 2. Of those that a mesh axis runs over, the one named last changes fastest.
Arguments:
- sources: bfloat16 [65536, 256], P('leaf', 'col'), may hold values from -6 to 6
- near_tiles: bfloat16 [256, 8, 256, 256], P('leaf', 'col'), may hold values from -0.125 to 0.125
- near_index: int32 [256, 8], P('leaf'), may hold values from 0 to 255, as said below
- near_count: int32 [256], P('leaf'), may hold values from 1 to 8, as said below
- leaf_basis: bfloat16 [256, 64, 256], P('leaf'), may hold values from -0.375 to 0.375
- leaf_coupling: bfloat16 [256, 64, 256], P('leaf'), may hold values from -0.375 to 0.375
- leaf_far: int32 [256, 4], P('leaf'), may hold values from 0 to 255, as said below
- up_leaf: bfloat16 [32, 64, 512], P('leaf'), may hold values from -0.25 to 0.25
- mid_coupling: bfloat16 [32, 64, 256], P('leaf'), may hold values from -0.375 to 0.375
- mid_far: int32 [32, 4], P('leaf'), may hold values from 0 to 31, as said below
- up_mid: bfloat16 [32, 64, 64], P('leaf'), may hold values from -0.75 to 0.75
- top_coupling: bfloat16 [4, 64, 256], replicated, may hold values from -0.4375 to 0.4375
Outputs:
- product: float32 [65536, 256], P('leaf', 'col')
Inputs may be any that keep to these rules, and one draw needn't show every extreme that they name: `near_index`: entry 0 of row i is i; the other 7 entries are distinct leaves j with j != i and |i - j| <= 8. Only the first near_count[i] slots of leaf i count; some leaf has all 8. `leaf_far`: row i holds 4 distinct leaves j != i with |i // 8 - j // 8| <= 1. `mid_far`: row a holds 4 distinct middle clusters b != a with |a // 8 - b // 8| <= 1.
All inputs are finite; a program needn't handle non-finite values.
Results may differ from a plain program's by a relative error of at most 0.01.
Values may be sent and summed in bfloat16 or wider, within the bound.
No kernel may reach another device: no remote copies, remote signals or barrier semaphores. Data moves between devices by JAX's collectives and lax.ppermute only.
A program may use at most 128 MiB of HBM per device.

v0:
```python
import jax
import jax.numpy as jnp
from jax import lax
from jax.experimental import pallas as pl
from jax.experimental.pallas import tpu as pltpu
from jax.sharding import PartitionSpec as P


CHILD = 8
FAR = 4
BATCH = 4

F32 = jnp.float32
BF16 = jnp.bfloat16
VMEM = pl.BlockSpec(memory_space=pltpu.VMEM)
SMEM = pl.BlockSpec(memory_space=pltpu.SMEM)
HBM = pl.BlockSpec(memory_space=pltpu.HBM)
ANY = pl.BlockSpec(memory_space=pl.ANY)


def mm(a, b):
    return jnp.dot(a, b, preferred_element_type=F32)


def mm_t(a, b):
    return lax.dot_general(a, b, (((0,), (0,)), ((), ())), preferred_element_type=F32)


def cost(flops, nbytes):
    return pl.CostEstimate(flops=flops, transcendentals=0, bytes_accessed=nbytes)


def params(mib):
    return pltpu.CompilerParams(vmem_limit_bytes=mib << 20)


def in_vmem(x):
    return pltpu.with_memory_space_constraint(x, pltpu.VMEM)


def in_hbm(x):
    return pltpu.with_memory_space_constraint(x, pltpu.HBM)


def blocks(start, count, size):
    return pl.ds(pl.multiple_of(start * size, size), count * size)


def upward(
    src_hbm, basis_hbm, up_leaf_hbm, up_mid_hbm,
    pack, half1, coef2, half2, coef,
    src, basis, up_leaf, up_mid, sems,
):
    loads = [
        pltpu.make_async_copy(a, b, sems.at[k])
        for k, (a, b) in enumerate(
            ((src_hbm, src), (basis_hbm, basis), (up_leaf_hbm, up_leaf), (up_mid_hbm, up_mid))
        )
    ]
    for load in loads:
        load.start()
    leaves, rank, leaf = basis.shape
    mids = up_leaf.shape[0]
    odd = lax.rem(lax.axis_index("leaf"), 2)
    for load in loads:
        load.wait()
    for i in range(leaves):
        coef[pl.ds(i * rank, rank), :] = mm(basis[i], src[pl.ds(i * leaf, leaf), :]).astype(BF16)
    total = None
    for q in range(mids):
        mid = mm(up_leaf[q], coef[pl.ds(q * CHILD * rank, CHILD * rank), :]).astype(BF16)
        pack[pl.ds(q * rank, rank), :] = mid
        lift = mm(up_mid[q], mid).astype(BF16).astype(F32)
        total = lift if total is None else total + lift
    pack[pl.ds(mids * rank, rank), :] = total.astype(BF16)
    first = (1 - odd) * (leaves - CHILD)
    second = odd * (leaves - CHILD)
    half1[...] = src[blocks(first, CHILD, leaf), :]
    half2[...] = src[blocks(second, CHILD, leaf), :]
    pack[pl.ds((mids + 1) * rank, CHILD * rank), :] = coef[blocks(first, CHILD, rank), :]
    coef2[...] = coef[blocks(second, CHILD, rank), :]


def prepare(index, count, tiles_hbm, tiles, work, sem):
    load = pltpu.make_async_copy(tiles_hbm, tiles, sem)
    load.start()
    leaves, slots = tiles.shape[:2]
    room = work.shape[1]
    device = lax.axis_index("leaf")
    odd = lax.rem(device, 2)
    core = lax.axis_index("col")
    first = device * leaves
    base = odd * (leaves - CHILD)

    def clear(n, _):
        for r in range(2):
            work[3 * r, n] = 0
            work[3 * r + 1, n] = 0
            work[3 * r + 2, n] = CHILD
        return 0

    lax.fori_loop(0, room, clear, 0)

    for r, owner in ((0, core), (1, 1 - core)):

        def note(n, found):
            row = n // slots
            k = lax.rem(n, slots)
            slot = owner * slots + k
            at = index[slot, base + row] - first
            outside = jnp.where(odd == 1, at - leaves, at + CHILD)
            use = (slot < count[base + row]) & (outside >= 0) & (outside < CHILD)

            @pl.when(use)
            def _():
                work[3 * r, found] = (base + row) * slots + k
                work[3 * r + 1, found] = outside
                work[3 * r + 2, found] = row

            return found + use.astype(jnp.int32)

        work[6, r] = lax.fori_loop(0, CHILD * slots, note, jnp.int32(0))
    load.wait()


def near_part(index, count, tiles, other, window, out, base, lowest, highest, zero):
    slots, leaf = tiles.shape[1:3]
    leaves = tiles.shape[0]
    first = lax.axis_index("leaf") * leaves
    core = lax.axis_index("col")

    def body(n, _):
        i = base + n
        live = count[i]
        acc = None
        for held, mine in ((tiles, core), (other, 1 - core)):
            for k in range(slots):
                slot = mine * slots + k
                at = index[slot, i] - first
                use = (slot < live) & (at >= lowest) & (at < highest)
                place = jnp.where(use, at - lowest, zero)
                part = mm(held[i, k], window[blocks(place, 1, leaf), :])
                acc = part if acc is None else acc + part
        out[blocks(n, 1, leaf), :] = acc
        return 0

    lax.fori_loop(0, CHILD, body, 0, unroll=2)


def near_own(index, count, tiles, other, src, out, window):
    leaves, _, leaf, _ = tiles.shape
    odd = lax.rem(lax.axis_index("leaf"), 2)
    window[pl.ds(0, leaves * leaf), :] = src[...]
    window[pl.ds(leaves * leaf, leaf), :] = jnp.zeros((leaf, src.shape[1]), BF16)
    near_part(index, count, tiles, other, window, out, odd * (leaves - CHILD), 0, leaves, leaves)


def near_first(index, count, tiles, other, src, half1, out, window):
    leaves, _, leaf, _ = tiles.shape
    odd = lax.rem(lax.axis_index("leaf"), 2)
    total = leaves + CHILD
    window[blocks(odd * CHILD, leaves, leaf), :] = src[...]
    window[blocks((1 - odd) * leaves, CHILD, leaf), :] = half1[...]
    window[pl.ds(total * leaf, leaf), :] = jnp.zeros((leaf, src.shape[1]), BF16)
    lowest = -odd * CHILD
    near_part(
        index, count, tiles, other, window, out,
        (1 - odd) * (leaves - CHILD), lowest, lowest + total, total,
    )


def downward(
    leaf_far, mid_far,
    near1, near2, coef, pack1, coef2, plane, before, after, tops,
    basis, leaf_coupling, up_leaf, mid_coupling, up_mid, top_coupling,
    out, acc2,
    full, window, chosen, stack, sem,
):
    leaves, rank, leaf = basis.shape
    mids = up_leaf.shape[0]
    group = CHILD // mids
    total_top = top_coupling.shape[0]
    device = lax.axis_index("leaf")
    odd = lax.rem(device, 2)
    parent = device // group
    member = lax.rem(device, group)
    top_row = CHILD * rank

    def put_top(value, ahead):
        at = lax.rem(parent + ahead, total_top)
        stack[blocks(at, 1, rank), :] = value

    put_top(jnp.zeros((rank, full.shape[1]), BF16), 0)
    put_top(before[pl.ds(top_row, rank), :], total_top - 1)
    put_top(after[pl.ds(top_row, rank), :], 1)
    for k in range(total_top - 3):
        put_top(tops[pl.ds(k * rank, rank), :], 2 + k)
    top_field = mm(top_coupling[parent], stack[...]).astype(BF16)

    window[pl.ds(CHILD * rank, leaves * rank), :] = coef[...]
    right = CHILD + leaves
    window[blocks((1 - odd) * right, CHILD, rank), :] = pack1[pl.ds((mids + 1) * rank, CHILD * rank), :]
    window[blocks(odd * right, CHILD, rank), :] = coef2[...]

    for q in range(mids):
        for f in range(FAR):
            b = mid_far[q, f]
            top = b // CHILD
            inside = lax.rem(b, CHILD)
            place = jnp.bitwise_xor(inside // mids, member) * mids + lax.rem(inside, mids)
            row = blocks(place, 1, rank)
            to = pl.ds(f * rank, rank)

            @pl.when(top == parent)
            def _():
                chosen[to, :] = plane[row, :]

            @pl.when(top < parent)
            def _():
                chosen[to, :] = before[row, :]

            @pl.when(top > parent)
            def _():
                chosen[to, :] = after[row, :]

        mid_field = (mm(mid_coupling[q], chosen[...]) + mm_t(up_mid[q], top_field)).astype(BF16)
        down = mm_t(up_leaf[q], mid_field)
        for k in range(CHILD):
            i = q * CHILD + k
            picked = [
                window[blocks(leaf_far[f, i] - (device * leaves - CHILD), 1, rank), :]
                for f in range(FAR)
            ]
            field = mm(leaf_coupling[i], jnp.concatenate(picked, axis=0)) + down[k * rank : (k + 1) * rank, :]
            full[pl.ds(i * leaf, leaf), :] = mm_t(basis[i], field.astype(BF16))

    rows1 = blocks((1 - odd) * (leaves - CHILD), CHILD, leaf)
    rows2 = blocks(odd * (leaves - CHILD), CHILD, leaf)
    full[rows1, :] += near1[...]
    store = pltpu.make_async_copy(full.at[rows1], out.at[rows1], sem)
    store.start()
    acc2[...] = full[rows2, :] + near2[...]
    store.wait()


def near_last(work, tiles, other, half2, acc2, out_in, out, acc, sem):
    leaves, slots, leaf, _ = tiles.shape
    odd = lax.rem(lax.axis_index("leaf"), 2)
    acc[pl.ds(0, CHILD * leaf), :] = acc2[...]

    def step(t, _):
        for b in range(BATCH):
            for r, held in ((0, tiles), (1, other)):
                n = t * BATCH + b
                tile = work[3 * r, n]
                part = mm(held[tile // slots, lax.rem(tile, slots)], half2[blocks(work[3 * r + 1, n], 1, leaf), :])
                acc[blocks(work[3 * r + 2, n], 1, leaf), :] += part
        return 0

    longest = jnp.maximum(work[6, 0], work[6, 1])
    lax.fori_loop(0, (longest + BATCH - 1) // BATCH, step, 0)
    rows = blocks(odd * (leaves - CHILD), CHILD, leaf)
    store = pltpu.make_async_copy(acc.at[pl.ds(0, CHILD * leaf)], out.at[rows], sem)
    store.start()
    store.wait()


def shards(
    sources,
    near_tiles,
    near_index,
    near_count,
    leaf_basis,
    leaf_coupling,
    leaf_far,
    up_leaf,
    mid_coupling,
    mid_far,
    up_mid,
    top_coupling,
):
    sds = jax.ShapeDtypeStruct
    leaves, rank, leaf = leaf_basis.shape
    mids = up_leaf.shape[0]
    cols = sources.shape[1]
    slots = near_tiles.shape[1]
    total_top = top_coupling.shape[0]
    devices = lax.axis_size("leaf")
    group = CHILD // mids
    edge = CHILD * leaf
    edge_c = CHILD * rank
    rows = leaves * leaf
    assert leaves == 2 * CHILD and group >= 2 and total_top >= 4
    product_flops = 2 * leaf * leaf * cols

    pair = [(i, i ^ 1) for i in range(devices)]
    rest = [(i, i + 1) for i in range(1, devices - 1, 2)]
    rest = rest + [(j, i) for i, j in rest]

    def shift(k):
        return [(i, (i + k * group) % devices) for i in range(devices)]

    def send(x, pairs, axis="leaf"):
        return lax.ppermute(x, axis, pairs)

    def call(kernel, out_shape, in_specs, out_specs, scratch, mib, estimate, **more):
        def run(*args):
            return pl.pallas_call(
                kernel,
                out_shape=out_shape,
                in_specs=in_specs,
                out_specs=out_specs,
                scratch_shapes=scratch,
                compiler_params=params(mib),
                cost_estimate=estimate,
                **more,
            )(*args)

        return run

    other = in_vmem(send(near_tiles, [(0, 1), (1, 0)], "col"))

    pack, half1, coef2, half2, coef = call(
        upward,
        (
            sds(((mids + 1) * rank + edge_c, cols), BF16),
            sds((edge, cols), BF16),
            sds((edge_c, cols), BF16),
            sds((edge, cols), BF16),
            sds((leaves * rank, cols), BF16),
        ),
        [HBM] * 4,
        (VMEM,) * 5,
        [
            pltpu.VMEM(sources.shape, BF16),
            pltpu.VMEM(leaf_basis.shape, BF16),
            pltpu.VMEM(up_leaf.shape, BF16),
            pltpu.VMEM(up_mid.shape, BF16),
            pltpu.SemaphoreType.DMA((4,)),
        ],
        8,
        cost(2 * leaves * rank * leaf * cols, 4 << 20),
    )(*map(in_hbm, (sources, leaf_basis, up_leaf, up_mid)))

    pack1 = send(pack, pair)
    half1 = send(half1, pair)

    index = near_index.T
    most = CHILD * slots
    tiles, work = call(
        prepare,
        (sds(near_tiles.shape, BF16), sds((7, most + BATCH), jnp.int32)),
        [SMEM, SMEM, HBM],
        (VMEM, SMEM),
        [pltpu.SemaphoreType.DMA],
        12,
        cost(0, near_tiles.size * 2),
    )(index, near_count, in_hbm(near_tiles))
    tiles = in_vmem(tiles)

    held = mids * rank
    plane = jnp.concatenate([pack[:held], pack1[:held]], axis=0)
    total = pack[held : held + rank].astype(F32) + pack1[held : held + rank].astype(F32)
    total = total.astype(BF16)
    k = 2
    while k < group:
        mine = jnp.concatenate([plane, total], axis=0)
        got = send(mine, [(i, i ^ k) for i in range(devices)])
        held = plane.shape[0]
        plane = jnp.concatenate([plane, got[:held]], axis=0)
        total = (total.astype(F32) + got[held:].astype(F32)).astype(BF16)
        k *= 2
    plane = jnp.concatenate([plane, total], axis=0)
    before = send(plane, shift(1))
    after = send(plane, shift(-1))
    tops = [send(total, shift(-k)) for k in range(2, total_top - 1)]
    tops = tops[0] if len(tops) == 1 else jnp.concatenate(tops, axis=0)

    coef2 = send(coef2, rest)
    half2 = send(half2, rest)

    near2 = call(
        near_own,
        sds((edge, cols), F32),
        [SMEM, SMEM, VMEM, VMEM, VMEM],
        VMEM,
        [pltpu.VMEM((rows + leaf, cols), BF16)],
        8,
        cost(CHILD * 2 * slots * product_flops, 16 << 20),
    )(index, near_count, tiles, other, sources)

    near1 = call(
        near_first,
        sds((edge, cols), F32),
        [SMEM, SMEM, VMEM, VMEM, VMEM, VMEM],
        VMEM,
        [pltpu.VMEM((rows + edge + leaf, cols), BF16)],
        8,
        cost(CHILD * 2 * slots * product_flops, 16 << 20),
    )(index, near_count, tiles, other, sources, half1)

    out, acc2 = call(
        downward,
        (sds((rows, cols), F32), sds((edge, cols), F32)),
        [SMEM] * 2 + [VMEM] * 15,
        (ANY, VMEM),
        [
            pltpu.VMEM((rows, cols), F32),
            pltpu.VMEM((2 * edge_c + leaves * rank, cols), BF16),
            pltpu.VMEM((FAR * rank, cols), BF16),
            pltpu.VMEM((total_top * rank, cols), BF16),
            pltpu.SemaphoreType.DMA,
        ],
        20,
        cost(leaves * 4 * product_flops, 12 << 20),
    )(
        leaf_far.T, mid_far,
        near1, near2, coef, pack1, coef2, plane, before, after, tops,
        leaf_basis, leaf_coupling, up_leaf, mid_coupling, up_mid, top_coupling,
    )

    return call(
        near_last,
        sds((rows, cols), F32),
        [SMEM, VMEM, VMEM, VMEM, VMEM, ANY],
        ANY,
        [pltpu.VMEM((edge + leaf, cols), F32), pltpu.SemaphoreType.DMA],
        8,
        cost(leaves * slots * product_flops, 4 << 20),
        input_output_aliases={5: 0},
    )(work, tiles, other, half2, acc2, out)


def solution(mesh):


    return jax.shard_map(
        shards,
        mesh=mesh,
        in_specs=(
            P("leaf", "col"),
            P("leaf", "col", None, None),
            P("leaf", None),
            P("leaf"),
            P("leaf", None, None),
            P("leaf", None, None),
            P("leaf", None),
            P("leaf", None, None),
            P("leaf", None, None),
            P("leaf", None),
            P("leaf", None, None),
            P(),
        ),
        out_specs=P("leaf", "col"),
        check_vma=False,
    )
```

profile of v0, /device:TPU:0, one launch (start us, length us, event | category | flops | bytes accessed | tf_op | source)
XLA Modules:
  0.0 47.5 jit_solution(7082369312311082038)
XLA Ops:
  0.0 0.5 %collective-permute-start = (bf16[16,4,256,256]{3,2,1,0:T(8,128)(2,1)}, bf16[16,4,256,256]{3,2,1,0:T(8,128)(2,1)S(1)}, u32[]{:S(2)}, u32[]{:S(2)}) collective-permute-start(bf16[16,4,256,256]{3,2,1,0:T(8,128)(2,1)} %tiles_hbm.1), channel_id=1, source_target_pairs={{0,1},{1,0},{2,3},{3,2},{4,5},{5,4},{6,7},{7,6},{8,9},{9,8},{10,11... | collective-permute-start | bytes 25165832 | tf_op jit(solution)/shard_map/ppermute | solution.py:304
  0.5 2.1 %shard_map.119 = (bf16[704,128]{1,0:T(8,128)(2,1)S(1)}, bf16[2048,128]{1,0:T(8,128)(2,1)S(1)}, bf16[512,128]{1,0:T(8,128)(2,1)S(1)}, bf16[2048,128]{1,0:T(8,128)(2,1)S(1)}, bf16[1024,128]{1,0:T(8,128)(2,1)S(1)}) custom-call(bf16[4096,128]{1,0:T(8,128)(2,1)} %src.3, bf16[16,64,256]{2,1,0:T(8,128)(2,1)} %basis.1, bf16[2,64,512]{2,1,0:T(8,128)(2,1)} %up_leaf.1, ...), custom_call_target="tpu_custom_call" | custom-call | flops 67108864 | bytes 4194304 | tf_op jit(solution)/shard_map/pallas_call | solution.py:308
  2.6 2.6 %collective-permute-start.3 = (bf16[704,128]{1,0:T(8,128)(2,1)S(1)}, bf16[704,128]{1,0:T(8,128)(2,1)S(1)}, u32[]{:S(2)}, u32[]{:S(2)}) collective-permute-start(bf16[704,128]{1,0:T(8,128)(2,1)S(1)} %get-tuple-element.19), channel_id=1, source_target_pairs={{0,2},{2,0},{4,6},{6,4},{8,10},{10,8},{12,14},{14,12},{16,18},{18,... | collective-permute-start | bytes 540680 | tf_op jit(solution)/shard_map/ppermute | solution.py:304
  5.2 0.1 collective-permute-start.2
  5.3 5.3 %collective-permute-done.3.pack1 = bf16[704,128]{1,0:T(8,128)(2,1)S(1)} collective-permute-done((bf16[704,128]{1,0:T(8,128)(2,1)S(1)}, bf16[704,128]{1,0:T(8,128)(2,1)S(1)}, u32[]{:S(2)}, u32[]{:S(2)}) %collective-permute-start.3) | collective-permute-done | bytes 180256 | tf_op jit(solution)/shard_map/ppermute | solution.py:304
  10.7 2.1 %collective-permute-start.5 = (bf16[320,128]{1,0:T(8,128)(2,1)S(1)}, bf16[320,128]{1,0:T(8,128)(2,1)S(1)}, u32[]{:S(2)}, u32[]{:S(2)}) collective-permute-start(bf16[320,128]{1,0:T(8,128)(2,1)S(1)} %pad_maximum_fusion.1), channel_id=1, source_target_pairs={{0,4},{2,6},{4,0},{6,2},{8,12},{10,14},{12,8},{14,10},{16,20},{18,... | collective-permute-start | bytes 245768 | tf_op jit(solution)/shard_map/ppermute | solution.py:304
  12.8 0.7 %collective-permute-start.4 = (bf16[512,128]{1,0:T(8,128)(2,1)S(1)}, bf16[512,128]{1,0:T(8,128)(2,1)S(1)}, u32[]{:S(2)}, u32[]{:S(2)}) collective-permute-start(bf16[512,128]{1,0:T(8,128)(2,1)S(1)} %get-tuple-element.20), channel_id=1, source_target_pairs={{2,4},{6,8},{10,12},{14,16},{18,20},{22,24},{26,28},{4,2},{8,6},{1... | collective-permute-start | bytes 393224 | tf_op jit(solution)/shard_map/ppermute | solution.py:304
  13.5 0.7 %collective-permute-start.1 = (bf16[2048,128]{1,0:T(8,128)(2,1)S(1)}, bf16[2048,128]{1,0:T(8,128)(2,1)S(1)}, u32[]{:S(2)}, u32[]{:S(2)}) collective-permute-start(bf16[2048,128]{1,0:T(8,128)(2,1)S(1)} %get-tuple-element.16), channel_id=1, source_target_pairs={{2,4},{6,8},{10,12},{14,16},{18,20},{22,24},{26,28},{4,2},{8,6},{1... | collective-permute-start | bytes 1572872 | tf_op jit(solution)/shard_map/ppermute | solution.py:304
  14.2 0.0 copy-start.7
  14.2 0.7 %copy-done.7 = s32[16,8]{0,1:T(8,128)S(1)} copy-done((s32[16,8]{0,1:T(8,128)S(1)}, s32[16,8]{0,1:T(8,128)}, u32[]{:S(2)}) %copy-start.7) | copy-done | bytes 536
  14.9 0.7 %copy-done.8 = s32[16]{0:T(128)S(1)} copy-done((s32[16]{0:T(128)S(1)}, s32[16]{0:T(128)}, u32[]{:S(2)}) %copy-start.8) | copy-done | bytes 88
  15.5 4.6 %shard_map.118 = (bf16[16,4,256,256]{3,2,1,0:T(8,128)(2,1)S(1)}, s32[7,36]{1,0:T(8,128)S(1)}) custom-call(s32[8,16]{1,0:T(8,128)S(1)} %bitcast.2, s32[16]{0:T(128)S(1)} %copy-done.8, bf16[16,4,256,256]{3,2,1,0:T(8,128)(2,1)} %tiles_hbm.1), custom_call_target="tpu_custom_call" | custom-call | bytes 8388608 | tf_op jit(solution)/shard_map/pallas_call | solution.py:308
  20.2 9.9 %collective-permute-start.7 = (bf16[576,128]{1,0:T(8,128)(2,1)S(1)}, bf16[576,128]{1,0:T(8,128)(2,1)S(1)}, u32[]{:S(2)}, u32[]{:S(2)}) collective-permute-start(bf16[576,128]{1,0:T(8,128)(2,1)S(1)} %pad_maximum_fusion.plane), channel_id=1, source_target_pairs={{0,24},{2,26},{4,28},{6,30},{8,0},{10,2},{12,4},{14,6},{16,8},{18,... | collective-permute-start | bytes 442376 | tf_op jit(solution)/shard_map/ppermute | solution.py:304
  30.2 0.0 collective-permute-done.other
  30.2 0.0 collective-permute-start.6
  30.2 3.6 %shard_map.121.near2 = f32[2048,128]{1,0:T(8,128)S(1)} custom-call(s32[8,16]{1,0:T(8,128)S(1)} %bitcast.3, s32[16]{0:T(128)S(1)} %copy-done.9, bf16[16,4,256,256]{3,2,1,0:T(8,128)(2,1)S(1)} %get-tuple-element.15.tiles, bf16[16,4,256,256]{3,2,1,0:T(8,128)(2,1)S(1)} %collective-permute-done.other, bf16[4096,128]{1,0:T(8,128)(2,1)S(1)} %copy-done), custom_call_target="tpu_custom_call" | custom-call | flops 1073741824 | bytes 16777216 | tf_op jit(solution)/shard_map/pallas_call | solution.py:308
  33.7 0.0 copy-start.1
  33.8 0.0 copy-start.2
  33.8 0.0 copy-start.3
  33.8 0.0 copy-start.4
  33.8 0.0 copy-start.5
  33.8 0.0 copy-start.6
  33.8 0.0 copy-start.10
  33.8 0.0 copy-start.11
  33.8 1.1 %collective-permute-done.2.half1 = bf16[2048,128]{1,0:T(8,128)(2,1)S(1)} collective-permute-done((bf16[2048,128]{1,0:T(8,128)(2,1)S(1)}, bf16[2048,128]{1,0:T(8,128)(2,1)S(1)}, u32[]{:S(2)}, u32[]{:S(2)}) %collective-permute-start.2) | collective-permute-done | bytes 524320 | tf_op jit(solution)/shard_map/ppermute | solution.py:304
  34.9 2.6 %collective-permute-start.8 = (bf16[64,128]{1,0:T(8,128)(2,1)S(1)}, bf16[64,128]{1,0:T(8,128)(2,1)S(1)}, u32[]{:S(2)}, u32[]{:S(2)}) collective-permute-start(bf16[64,128]{1,0:T(8,128)(2,1)S(1)} %add_convert_fusion), channel_id=1, source_target_pairs={{0,16},{2,18},{4,20},{6,22},{8,24},{10,26},{12,28},{14,30},{16,0},... | collective-permute-start | bytes 49160 | tf_op jit(solution)/shard_map/ppermute | solution.py:304
  37.5 3.6 %shard_map.120.near1 = f32[2048,128]{1,0:T(8,128)S(1)} custom-call(s32[8,16]{1,0:T(8,128)S(1)} %bitcast.4, s32[16]{0:T(128)S(1)} %copy-done.9, bf16[16,4,256,256]{3,2,1,0:T(8,128)(2,1)S(1)} %get-tuple-element.15.tiles, bf16[16,4,256,256]{3,2,1,0:T(8,128)(2,1)S(1)} %collective-permute-done.other, bf16[4096,128]{1,0:T(8,128)(2,1)S(1)} %copy-done, ...), custom_call_target="tpu_custom_call" | custom-call | flops 1073741824 | bytes 16777216 | tf_op jit(solution)/shard_map/pallas_call | solution.py:308
  41.1 0.0 collective-permute-done.8.tops
  41.1 0.0 collective-permute-done.7.after
  41.2 4.6 %shard_map.122 = (f32[4096,128]{1,0:T(8,128)}, f32[2048,128]{1,0:T(8,128)S(1)}) custom-call(s32[4,16]{1,0:T(4,128)S(1)} %bitcast.5, s32[2,4]{1,0:T(2,128)S(1)} %copy-done.11, f32[2048,128]{1,0:T(8,128)S(1)} %shard_map.120.near1, f32[2048,128]{1,0:T(8,128)S(1)} %shard_map.121.near2, bf16[1024,128]{1,0:T(8,128)(2,1)S(1)} %get-tuple-element.18.coef, ...), custom_call_target="tpu_custom_call" | custom-call | flops 1073741824 | bytes 12582912 | tf_op jit(solution)/shard_map/pallas_call | solution.py:308
  45.8 0.0 collective-permute-done.1.half2
  45.8 1.7 %shard_map.123 = f32[4096,128]{1,0:T(8,128)} custom-call(s32[7,36]{1,0:T(8,128)S(1)} %get-tuple-element.14.work, bf16[16,4,256,256]{3,2,1,0:T(8,128)(2,1)S(1)} %get-tuple-element.15.tiles, bf16[16,4,256,256]{3,2,1,0:T(8,128)(2,1)S(1)} %collective-permute-done.other, ...), custom_call_target="tpu_custom_call", output_to_operand_aliasing={{}: (5, {})} | custom-call | flops 1073741824 | bytes 4194304 | tf_op jit(solution)/shard_map/pallas_call | solution.py:308
  (23 shorter events, 0.1 us)
Async XLA Ops:
  0.0 30.2 %copy-start = (bf16[4096,128]{1,0:T(8,128)(2,1)S(1)}, bf16[4096,128]{1,0:T(8,128)(2,1)}, u32[]{:S(2)}) copy-start(bf16[4096,128]{1,0:T(8,128)(2,1)} %src.3) | copy-start | bytes 3145732
  0.0 30.2 %copy-start.9 = (s32[16]{0:T(128)S(1)}, s32[16]{0:T(128)}, u32[]{:S(2)}) copy-start(s32[16]{0:T(128)} %count.5) | copy-start | bytes 196
  0.0 30.1 %collective-permute-start = (bf16[16,4,256,256]{3,2,1,0:T(8,128)(2,1)}, bf16[16,4,256,256]{3,2,1,0:T(8,128)(2,1)S(1)}, u32[]{:S(2)}, u32[]{:S(2)}) collective-permute-start(bf16[16,4,256,256]{3,2,1,0:T(8,128)(2,1)} %tiles_hbm.1), channel_id=1, source_target_pairs={{0,1},{1,0},{2,3},{3,2},{4,5},{5,4},{6,7},{7,6},{8,9},{9,8},{10,11... | collective-permute-start | bytes 25165832 | tf_op jit(solution)/shard_map/ppermute | solution.py:304
  2.6 8.0 %collective-permute-start.3 = (bf16[704,128]{1,0:T(8,128)(2,1)S(1)}, bf16[704,128]{1,0:T(8,128)(2,1)S(1)}, u32[]{:S(2)}, u32[]{:S(2)}) collective-permute-start(bf16[704,128]{1,0:T(8,128)(2,1)S(1)} %get-tuple-element.19), channel_id=1, source_target_pairs={{0,2},{2,0},{4,6},{6,4},{8,10},{10,8},{12,14},{14,12},{16,18},{18,... | collective-permute-start | bytes 540680 | tf_op jit(solution)/shard_map/ppermute | solution.py:304
  5.2 29.7 %collective-permute-start.2 = (bf16[2048,128]{1,0:T(8,128)(2,1)S(1)}, bf16[2048,128]{1,0:T(8,128)(2,1)S(1)}, u32[]{:S(2)}, u32[]{:S(2)}) collective-permute-start(bf16[2048,128]{1,0:T(8,128)(2,1)S(1)} %get-tuple-element.17), channel_id=1, source_target_pairs={{0,2},{2,0},{4,6},{6,4},{8,10},{10,8},{12,14},{14,12},{16,18},{18,... | collective-permute-start | bytes 1572872 | tf_op jit(solution)/shard_map/ppermute | solution.py:304
  10.7 9.5 %collective-permute-start.5 = (bf16[320,128]{1,0:T(8,128)(2,1)S(1)}, bf16[320,128]{1,0:T(8,128)(2,1)S(1)}, u32[]{:S(2)}, u32[]{:S(2)}) collective-permute-start(bf16[320,128]{1,0:T(8,128)(2,1)S(1)} %pad_maximum_fusion.1), channel_id=1, source_target_pairs={{0,4},{2,6},{4,0},{6,2},{8,12},{10,14},{12,8},{14,10},{16,20},{18,... | collective-permute-start | bytes 245768 | tf_op jit(solution)/shard_map/ppermute | solution.py:304
  12.8 28.3 %collective-permute-start.4 = (bf16[512,128]{1,0:T(8,128)(2,1)S(1)}, bf16[512,128]{1,0:T(8,128)(2,1)S(1)}, u32[]{:S(2)}, u32[]{:S(2)}) collective-permute-start(bf16[512,128]{1,0:T(8,128)(2,1)S(1)} %get-tuple-element.20), channel_id=1, source_target_pairs={{2,4},{6,8},{10,12},{14,16},{18,20},{22,24},{26,28},{4,2},{8,6},{1... | collective-permute-start | bytes 393224 | tf_op jit(solution)/shard_map/ppermute | solution.py:304
  13.5 32.4 %collective-permute-start.1 = (bf16[2048,128]{1,0:T(8,128)(2,1)S(1)}, bf16[2048,128]{1,0:T(8,128)(2,1)S(1)}, u32[]{:S(2)}, u32[]{:S(2)}) collective-permute-start(bf16[2048,128]{1,0:T(8,128)(2,1)S(1)} %get-tuple-element.16), channel_id=1, source_target_pairs={{2,4},{6,8},{10,12},{14,16},{18,20},{22,24},{26,28},{4,2},{8,6},{1... | collective-permute-start | bytes 1572872 | tf_op jit(solution)/shard_map/ppermute | solution.py:304
  14.2 0.7 %copy-start.7 = (s32[16,8]{0,1:T(8,128)S(1)}, s32[16,8]{0,1:T(8,128)}, u32[]{:S(2)}) copy-start(s32[16,8]{0,1:T(8,128)} %param.14) | copy-start | bytes 1540
  14.9 0.7 %copy-start.8 = (s32[16]{0:T(128)S(1)}, s32[16]{0:T(128)}, u32[]{:S(2)}) copy-start(s32[16]{0:T(128)} %count.5) | copy-start | bytes 196
  20.2 20.9 %collective-permute-start.7 = (bf16[576,128]{1,0:T(8,128)(2,1)S(1)}, bf16[576,128]{1,0:T(8,128)(2,1)S(1)}, u32[]{:S(2)}, u32[]{:S(2)}) collective-permute-start(bf16[576,128]{1,0:T(8,128)(2,1)S(1)} %pad_maximum_fusion.plane), channel_id=1, source_target_pairs={{0,24},{2,26},{4,28},{6,30},{8,0},{10,2},{12,4},{14,6},{16,8},{18,... | collective-permute-start | bytes 442376 | tf_op jit(solution)/shard_map/ppermute | solution.py:304
  30.2 11.0 %collective-permute-start.6 = (bf16[576,128]{1,0:T(8,128)(2,1)S(1)}, bf16[576,128]{1,0:T(8,128)(2,1)S(1)}, u32[]{:S(2)}, u32[]{:S(2)}) collective-permute-start(bf16[576,128]{1,0:T(8,128)(2,1)S(1)} %pad_maximum_fusion.plane), channel_id=1, source_target_pairs={{0,8},{2,10},{4,12},{6,14},{8,16},{10,18},{12,20},{14,22},{16,24},... | collective-permute-start | bytes 442376 | tf_op jit(solution)/shard_map/ppermute | solution.py:304
  33.7 7.4 %copy-start.1 = (bf16[16,64,256]{2,1,0:T(8,128)(2,1)S(1)}, bf16[16,64,256]{2,1,0:T(8,128)(2,1)}, u32[]{:S(2)}) copy-start(bf16[16,64,256]{2,1,0:T(8,128)(2,1)} %basis.1) | copy-start | bytes 1572868
  33.8 7.4 %copy-start.2 = (bf16[16,64,256]{2,1,0:T(8,128)(2,1)S(1)}, bf16[16,64,256]{2,1,0:T(8,128)(2,1)}, u32[]{:S(2)}) copy-start(bf16[16,64,256]{2,1,0:T(8,128)(2,1)} %leaf_coupling.1) | copy-start | bytes 1572868
  33.8 7.4 %copy-start.3 = (bf16[2,64,512]{2,1,0:T(8,128)(2,1)S(1)}, bf16[2,64,512]{2,1,0:T(8,128)(2,1)}, u32[]{:S(2)}) copy-start(bf16[2,64,512]{2,1,0:T(8,128)(2,1)} %up_leaf.1) | copy-start | bytes 393220
  33.8 7.4 %copy-start.4 = (bf16[2,64,64]{2,1,0:T(8,128)(2,1)S(1)}, bf16[2,64,64]{2,1,0:T(8,128)(2,1)}, u32[]{:S(2)}) copy-start(bf16[2,64,64]{2,1,0:T(8,128)(2,1)} %up_mid.1) | copy-start | bytes 49156
  33.8 7.4 %copy-start.5 = (bf16[4,64,256]{2,1,0:T(8,128)(2,1)S(1)}, bf16[4,64,256]{2,1,0:T(8,128)(2,1)}, u32[]{:S(2)}) copy-start(bf16[4,64,256]{2,1,0:T(8,128)(2,1)} %top_coupling.1) | copy-start | bytes 393220
  33.8 7.4 %copy-start.6 = (bf16[2,64,256]{2,1,0:T(8,128)(2,1)S(1)}, bf16[2,64,256]{2,1,0:T(8,128)(2,1)}, u32[]{:S(2)}) copy-start(bf16[2,64,256]{2,1,0:T(8,128)(2,1)} %mid_coupling.1) | copy-start | bytes 196612
  33.8 7.4 %copy-start.10 = (s32[16,4]{0,1:T(4,128)S(1)}, s32[16,4]{0,1:T(4,128)}, u32[]{:S(2)}) copy-start(s32[16,4]{0,1:T(4,128)} %param.18) | copy-start | bytes 772
  33.8 7.4 %copy-start.11 = (s32[2,4]{1,0:T(2,128)S(1)}, s32[2,4]{1,0:T(2,128)}, u32[]{:S(2)}) copy-start(s32[2,4]{1,0:T(2,128)} %mid_far.1) | copy-start | bytes 100
  34.9 6.2 %collective-permute-start.8 = (bf16[64,128]{1,0:T(8,128)(2,1)S(1)}, bf16[64,128]{1,0:T(8,128)(2,1)S(1)}, u32[]{:S(2)}, u32[]{:S(2)}) collective-permute-start(bf16[64,128]{1,0:T(8,128)(2,1)S(1)} %add_convert_fusion), channel_id=1, source_target_pairs={{0,16},{2,18},{4,20},{6,22},{8,24},{10,26},{12,28},{14,30},{16,0},... | collective-permute-start | bytes 49160 | tf_op jit(solution)/shard_map/ppermute | solution.py:304
where the time goes:
time: 48.2 us; the launch traced here: 47.5 us
  Pallas kernels  20.2 us (42%)
  starting transfers between devices  19.2 us (40%)
  waiting for transfers between devices  6.41 us (13%)
  local copies, waits for them, and re-layouts  1.41 us (3%)
    pallas_call x6, Pallas kernels, run(): pl.pallas_call(kernel, out_shape=out_shape, in_specs=in_specs, out_specs=...  20.2 us
    ppermute x9, starting transfers between devices, send(): return lax.ppermute(x, axis, pairs)  19.2 us
    ppermute x9, waiting for transfers between devices, send(): return lax.ppermute(x, axis, pairs)  6.41 us
    unnamed x24, local copies, waits for them, and re-layouts  1.39 us
  transfers between devices with their start and end apart: 9, of which 2 were waited for; matrix products, arithmetic and copies ran while one was open for 0% of the time, Pallas kernels for 39%

commit v1 on v0

v1 whole, which is shorter than its diff:
```python
import jax
import jax.numpy as jnp
from jax import lax
from jax.experimental import pallas as pl
from jax.experimental.pallas import tpu as pltpu
from jax.sharding import PartitionSpec as P


CHILD = 8
FAR = 4
BATCH = 4
PARTS = 4

F32 = jnp.float32
BF16 = jnp.bfloat16
VMEM = pl.BlockSpec(memory_space=pltpu.VMEM)
SMEM = pl.BlockSpec(memory_space=pltpu.SMEM)
HBM = pl.BlockSpec(memory_space=pltpu.HBM)
ANY = pl.BlockSpec(memory_space=pl.ANY)


def mm(a, b):
    return jnp.dot(a, b, preferred_element_type=F32)


def mm_t(a, b):
    return lax.dot_general(a, b, (((0,), (0,)), ((), ())), preferred_element_type=F32)


def cost(flops, nbytes):
    return pl.CostEstimate(flops=flops, transcendentals=0, bytes_accessed=nbytes)


def params(mib):
    return pltpu.CompilerParams(vmem_limit_bytes=mib << 20)


def in_vmem(x):
    return pltpu.with_memory_space_constraint(x, pltpu.VMEM)


def in_hbm(x):
    return pltpu.with_memory_space_constraint(x, pltpu.HBM)


def blocks(start, count, size):
    return pl.ds(pl.multiple_of(start * size, size), count * size)


def upward(
    src_hbm, basis_hbm, up_leaf_hbm, up_mid_hbm,
    pack, half1, coef2, half2, coef,
    src, basis, up_leaf, up_mid, sems,
):
    leaves, rank, leaf = basis.shape
    mids = up_leaf.shape[0]
    step = leaves // PARTS
    loads = []
    for p in range(PARTS):
        near = pl.ds(p * step * leaf, step * leaf)
        far = pl.ds(p * step, step)
        loads.append(pltpu.make_async_copy(src_hbm.at[near], src.at[near], sems.at[2 * p]))
        loads.append(pltpu.make_async_copy(basis_hbm.at[far], basis.at[far], sems.at[2 * p + 1]))
    loads.append(pltpu.make_async_copy(up_leaf_hbm, up_leaf, sems.at[2 * PARTS]))
    loads.append(pltpu.make_async_copy(up_mid_hbm, up_mid, sems.at[2 * PARTS + 1]))
    for load in loads:
        load.start()
    odd = lax.rem(lax.axis_index("leaf"), 2)
    for p in range(PARTS):
        loads[2 * p].wait()
        loads[2 * p + 1].wait()
        for i in range(p * step, (p + 1) * step):
            coef[pl.ds(i * rank, rank), :] = mm(basis[i], src[pl.ds(i * leaf, leaf), :]).astype(BF16)
    first = (1 - odd) * (leaves - CHILD)
    second = odd * (leaves - CHILD)
    pack[pl.ds((mids + 1) * rank, CHILD * rank), :] = coef[blocks(first, CHILD, rank), :]
    coef2[...] = coef[blocks(second, CHILD, rank), :]
    half1[...] = src[blocks(first, CHILD, leaf), :]
    half2[...] = src[blocks(second, CHILD, leaf), :]
    loads[2 * PARTS].wait()
    loads[2 * PARTS + 1].wait()
    total = None
    for q in range(mids):
        mid = mm(up_leaf[q], coef[pl.ds(q * CHILD * rank, CHILD * rank), :]).astype(BF16)
        pack[pl.ds(q * rank, rank), :] = mid
        lift = mm(up_mid[q], mid).astype(BF16).astype(F32)
        total = lift if total is None else total + lift
    pack[pl.ds(mids * rank, rank), :] = total.astype(BF16)


def lists(index, count, work):
    leaves = index.shape[1]
    slots = index.shape[0] // 2
    device = lax.axis_index("leaf")
    odd = lax.rem(device, 2)
    core = lax.axis_index("col")
    first = device * leaves
    base = odd * (leaves - CHILD)
    lowest = jnp.where(odd == 1, leaves, -CHILD) + first

    def row(n, found):
        live = count[base + n]
        out = []
        for r, owner in ((0, core), (1, 1 - core)):
            at = found[r]
            for k in range(slots):
                slot = owner * slots + k
                outside = index[slot, base + n] - lowest
                work[3 * r, at] = n * slots + k
                work[3 * r + 1, at] = outside
                work[3 * r + 2, at] = n
                use = (slot < live) & (outside >= 0) & (outside < CHILD)
                at = at + use.astype(jnp.int32)
            out.append(at)
        return tuple(out)

    found = lax.fori_loop(0, CHILD, row, (jnp.int32(0), jnp.int32(0)))
    longest = jnp.maximum(found[0], found[1])
    rounds = (longest + BATCH - 1) // BATCH
    work[6, 0] = rounds
    for r in range(2):

        def fill(n, _):
            work[3 * r, n] = 0
            work[3 * r + 1, n] = 0
            work[3 * r + 2, n] = CHILD
            return 0

        lax.fori_loop(found[r], rounds * BATCH, fill, 0)


def load_tiles(tiles_hbm, tiles, sems, base):
    leaves = tiles.shape[0]
    loads = [
        pltpu.make_async_copy(tiles_hbm.at[base + n], tiles.at[n], sems.at[n]) for n in range(leaves)
    ]
    for load in loads:
        load.start()
    return loads


def place_of(index, live, slot, i, lowest, total):
    at = index[slot, i] - lowest
    return jnp.where((slot < live) & (at >= 0) & (at < total), at, total)


def near_a(index, count, tiles_hbm, src, out, tiles, window, sems, sem):
    slots, leaf = tiles.shape[1:3]
    leaves = tiles_hbm.shape[0]
    own = pltpu.make_async_copy(src, window.at[pl.ds(0, leaves * leaf)], sem)
    own.start()
    device = lax.axis_index("leaf")
    base = lax.rem(device, 2) * (leaves - CHILD)
    loads = load_tiles(tiles_hbm, tiles, sems, base)
    core = lax.axis_index("col")
    window[pl.ds(leaves * leaf, leaf), :] = jnp.zeros((leaf, src.shape[1]), BF16)
    own.wait()
    for n in range(CHILD):
        i = base + n
        live = count[i]
        loads[n].wait()
        acc = None
        for k in range(slots):
            place = place_of(index, live, core * slots + k, i, device * leaves, leaves)
            part = mm(tiles[n, k], window[blocks(place, 1, leaf), :])
            acc = part if acc is None else acc + part
        out[pl.ds(n * leaf, leaf), :] = acc


def near_mid(
    index, count, tiles_hbm, other, src, half1, far, near2,
    out, acc2,
    tiles, window, full, sems, sem,
):
    slots, leaf = tiles.shape[1:3]
    leaves = tiles_hbm.shape[0]
    device = lax.axis_index("leaf")
    odd = lax.rem(device, 2)
    core = lax.axis_index("col")
    base1 = (1 - odd) * (leaves - CHILD)
    base2 = odd * (leaves - CHILD)
    total = leaves + CHILD
    own = pltpu.make_async_copy(src, window.at[blocks(odd * CHILD, leaves, leaf)], sem)
    own.start()
    load_tiles(tiles_hbm, tiles, sems, base1)
    window[blocks((1 - odd) * leaves, CHILD, leaf), :] = half1[...]
    window[pl.ds(total * leaf, leaf), :] = jnp.zeros((leaf, src.shape[1]), BF16)
    lowest = device * leaves - odd * CHILD
    own.wait()

    def product(held, n, k, slot, i, live):
        place = place_of(index, live, slot, i, lowest, total)
        return mm(held[n, k], window[blocks(place, 1, leaf), :])

    def first_half(n, _):
        i = base1 + n
        live = count[i]
        pltpu.make_async_copy(tiles_hbm.at[0], tiles.at[n], sems.at[n]).wait()
        acc = far[blocks(i, 1, leaf), :]
        for k in range(slots):
            acc += product(other, i, k, (1 - core) * slots + k, i, live)
        for k in range(slots):
            acc += product(tiles, n, k, core * slots + k, i, live)
        full[blocks(n, 1, leaf), :] = acc
        return 0

    lax.fori_loop(0, CHILD, first_half, 0, unroll=2)
    store = pltpu.make_async_copy(full, out.at[blocks(base1, CHILD, leaf)], sem)
    store.start()

    def second_half(n, _):
        i = base2 + n
        live = count[i]
        acc = far[blocks(i, 1, leaf), :] + near2[blocks(n, 1, leaf), :]
        for k in range(slots):
            acc += product(other, i, k, (1 - core) * slots + k, i, live)
        acc2[blocks(n, 1, leaf), :] = acc
        return 0

    lax.fori_loop(0, CHILD, second_half, 0, unroll=2)
    store.wait()


def downward(
    leaf_far, mid_far,
    coef, pack1, coef2, plane, before, after, tops,
    basis, leaf_coupling, up_leaf, mid_coupling, up_mid, top_coupling,
    far,
    window, chosen, stack,
):
    leaves, rank, leaf = basis.shape
    mids = up_leaf.shape[0]
    group = CHILD // mids
    total_top = top_coupling.shape[0]
    device = lax.axis_index("leaf")
    odd = lax.rem(device, 2)
    parent = device // group
    member = lax.rem(device, group)
    top_row = CHILD * rank

    def put_top(value, ahead):
        at = lax.rem(parent + ahead, total_top)
        stack[blocks(at, 1, rank), :] = value

    put_top(jnp.zeros((rank, far.shape[1]), BF16), 0)
    put_top(before[pl.ds(top_row, rank), :], total_top - 1)
    put_top(after[pl.ds(top_row, rank), :], 1)
    for k in range(total_top - 3):
        put_top(tops[pl.ds(k * rank, rank), :], 2 + k)
    top_field = mm(top_coupling[parent], stack[...]).astype(BF16)

    window[pl.ds(CHILD * rank, leaves * rank), :] = coef[...]
    right = CHILD + leaves
    window[blocks((1 - odd) * right, CHILD, rank), :] = pack1[pl.ds((mids + 1) * rank, CHILD * rank), :]
    window[blocks(odd * right, CHILD, rank), :] = coef2[...]

    for q in range(mids):
        for f in range(FAR):
            b = mid_far[q, f]
            top = b // CHILD
            inside = lax.rem(b, CHILD)
            place = jnp.bitwise_xor(inside // mids, member) * mids + lax.rem(inside, mids)
            row = blocks(place, 1, rank)
            to = pl.ds(f * rank, rank)

            @pl.when(top == parent)
            def _():
                chosen[to, :] = plane[row, :]

            @pl.when(top < parent)
            def _():
                chosen[to, :] = before[row, :]

            @pl.when(top > parent)
            def _():
                chosen[to, :] = after[row, :]

        mid_field = (mm(mid_coupling[q], chosen[...]) + mm_t(up_mid[q], top_field)).astype(BF16)
        down = mm_t(up_leaf[q], mid_field)
        for k in range(CHILD):
            i = q * CHILD + k
            picked = [
                window[blocks(leaf_far[f, i] - (device * leaves - CHILD), 1, rank), :]
                for f in range(FAR)
            ]
            field = mm(leaf_coupling[i], jnp.concatenate(picked, axis=0)) + down[k * rank : (k + 1) * rank, :]
            far[pl.ds(i * leaf, leaf), :] = mm_t(basis[i], field.astype(BF16))


def near_last(work, tiles, other, half2, acc2, out_in, out, acc, sem):
    leaves, slots, leaf, _ = other.shape
    odd = lax.rem(lax.axis_index("leaf"), 2)
    base = odd * (leaves - CHILD)
    acc[pl.ds(0, CHILD * leaf), :] = acc2[...]

    def step(t, _):
        for b in range(BATCH):
            n = t * BATCH + b
            for r, held, low in ((0, tiles, 0), (1, other, base)):
                tile = work[3 * r, n]
                part = mm(
                    held[low + tile // slots, lax.rem(tile, slots)],
                    half2[blocks(work[3 * r + 1, n], 1, leaf), :],
                )
                acc[blocks(work[3 * r + 2, n], 1, leaf), :] += part
        return 0

    lax.fori_loop(0, work[6, 0], step, 0)
    rows = blocks(base, CHILD, leaf)
    store = pltpu.make_async_copy(acc.at[pl.ds(0, CHILD * leaf)], out.at[rows], sem)
    store.start()
    store.wait()


def shards(
    sources,
    near_tiles,
    near_index,
    near_count,
    leaf_basis,
    leaf_coupling,
    leaf_far,
    up_leaf,
    mid_coupling,
    mid_far,
    up_mid,
    top_coupling,
):
    sds = jax.ShapeDtypeStruct
    leaves, rank, leaf = leaf_basis.shape
    mids = up_leaf.shape[0]
    cols = sources.shape[1]
    slots = near_tiles.shape[1]
    total_top = top_coupling.shape[0]
    devices = lax.axis_size("leaf")
    group = CHILD // mids
    edge = CHILD * leaf
    edge_c = CHILD * rank
    rows = leaves * leaf
    assert leaves == 2 * CHILD and group >= 2 and total_top >= 4
    product_flops = 2 * leaf * leaf * cols

    pair = [(i, i ^ 1) for i in range(devices)]
    rest = [(i, i + 1) for i in range(1, devices - 1, 2)]
    rest = rest + [(j, i) for i, j in rest]

    def shift(k):
        return [(i, (i + k * group) % devices) for i in range(devices)]

    def send(x, pairs, axis="leaf"):
        return lax.ppermute(x, axis, pairs)

    def call(kernel, out_shape, in_specs, out_specs, scratch, mib, estimate, **more):
        def run(*args):
            return pl.pallas_call(
                kernel,
                out_shape=out_shape,
                in_specs=in_specs,
                out_specs=out_specs,
                scratch_shapes=scratch,
                compiler_params=params(mib),
                cost_estimate=estimate,
                **more,
            )(*args)

        return run

    index, count, far_index, mid_index = map(in_hbm, (near_index.T, near_count, leaf_far.T, mid_far))
    own_tiles = in_hbm(near_tiles)

    pack, half1, coef2, half2, coef = call(
        upward,
        (
            sds(((mids + 1) * rank + edge_c, cols), BF16),
            sds((edge, cols), BF16),
            sds((edge_c, cols), BF16),
            sds((edge, cols), BF16),
            sds((leaves * rank, cols), BF16),
        ),
        [HBM] * 4,
        (VMEM,) * 5,
        [
            pltpu.VMEM(sources.shape, BF16),
            pltpu.VMEM(leaf_basis.shape, BF16),
            pltpu.VMEM(up_leaf.shape, BF16),
            pltpu.VMEM(up_mid.shape, BF16),
            pltpu.SemaphoreType.DMA((2 * PARTS + 2,)),
        ],
        8,
        cost(2 * leaves * rank * leaf * cols, 4 << 20),
    )(*map(in_hbm, (sources, leaf_basis, up_leaf, up_mid)))

    pack1 = send(pack, pair)
    coef2 = send(coef2, rest)
    half1 = send(half1, pair)
    other = in_vmem(send(near_tiles, [(0, 1), (1, 0)], "col"))

    work = call(
        lists,
        sds((7, CHILD * slots + BATCH), jnp.int32),
        [SMEM, SMEM],
        SMEM,
        [],
        8,
        cost(0, 1 << 20),
    )(index, count)

    held = mids * rank
    plane = jnp.concatenate([pack[:held], pack1[:held]], axis=0)
    total = pack[held : held + rank].astype(F32) + pack1[held : held + rank].astype(F32)
    total = total.astype(BF16)
    k = 2
    while k < group:
        mine = jnp.concatenate([plane, total], axis=0)
        got = send(mine, [(i, i ^ k) for i in range(devices)])
        held = plane.shape[0]
        plane = jnp.concatenate([plane, got[:held]], axis=0)
        total = (total.astype(F32) + got[held:].astype(F32)).astype(BF16)
        k *= 2
    half2 = send(half2, rest)

    near2, tiles2 = call(
        near_a,
        (sds((edge, cols), F32), sds((CHILD,) + near_tiles.shape[1:], BF16)),
        [SMEM, SMEM, HBM, HBM],
        (VMEM, VMEM),
        [
            pltpu.VMEM((rows + leaf, cols), BF16),
            pltpu.SemaphoreType.DMA((CHILD,)),
            pltpu.SemaphoreType.DMA,
        ],
        12,
        cost(CHILD * slots * product_flops, 8 << 20),
    )(index, count, own_tiles, in_hbm(sources))
    tiles2 = in_vmem(tiles2)

    plane = jnp.concatenate([plane, total], axis=0)
    before = send(plane, shift(1))
    after = send(plane, shift(-1))
    tops = [send(total, shift(-k)) for k in range(2, total_top - 1)]
    tops = tops[0] if len(tops) == 1 else jnp.concatenate(tops, axis=0)

    far = call(
        downward,
        sds((rows, cols), F32),
        [SMEM] * 2 + [VMEM] * 13,
        VMEM,
        [
            pltpu.VMEM((2 * edge_c + leaves * rank, cols), BF16),
            pltpu.VMEM((FAR * rank, cols), BF16),
            pltpu.VMEM((total_top * rank, cols), BF16),
        ],
        16,
        cost(leaves * 4 * product_flops, 12 << 20),
    )(
        far_index, mid_index,
        coef, pack1, coef2, plane, before, after, tops,
        leaf_basis, leaf_coupling, up_leaf, mid_coupling, up_mid, top_coupling,
    )

    out, acc2 = call(
        near_mid,
        (sds((rows, cols), F32), sds((edge, cols), F32)),
        [SMEM, SMEM, HBM, VMEM, HBM] + [VMEM] * 3,
        (ANY, VMEM),
        [
            pltpu.VMEM((CHILD,) + near_tiles.shape[1:], BF16),
            pltpu.VMEM((rows + edge + leaf, cols), BF16),
            pltpu.VMEM((edge, cols), F32),
            pltpu.SemaphoreType.DMA((CHILD,)),
            pltpu.SemaphoreType.DMA,
        ],
        16,
        cost(CHILD * 3 * slots * product_flops, 16 << 20),
    )(index, count, own_tiles, other, in_hbm(sources), half1, far, near2)

    return call(
        near_last,
        sds((rows, cols), F32),
        [SMEM, VMEM, VMEM, VMEM, VMEM, ANY],
        ANY,
        [pltpu.VMEM((edge + leaf, cols), F32), pltpu.SemaphoreType.DMA],
        8,
        cost(leaves * slots * product_flops, 4 << 20),
        input_output_aliases={5: 0},
    )(work, tiles2, other, half2, acc2, out)


def solution(mesh):


    return jax.shard_map(
        shards,
        mesh=mesh,
        in_specs=(
            P("leaf", "col"),
            P("leaf", "col", None, None),
            P("leaf", None),
            P("leaf"),
            P("leaf", None, None),
            P("leaf", None, None),
            P("leaf", None),
            P("leaf", None, None),
            P("leaf", None, None),
            P("leaf", None),
            P("leaf", None, None),
            P(),
        ),
        out_specs=P("leaf", "col"),
        check_vma=False,
    )
```

time: 48.2 us -> 57.2 us (1.19)
  waiting for transfers between devices: 6.41 us -> 16 us
  Pallas kernels: 20.2 us -> 22.2 us
  local copies, waits for them, and re-layouts: 1.41 us -> 0.05 us
  starting transfers between devices: 19.2 us -> 18.4 us
    ppermute x9, waiting for transfers between devices: 6.41 us -> 16 us  [send(): return lax.ppermute(x, axis, pairs)]
    pallas_call x6, Pallas kernels: 20.2 us -> 22.2 us  [run(): pl.pallas_call(kernel, out_shape=out_shape, in_specs=in_specs, out_specs=...]
    unnamed x24 -> x12, local copies, waits for them, and re-layouts: 1.39 us -> 0.04 us
    ppermute x9, starting transfers between devices: 19.2 us -> 18.4 us  [send(): return lax.ppermute(x, axis, pairs)]
  transfers between devices with their start and end apart: 9 -> 9, of which waited for: 2 -> 2; matrix products, arithmetic and copies ran while one was open for 0% -> 0% of each run, Pallas kernels for 39% -> 36%
where the time goes in v1:
time: 57.2 us; the launch traced here: 57 us
  Pallas kernels  22.2 us (39%)
  starting transfers between devices  18.4 us (32%)
  waiting for transfers between devices  16 us (28%)
    pallas_call x6, Pallas kernels, run(): pl.pallas_call(kernel, out_shape=out_shape, in_specs=in_specs, out_specs=...  22.2 us
    ppermute x9, starting transfers between devices, send(): return lax.ppermute(x, axis, pairs)  18.4 us
    ppermute x9, waiting for transfers between devices, send(): return lax.ppermute(x, axis, pairs)  16 us
  transfers between devices with their start and end apart: 9, of which 2 were waited for; matrix products, arithmetic and copies ran while one was open for 0% of the time, Pallas kernels for 36%

profile of v1, /device:TPU:0, one launch (start us, length us, event | category | flops | bytes accessed | tf_op | source)
XLA Modules:
  0.0 57.0 jit_solution(5352838598288831499)
XLA Ops:
  0.0 0.5 collective-permute-start
  0.5 2.3 %shard_map.120 = (bf16[704,128]{1,0:T(8,128)(2,1)S(1)}, bf16[2048,128]{1,0:T(8,128)(2,1)S(1)}, bf16[512,128]{1,0:T(8,128)(2,1)S(1)}, bf16[2048,128]{1,0:T(8,128)(2,1)S(1)}, bf16[1024,128]{1,0:T(8,128)(2,1)S(1)}) custom-call(bf16[4096,128]{1,0:T(8,128)(2,1)} %src.3, bf16[16,64,256]{2,1,0:T(8,128)(2,1)} %basis.1, bf16[2,64,512]{2,1,0:T(8,128)(2,1)} %up_leaf.1, ...), custom_call_target="tpu_custom_call" | custom-call | flops 67108864 | bytes 4194304 | tf_op jit(solution)/shard_map/pallas_call | solution.py:355
  2.8 2.5 %collective-permute-start.3 = (bf16[704,128]{1,0:T(8,128)(2,1)S(1)}, bf16[704,128]{1,0:T(8,128)(2,1)S(1)}, u32[]{:S(2)}, u32[]{:S(2)}) collective-permute-start(bf16[704,128]{1,0:T(8,128)(2,1)S(1)} %get-tuple-element.18), channel_id=1, source_target_pairs={{0,2},{2,0},{4,6},{6,4},{8,10},{10,8},{12,14},{14,12},{16,18},{18,... | collective-permute-start | bytes 540680 | tf_op jit(solution)/shard_map/ppermute | solution.py:351
  5.3 5.2 %collective-permute-done.3.pack1 = bf16[704,128]{1,0:T(8,128)(2,1)S(1)} collective-permute-done((bf16[704,128]{1,0:T(8,128)(2,1)S(1)}, bf16[704,128]{1,0:T(8,128)(2,1)S(1)}, u32[]{:S(2)}, u32[]{:S(2)}) %collective-permute-start.3) | collective-permute-done | bytes 180256 | tf_op jit(solution)/shard_map/ppermute | solution.py:351
  10.6 1.8 %collective-permute-start.5 = (bf16[320,128]{1,0:T(8,128)(2,1)S(1)}, bf16[320,128]{1,0:T(8,128)(2,1)S(1)}, u32[]{:S(2)}, u32[]{:S(2)}) collective-permute-start(bf16[320,128]{1,0:T(8,128)(2,1)S(1)} %pad_maximum_fusion.1), channel_id=1, source_target_pairs={{0,4},{2,6},{4,0},{6,2},{8,12},{10,14},{12,8},{14,10},{16,20},{18,... | collective-permute-start | bytes 245768 | tf_op jit(solution)/shard_map/ppermute | solution.py:351
  12.4 0.7 %collective-permute-start.4 = (bf16[512,128]{1,0:T(8,128)(2,1)S(1)}, bf16[512,128]{1,0:T(8,128)(2,1)S(1)}, u32[]{:S(2)}, u32[]{:S(2)}) collective-permute-start(bf16[512,128]{1,0:T(8,128)(2,1)S(1)} %get-tuple-element.19), channel_id=1, source_target_pairs={{2,4},{6,8},{10,12},{14,16},{18,20},{22,24},{26,28},{4,2},{8,6},{1... | collective-permute-start | bytes 393224 | tf_op jit(solution)/shard_map/ppermute | solution.py:351
  13.1 3.0 %collective-permute-start.2 = (bf16[2048,128]{1,0:T(8,128)(2,1)S(1)}, bf16[2048,128]{1,0:T(8,128)(2,1)S(1)}, u32[]{:S(2)}, u32[]{:S(2)}) collective-permute-start(bf16[2048,128]{1,0:T(8,128)(2,1)S(1)} %get-tuple-element.16), channel_id=1, source_target_pairs={{0,2},{2,0},{4,6},{6,4},{8,10},{10,8},{12,14},{14,12},{16,18},{18,... | collective-permute-start | bytes 1572872 | tf_op jit(solution)/shard_map/ppermute | solution.py:351
  16.1 0.7 %collective-permute-start.1 = (bf16[2048,128]{1,0:T(8,128)(2,1)S(1)}, bf16[2048,128]{1,0:T(8,128)(2,1)S(1)}, u32[]{:S(2)}, u32[]{:S(2)}) collective-permute-start(bf16[2048,128]{1,0:T(8,128)(2,1)S(1)} %get-tuple-element.15), channel_id=1, source_target_pairs={{2,4},{6,8},{10,12},{14,16},{18,20},{22,24},{26,28},{4,2},{8,6},{1... | collective-permute-start | bytes 1572872 | tf_op jit(solution)/shard_map/ppermute | solution.py:351
  16.8 0.0 collective-permute-done.5
  16.8 6.4 %collective-permute-start.8 = (bf16[64,128]{1,0:T(8,128)(2,1)S(1)}, bf16[64,128]{1,0:T(8,128)(2,1)S(1)}, u32[]{:S(2)}, u32[]{:S(2)}) collective-permute-start(bf16[64,128]{1,0:T(8,128)(2,1)S(1)} %add_convert_fusion), channel_id=1, source_target_pairs={{0,16},{2,18},{4,20},{6,22},{8,24},{10,26},{12,28},{14,30},{16,0},... | collective-permute-start | bytes 49160 | tf_op jit(solution)/shard_map/ppermute | solution.py:351
  23.3 0.0 collective-permute-done.4.coef2
  23.3 1.6 %collective-permute-start.6 = (bf16[576,128]{1,0:T(8,128)(2,1)S(1)}, bf16[576,128]{1,0:T(8,128)(2,1)S(1)}, u32[]{:S(2)}, u32[]{:S(2)}) collective-permute-start(bf16[576,128]{1,0:T(8,128)(2,1)S(1)} %pad_maximum_fusion.plane), channel_id=1, source_target_pairs={{0,8},{2,10},{4,12},{6,14},{8,16},{10,18},{12,20},{14,22},{16,24},... | collective-permute-start | bytes 442376 | tf_op jit(solution)/shard_map/ppermute | solution.py:351
  24.9 10.8 %collective-permute-done.8.tops = bf16[64,128]{1,0:T(8,128)(2,1)S(1)} collective-permute-done((bf16[64,128]{1,0:T(8,128)(2,1)S(1)}, bf16[64,128]{1,0:T(8,128)(2,1)S(1)}, u32[]{:S(2)}, u32[]{:S(2)}) %collective-permute-start.8) | collective-permute-done | bytes 16416 | tf_op jit(solution)/shard_map/ppermute | solution.py:351
  35.7 1.1 %collective-permute-start.7 = (bf16[576,128]{1,0:T(8,128)(2,1)S(1)}, bf16[576,128]{1,0:T(8,128)(2,1)S(1)}, u32[]{:S(2)}, u32[]{:S(2)}) collective-permute-start(bf16[576,128]{1,0:T(8,128)(2,1)S(1)} %pad_maximum_fusion.plane), channel_id=1, source_target_pairs={{0,24},{2,26},{4,28},{6,30},{8,0},{10,2},{12,4},{14,6},{16,8},{18,... | collective-permute-start | bytes 442376 | tf_op jit(solution)/shard_map/ppermute | solution.py:351
  36.8 1.9 %shard_map.118.work = s32[7,36]{1,0:T(8,128)S(1)} custom-call(s32[8,16]{1,0:T(8,128)} %bitcast.2, s32[16]{0:T(128)} %count.5), custom_call_target="tpu_custom_call" | custom-call | bytes 1048576 | tf_op jit(solution)/shard_map/pallas_call | solution.py:355
  38.8 0.0 copy-start
  38.8 0.0 copy-start.1
  38.8 0.0 copy-start.2
  38.8 0.0 copy-start.3
  38.8 0.0 copy-start.4
  38.8 0.0 copy-start.5
  38.8 4.7 %shard_map.119 = (f32[2048,128]{1,0:T(8,128)S(1)}, bf16[8,4,256,256]{3,2,1,0:T(8,128)(2,1)S(1)}) custom-call(s32[8,16]{1,0:T(8,128)} %bitcast.3, s32[16]{0:T(128)} %count.5, bf16[16,4,256,256]{3,2,1,0:T(8,128)(2,1)} %tiles_hbm.3, bf16[4096,128]{1,0:T(8,128)(2,1)} %src.3), custom_call_target="tpu_custom_call" | custom-call | flops 536870912 | bytes 8388608 | tf_op jit(solution)/shard_map/pallas_call | solution.py:355
  43.5 0.0 collective-permute-done.6.before
  43.6 0.0 collective-permute-done.7.after
  43.6 0.0 copy-done
  43.6 0.0 copy-done.1
  43.6 3.4 %shard_map.121.far = f32[4096,128]{1,0:T(8,128)S(1)} custom-call(s32[4,16]{1,0:T(4,128)} %bitcast.5, s32[2,4]{1,0:T(2,128)} %mid_far.1, bf16[1024,128]{1,0:T(8,128)(2,1)S(1)} %get-tuple-element.17.coef, bf16[704,128]{1,0:T(8,128)(2,1)S(1)} %collective-permute-done.3.pack1, bf16[512,128]{1,0:T(8,128)(2,1)S(1)} %collective-permute-done.4.coef2, ...), custom_call_target="tpu_custom_call" | custom-call | flops 1073741824 | bytes 12582912 | tf_op jit(solution)/shard_map/pallas_call | solution.py:355
  47.1 0.0 collective-permute-done.2.half1
  47.1 0.0 collective-permute-done.other
  47.1 8.2 %shard_map.122 = (f32[4096,128]{1,0:T(8,128)}, f32[2048,128]{1,0:T(8,128)S(1)}) custom-call(s32[8,16]{1,0:T(8,128)} %bitcast.4, s32[16]{0:T(128)} %count.5, bf16[16,4,256,256]{3,2,1,0:T(8,128)(2,1)} %tiles_hbm.3, bf16[16,4,256,256]{3,2,1,0:T(8,128)(2,1)S(1)} %collective-permute-done.other, bf16[4096,128]{1,0:T(8,128)(2,1)} %src.3, ...), custom_call_target="tpu_custom_call" | custom-call | flops 1610612736 | bytes 16777216 | tf_op jit(solution)/shard_map/pallas_call | solution.py:355
  55.3 0.0 collective-permute-done.1.half2
  55.3 1.7 %shard_map.123 = f32[4096,128]{1,0:T(8,128)} custom-call(s32[7,36]{1,0:T(8,128)S(1)} %shard_map.118.work, bf16[8,4,256,256]{3,2,1,0:T(8,128)(2,1)S(1)} %get-tuple-element.14.tiles, bf16[16,4,256,256]{3,2,1,0:T(8,128)(2,1)S(1)} %collective-permute-done.other, bf16[2048,128]{1,0:T(8,128)(2,1)S(1)} %collective-permute-done.1.half2, ...), custom_call_target="tpu_custom_call", output_to_operand_aliasing={{}: (5, {})} | custom-call | flops 1073741824 | bytes 4194304 | tf_op jit(solution)/shard_map/pallas_call | solution.py:355
  (11 shorter events, 0.1 us)
Async XLA Ops:
  0.0 47.1 %collective-permute-start = (bf16[16,4,256,256]{3,2,1,0:T(8,128)(2,1)}, bf16[16,4,256,256]{3,2,1,0:T(8,128)(2,1)S(1)}, u32[]{:S(2)}, u32[]{:S(2)}) collective-permute-start(bf16[16,4,256,256]{3,2,1,0:T(8,128)(2,1)} %tiles_hbm.3), channel_id=1, source_target_pairs={{0,1},{1,0},{2,3},{3,2},{4,5},{5,4},{6,7},{7,6},{8,9},{9,8},{10,11... | collective-permute-start | bytes 25165832 | tf_op jit(solution)/shard_map/ppermute | solution.py:351
  2.8 7.8 %collective-permute-start.3 = (bf16[704,128]{1,0:T(8,128)(2,1)S(1)}, bf16[704,128]{1,0:T(8,128)(2,1)S(1)}, u32[]{:S(2)}, u32[]{:S(2)}) collective-permute-start(bf16[704,128]{1,0:T(8,128)(2,1)S(1)} %get-tuple-element.18), channel_id=1, source_target_pairs={{0,2},{2,0},{4,6},{6,4},{8,10},{10,8},{12,14},{14,12},{16,18},{18,... | collective-permute-start | bytes 540680 | tf_op jit(solution)/shard_map/ppermute | solution.py:351
  10.6 6.2 %collective-permute-start.5 = (bf16[320,128]{1,0:T(8,128)(2,1)S(1)}, bf16[320,128]{1,0:T(8,128)(2,1)S(1)}, u32[]{:S(2)}, u32[]{:S(2)}) collective-permute-start(bf16[320,128]{1,0:T(8,128)(2,1)S(1)} %pad_maximum_fusion.1), channel_id=1, source_target_pairs={{0,4},{2,6},{4,0},{6,2},{8,12},{10,14},{12,8},{14,10},{16,20},{18,... | collective-permute-start | bytes 245768 | tf_op jit(solution)/shard_map/ppermute | solution.py:351
  12.4 10.9 %collective-permute-start.4 = (bf16[512,128]{1,0:T(8,128)(2,1)S(1)}, bf16[512,128]{1,0:T(8,128)(2,1)S(1)}, u32[]{:S(2)}, u32[]{:S(2)}) collective-permute-start(bf16[512,128]{1,0:T(8,128)(2,1)S(1)} %get-tuple-element.19), channel_id=1, source_target_pairs={{2,4},{6,8},{10,12},{14,16},{18,20},{22,24},{26,28},{4,2},{8,6},{1... | collective-permute-start | bytes 393224 | tf_op jit(solution)/shard_map/ppermute | solution.py:351
  13.1 34.0 %collective-permute-start.2 = (bf16[2048,128]{1,0:T(8,128)(2,1)S(1)}, bf16[2048,128]{1,0:T(8,128)(2,1)S(1)}, u32[]{:S(2)}, u32[]{:S(2)}) collective-permute-start(bf16[2048,128]{1,0:T(8,128)(2,1)S(1)} %get-tuple-element.16), channel_id=1, source_target_pairs={{0,2},{2,0},{4,6},{6,4},{8,10},{10,8},{12,14},{14,12},{16,18},{18,... | collective-permute-start | bytes 1572872 | tf_op jit(solution)/shard_map/ppermute | solution.py:351
  16.1 39.2 %collective-permute-start.1 = (bf16[2048,128]{1,0:T(8,128)(2,1)S(1)}, bf16[2048,128]{1,0:T(8,128)(2,1)S(1)}, u32[]{:S(2)}, u32[]{:S(2)}) collective-permute-start(bf16[2048,128]{1,0:T(8,128)(2,1)S(1)} %get-tuple-element.15), channel_id=1, source_target_pairs={{2,4},{6,8},{10,12},{14,16},{18,20},{22,24},{26,28},{4,2},{8,6},{1... | collective-permute-start | bytes 1572872 | tf_op jit(solution)/shard_map/ppermute | solution.py:351
  16.8 18.9 %collective-permute-start.8 = (bf16[64,128]{1,0:T(8,128)(2,1)S(1)}, bf16[64,128]{1,0:T(8,128)(2,1)S(1)}, u32[]{:S(2)}, u32[]{:S(2)}) collective-permute-start(bf16[64,128]{1,0:T(8,128)(2,1)S(1)} %add_convert_fusion), channel_id=1, source_target_pairs={{0,16},{2,18},{4,20},{6,22},{8,24},{10,26},{12,28},{14,30},{16,0},... | collective-permute-start | bytes 49160 | tf_op jit(solution)/shard_map/ppermute | solution.py:351
  23.3 20.2 %collective-permute-start.6 = (bf16[576,128]{1,0:T(8,128)(2,1)S(1)}, bf16[576,128]{1,0:T(8,128)(2,1)S(1)}, u32[]{:S(2)}, u32[]{:S(2)}) collective-permute-start(bf16[576,128]{1,0:T(8,128)(2,1)S(1)} %pad_maximum_fusion.plane), channel_id=1, source_target_pairs={{0,8},{2,10},{4,12},{6,14},{8,16},{10,18},{12,20},{14,22},{16,24},... | collective-permute-start | bytes 442376 | tf_op jit(solution)/shard_map/ppermute | solution.py:351
  35.7 7.8 %collective-permute-start.7 = (bf16[576,128]{1,0:T(8,128)(2,1)S(1)}, bf16[576,128]{1,0:T(8,128)(2,1)S(1)}, u32[]{:S(2)}, u32[]{:S(2)}) collective-permute-start(bf16[576,128]{1,0:T(8,128)(2,1)S(1)} %pad_maximum_fusion.plane), channel_id=1, source_target_pairs={{0,24},{2,26},{4,28},{6,30},{8,0},{10,2},{12,4},{14,6},{16,8},{18,... | collective-permute-start | bytes 442376 | tf_op jit(solution)/shard_map/ppermute | solution.py:351
  38.8 4.8 %copy-start = (bf16[16,64,256]{2,1,0:T(8,128)(2,1)S(1)}, bf16[16,64,256]{2,1,0:T(8,128)(2,1)}, u32[]{:S(2)}) copy-start(bf16[16,64,256]{2,1,0:T(8,128)(2,1)} %basis.1) | copy-start | bytes 1572868
  38.8 4.8 %copy-start.1 = (bf16[16,64,256]{2,1,0:T(8,128)(2,1)S(1)}, bf16[16,64,256]{2,1,0:T(8,128)(2,1)}, u32[]{:S(2)}) copy-start(bf16[16,64,256]{2,1,0:T(8,128)(2,1)} %leaf_coupling.1) | copy-start | bytes 1572868
  38.8 4.8 %copy-start.2 = (bf16[2,64,512]{2,1,0:T(8,128)(2,1)S(1)}, bf16[2,64,512]{2,1,0:T(8,128)(2,1)}, u32[]{:S(2)}) copy-start(bf16[2,64,512]{2,1,0:T(8,128)(2,1)} %up_leaf.1) | copy-start | bytes 393220
  38.8 4.8 %copy-start.3 = (bf16[2,64,64]{2,1,0:T(8,128)(2,1)S(1)}, bf16[2,64,64]{2,1,0:T(8,128)(2,1)}, u32[]{:S(2)}) copy-start(bf16[2,64,64]{2,1,0:T(8,128)(2,1)} %up_mid.1) | copy-start | bytes 49156
  38.8 4.8 %copy-start.4 = (bf16[4,64,256]{2,1,0:T(8,128)(2,1)S(1)}, bf16[4,64,256]{2,1,0:T(8,128)(2,1)}, u32[]{:S(2)}) copy-start(bf16[4,64,256]{2,1,0:T(8,128)(2,1)} %top_coupling.1) | copy-start | bytes 393220
  38.8 4.8 %copy-start.5 = (bf16[2,64,256]{2,1,0:T(8,128)(2,1)S(1)}, bf16[2,64,256]{2,1,0:T(8,128)(2,1)}, u32[]{:S(2)}) copy-start(bf16[2,64,256]{2,1,0:T(8,128)(2,1)} %mid_coupling.1) | copy-start | bytes 196612

commit v2 on v1

v2 whole, which is shorter than its diff:
```python
import jax
import jax.numpy as jnp
from jax import lax
from jax.experimental import pallas as pl
from jax.experimental.pallas import tpu as pltpu
from jax.sharding import PartitionSpec as P


CHILD = 8
FAR = 4
BATCH = 4
PARTS = 4

F32 = jnp.float32
BF16 = jnp.bfloat16
VMEM = pl.BlockSpec(memory_space=pltpu.VMEM)
SMEM = pl.BlockSpec(memory_space=pltpu.SMEM)
HBM = pl.BlockSpec(memory_space=pltpu.HBM)
ANY = pl.BlockSpec(memory_space=pl.ANY)


def mm(a, b):
    return jnp.dot(a, b, preferred_element_type=F32)


def mm_t(a, b):
    return lax.dot_general(a, b, (((0,), (0,)), ((), ())), preferred_element_type=F32)


def cost(flops, nbytes):
    return pl.CostEstimate(flops=flops, transcendentals=0, bytes_accessed=nbytes)


def params(mib):
    return pltpu.CompilerParams(vmem_limit_bytes=mib << 20)


def in_vmem(x):
    return pltpu.with_memory_space_constraint(x, pltpu.VMEM)


def in_hbm(x):
    return pltpu.with_memory_space_constraint(x, pltpu.HBM)


def blocks(start, count, size):
    return pl.ds(pl.multiple_of(start * size, size), count * size)


def upward(
    src_hbm, basis_hbm, up_leaf_hbm, up_mid_hbm,
    pack, bulk1, coef, src,
    basis, up_leaf, up_mid, sems,
):
    leaves, rank, leaf = basis.shape
    mids = up_leaf.shape[0]
    step = leaves // PARTS
    loads = []
    for p in range(PARTS):
        near = pl.ds(p * step * leaf, step * leaf)
        far = pl.ds(p * step, step)
        loads.append(pltpu.make_async_copy(src_hbm.at[near], src.at[near], sems.at[2 * p]))
        loads.append(pltpu.make_async_copy(basis_hbm.at[far], basis.at[far], sems.at[2 * p + 1]))
    loads.append(pltpu.make_async_copy(up_leaf_hbm, up_leaf, sems.at[2 * PARTS]))
    loads.append(pltpu.make_async_copy(up_mid_hbm, up_mid, sems.at[2 * PARTS + 1]))
    for load in loads:
        load.start()
    src[pl.ds(leaves * leaf, leaf), :] = jnp.zeros((leaf, src.shape[1]), BF16)
    odd = lax.rem(lax.axis_index("leaf"), 2)
    for p in range(PARTS):
        loads[2 * p].wait()
        loads[2 * p + 1].wait()
        for i in range(p * step, (p + 1) * step):
            coef[pl.ds(i * rank, rank), :] = mm(basis[i], src[pl.ds(i * leaf, leaf), :]).astype(BF16)
    first = (1 - odd) * (leaves - CHILD)
    bulk1[pl.ds(0, CHILD * rank), :] = coef[blocks(first, CHILD, rank), :]
    bulk1[pl.ds(CHILD * rank, CHILD * leaf), :] = src[blocks(first, CHILD, leaf), :]
    loads[2 * PARTS].wait()
    loads[2 * PARTS + 1].wait()
    total = None
    for q in range(mids):
        mid = mm(up_leaf[q], coef[pl.ds(q * CHILD * rank, CHILD * rank), :]).astype(BF16)
        pack[pl.ds(q * rank, rank), :] = mid
        lift = mm(up_mid[q], mid).astype(BF16).astype(F32)
        total = lift if total is None else total + lift
    pack[pl.ds(mids * rank, rank), :] = total.astype(BF16)


def prepare(index, count, coef, src, work, bulk2):
    leaves = index.shape[1]
    slots = index.shape[0] // 2
    rank = coef.shape[0] // leaves
    leaf = src.shape[0] // (leaves + 1)
    device = lax.axis_index("leaf")
    odd = lax.rem(device, 2)
    core = lax.axis_index("col")
    base = odd * (leaves - CHILD)
    bulk2[pl.ds(0, CHILD * rank), :] = coef[blocks(base, CHILD, rank), :]
    bulk2[pl.ds(CHILD * rank, CHILD * leaf), :] = src[blocks(base, CHILD, leaf), :]
    lowest = jnp.where(odd == 1, leaves, -CHILD) + device * leaves

    def row(n, found):
        live = count[base + n]
        out = []
        for r, owner in ((0, core), (1, 1 - core)):
            at = found[r]
            for k in range(slots):
                slot = owner * slots + k
                outside = index[slot, base + n] - lowest
                work[3 * r, at] = n * slots + k
                work[3 * r + 1, at] = outside
                work[3 * r + 2, at] = n
                use = (slot < live) & (outside >= 0) & (outside < CHILD)
                at = at + use.astype(jnp.int32)
            out.append(at)
        return tuple(out)

    found = lax.fori_loop(0, CHILD, row, (jnp.int32(0), jnp.int32(0)))
    longest = jnp.maximum(found[0], found[1])
    rounds = (longest + BATCH - 1) // BATCH
    work[6, 0] = rounds
    for r in range(2):

        def fill(n, _):
            work[3 * r, n] = 0
            work[3 * r + 1, n] = 0
            work[3 * r + 2, n] = CHILD
            return 0

        lax.fori_loop(found[r], rounds * BATCH, fill, 0)


def load_tiles(tiles_hbm, tiles, sems, base):
    loads = [
        pltpu.make_async_copy(tiles_hbm.at[base + n], tiles.at[n], sems.at[n])
        for n in range(tiles.shape[0])
    ]
    for load in loads:
        load.start()
    return loads


def product(index, live, held, n, k, slot, i, window, lowest, total):
    leaf = held.shape[3]
    at = index[slot, i] - lowest
    place = jnp.where((slot < live) & (at >= 0) & (at < total), at, total)
    return mm(held[n, k], window[blocks(place, 1, leaf), :])


def near_most(index, count, tiles_hbm, other, src, bulk1, acc1, acc2, tiles2, tiles1, window, sems1, sems2):
    leaves, slots, leaf, _ = other.shape
    device = lax.axis_index("leaf")
    odd = lax.rem(device, 2)
    core = lax.axis_index("col")
    base1 = (1 - odd) * (leaves - CHILD)
    base2 = odd * (leaves - CHILD)
    loads2 = load_tiles(tiles_hbm, tiles2, sems2, base2)
    loads1 = load_tiles(tiles_hbm, tiles1, sems1, base1)
    total = leaves + CHILD
    window[blocks(odd * CHILD, leaves, leaf), :] = src[pl.ds(0, leaves * leaf), :]
    window[blocks((1 - odd) * leaves, CHILD, leaf), :] = bulk1[pl.ds(bulk1.shape[0] - CHILD * leaf, CHILD * leaf), :]
    window[pl.ds(total * leaf, leaf), :] = jnp.zeros((leaf, src.shape[1]), BF16)
    lowest = device * leaves - odd * CHILD

    def others2(n, _):
        i = base2 + n
        acc2[blocks(n, 1, leaf), :] = sum(
            product(index, count[i], other, i, k, (1 - core) * slots + k, i, src, device * leaves, leaves)
            for k in range(slots)
        )
        return 0

    lax.fori_loop(0, CHILD, others2, 0, unroll=4)
    for load in loads2:
        load.wait()

    def own2(n, _):
        i = base2 + n
        acc2[blocks(n, 1, leaf), :] += sum(
            product(index, count[i], tiles2, n, k, core * slots + k, i, src, device * leaves, leaves)
            for k in range(slots)
        )
        return 0

    lax.fori_loop(0, CHILD, own2, 0, unroll=4)
    for load in loads1:
        load.wait()

    def all1(n, _):
        i = base1 + n
        acc1[blocks(n, 1, leaf), :] = sum(
            product(index, count[i], held, at, k, owner * slots + k, i, window, lowest, total)
            for held, at, owner in ((tiles1, n, core), (other, i, 1 - core))
            for k in range(slots)
        )
        return 0

    lax.fori_loop(0, CHILD, all1, 0, unroll=2)


def downward(
    leaf_far, mid_far,
    near1, near2, coef, bulk1, plane, next_a, next_b,
    basis, leaf_coupling, up_leaf, mid_coupling, up_mid, top_coupling,
    *refs,
):
    total_top = top_coupling.shape[0]
    tops = refs[: total_top - 1]
    out, acc2, turned, full, down, window, chosen, stack, sems = refs[total_top - 1 :]
    leaves, rank, leaf = basis.shape
    mids = up_leaf.shape[0]
    group = CHILD // mids
    device = lax.axis_index("leaf")
    odd = lax.rem(device, 2)
    parent = device // group
    member = lax.rem(device, group)

    stack[blocks(parent, 1, rank), :] = jnp.zeros((rank, full.shape[1]), BF16)
    for p in range(1, total_top):
        stack[blocks(jnp.bitwise_xor(parent, p), 1, rank), :] = tops[p - 1][...]
    top_field = mm(top_coupling[parent], stack[...]).astype(BF16)

    total = leaves + CHILD
    lowest = device * leaves - odd * CHILD
    window[blocks(odd * CHILD, leaves, rank), :] = coef[...]
    window[blocks((1 - odd) * leaves, CHILD, rank), :] = bulk1[pl.ds(0, CHILD * rank), :]
    window[pl.ds(total * rank, rank), :] = jnp.zeros((rank, full.shape[1]), BF16)

    for q in range(mids):
        for f in range(FAR):
            b = mid_far[q, f]
            above = b // CHILD
            inside = lax.rem(b, CHILD)
            place = jnp.bitwise_xor(inside // mids, member) * mids + lax.rem(inside, mids)
            row = blocks(place, 1, rank)
            to = pl.ds((q * FAR + f) * rank, rank)
            beside = jnp.bitwise_xor(parent, 1)

            @pl.when(above == parent)
            def _():
                chosen[to, :] = plane[row, :]

            @pl.when(above == beside)
            def _():
                chosen[to, :] = next_a[row, :]

            @pl.when((above != parent) & (above != beside))
            def _():
                chosen[to, :] = next_b[row, :]

    for q in range(mids):
        picked = chosen[pl.ds(q * FAR * rank, FAR * rank), :]
        mid_field = (mm(mid_coupling[q], picked) + mm_t(up_mid[q], top_field)).astype(BF16)
        down[pl.ds(q * CHILD * rank, CHILD * rank), :] = mm_t(up_leaf[q], mid_field)

    def field_of(i):
        field = far_sum(leaf_far, leaf_coupling, window, i, lowest, total)
        return (field + down[blocks(i, 1, rank), :]).astype(BF16)

    base1 = (1 - odd) * (leaves - CHILD)
    base2 = odd * (leaves - CHILD)
    stores = []
    for n in range(CHILD):
        rows = pl.ds(n * leaf, leaf)
        full[rows, :] = near1[rows, :] + mm_t(basis[base1 + n], field_of(base1 + n))
        if n % 2 == 1:
            rows = pl.ds((n - 1) * leaf, 2 * leaf)
            stores.append(
                pltpu.make_async_copy(full.at[rows], out.at[blocks(base1 + n - 1, 2, leaf)], sems.at[n // 2])
            )
            stores[-1].start()
    for n in range(CHILD):
        rows = pl.ds(n * leaf, leaf)
        turned[n] = basis[base2 + n].T
        acc2[rows, :] = near2[rows, :] + mm(turned[n], field_of(base2 + n))
    for store in stores:
        store.wait()


def far_sum(leaf_far, leaf_coupling, window, i, lowest, total):
    rank = leaf_coupling.shape[1]
    picked = []
    for f in range(FAR):
        at = leaf_far[f, i] - lowest
        place = jnp.where((at >= 0) & (at < total), at, total)
        picked.append(window[blocks(place, 1, rank), :])
    return mm(leaf_coupling[i], jnp.concatenate(picked, axis=0))


def near_last(work, leaf_far, tiles, other, bulk2, acc_in, leaf_coupling, turned, out_in, out, acc, window, sems):
    leaves, slots, leaf, _ = other.shape
    rank = leaf_coupling.shape[1]
    device = lax.axis_index("leaf")
    odd = lax.rem(device, 2)
    base = odd * (leaves - CHILD)
    window[pl.ds(0, CHILD * rank), :] = bulk2[pl.ds(0, CHILD * rank), :]
    window[pl.ds(CHILD * rank, rank), :] = jnp.zeros((rank, bulk2.shape[1]), BF16)
    lowest = device * leaves + jnp.where(odd == 1, leaves, -CHILD)
    for n in range(CHILD):
        field = far_sum(leaf_far, leaf_coupling, window, base + n, lowest, CHILD)
        acc[pl.ds(n * leaf, leaf), :] += mm(turned[n], field.astype(BF16))
    skip = CHILD * rank

    def step(t, _):
        for b in range(BATCH):
            n = t * BATCH + b
            for r, held, low in ((0, tiles, 0), (1, other, base)):
                tile = work[3 * r, n]
                at = pl.multiple_of(skip + work[3 * r + 1, n] * leaf, rank)
                part = mm(held[low + tile // slots, lax.rem(tile, slots)], bulk2[pl.ds(at, leaf), :])
                acc[blocks(work[3 * r + 2, n], 1, leaf), :] += part
        return 0

    lax.fori_loop(0, work[6, 0], step, 0)
    stores = []
    for n in range(0, CHILD, 2):
        stores.append(
            pltpu.make_async_copy(acc.at[pl.ds(n * leaf, 2 * leaf)], out.at[blocks(base + n, 2, leaf)], sems.at[n // 2])
        )
        stores[-1].start()
    for store in stores:
        store.wait()


def shards(
    sources,
    near_tiles,
    near_index,
    near_count,
    leaf_basis,
    leaf_coupling,
    leaf_far,
    up_leaf,
    mid_coupling,
    mid_far,
    up_mid,
    top_coupling,
):
    sds = jax.ShapeDtypeStruct
    leaves, rank, leaf = leaf_basis.shape
    mids = up_leaf.shape[0]
    cols = sources.shape[1]
    slots = near_tiles.shape[1]
    total_top = top_coupling.shape[0]
    devices = lax.axis_size("leaf")
    group = CHILD // mids
    edge = CHILD * leaf
    edge_c = CHILD * rank
    rows = leaves * leaf
    assert leaves == 2 * CHILD and group >= 2 and total_top >= 4
    product_flops = 2 * leaf * leaf * cols

    rest = [(i, i + 1) for i in range(1, devices - 1, 2)]
    rest = rest + [(j, i) for i, j in rest]

    def swap(k):
        return [(i, i ^ k) for i in range(devices)]

    def send(x, pairs, axis="leaf"):
        return lax.ppermute(x, axis, pairs)

    def call(kernel, out_shape, in_specs, out_specs, scratch, mib, estimate, **more):
        def run(*args):
            return pl.pallas_call(
                kernel,
                out_shape=out_shape,
                in_specs=in_specs,
                out_specs=out_specs,
                scratch_shapes=scratch,
                compiler_params=params(mib),
                cost_estimate=estimate,
                **more,
            )(*args)

        return run

    index, count, far_index, mid_index = map(in_hbm, (near_index.T, near_count, leaf_far.T, mid_far))
    own_tiles = in_hbm(near_tiles)

    pack, bulk1, coef, src = call(
        upward,
        (
            sds(((mids + 1) * rank, cols), BF16),
            sds((edge_c + edge, cols), BF16),
            sds((leaves * rank, cols), BF16),
            sds((rows + leaf, cols), BF16),
        ),
        [HBM] * 4,
        (VMEM,) * 4,
        [
            pltpu.VMEM(leaf_basis.shape, BF16),
            pltpu.VMEM(up_leaf.shape, BF16),
            pltpu.VMEM(up_mid.shape, BF16),
            pltpu.SemaphoreType.DMA((2 * PARTS + 2,)),
        ],
        8,
        cost(2 * leaves * rank * leaf * cols, 4 << 20),
    )(*map(in_hbm, (sources, leaf_basis, up_leaf, up_mid)))
    src = in_vmem(src)

    pack1 = send(pack, swap(1))
    bulk1 = send(bulk1, swap(1))
    other = in_vmem(send(near_tiles, [(0, 1), (1, 0)], "col"))

    work, bulk2 = call(
        prepare,
        (sds((7, CHILD * slots + BATCH), jnp.int32), sds((edge_c + edge, cols), BF16)),
        [SMEM, SMEM, VMEM, VMEM],
        (SMEM, VMEM),
        [],
        8,
        cost(0, 4 << 20),
    )(index, count, coef, src)

    held = mids * rank
    plane = jnp.concatenate([pack[:held], pack1[:held]], axis=0)
    total = pack[held : held + rank].astype(F32) + pack1[held : held + rank].astype(F32)
    total = total.astype(BF16)
    k = 2
    while k < group:
        got = send(jnp.concatenate([plane, total], axis=0), swap(k))
        held = plane.shape[0]
        plane = jnp.concatenate([plane, got[:held]], axis=0)
        total = (total.astype(F32) + got[held:].astype(F32)).astype(BF16)
        k *= 2

    tops = [send(total, swap(k * group)) for k in range(1, total_top)]
    beyond = [(i, i + group) for i in range(group, devices - group) if i % (2 * group) >= group]
    next_a = send(plane, swap(group))
    next_b = send(plane, beyond + [(j, i) for i, j in beyond])
    bulk2 = send(bulk2, rest)

    half_tiles = (CHILD,) + near_tiles.shape[1:]
    near1, near2, tiles2 = call(
        near_most,
        (sds((edge, cols), F32), sds((edge, cols), F32), sds(half_tiles, BF16)),
        [SMEM, SMEM, HBM] + [VMEM] * 3,
        (VMEM,) * 3,
        [
            pltpu.VMEM(half_tiles, BF16),
            pltpu.VMEM((rows + edge + leaf, cols), BF16),
            pltpu.SemaphoreType.DMA((CHILD,)),
            pltpu.SemaphoreType.DMA((CHILD,)),
        ],
        20,
        cost(leaves * 2 * slots * product_flops, 16 << 20),
    )(index, count, own_tiles, other, src, bulk1)

    out, acc2, turned = call(
        downward,
        (sds((rows, cols), F32), sds((edge + leaf, cols), F32), sds((CHILD, leaf, rank), BF16)),
        [SMEM] * 2 + [VMEM] * (12 + total_top),
        (ANY, VMEM, VMEM),
        [
            pltpu.VMEM((edge, cols), F32),
            pltpu.VMEM((leaves * rank, cols), F32),
            pltpu.VMEM((edge_c + (leaves + 1) * rank, cols), BF16),
            pltpu.VMEM((mids * FAR * rank, cols), BF16),
            pltpu.VMEM((total_top * rank, cols), BF16),
            pltpu.SemaphoreType.DMA((CHILD // 2,)),
        ],
        16,
        cost(leaves * 4 * product_flops, 12 << 20),
    )(
        far_index, mid_index,
        near1, near2, coef, bulk1, plane, next_a, next_b,
        leaf_basis, leaf_coupling, up_leaf, mid_coupling, up_mid, top_coupling, *tops,
    )

    product, _ = call(
        near_last,
        (sds((rows, cols), F32), sds((edge + leaf, cols), F32)),
        [SMEM] * 2 + [VMEM] * 6 + [ANY],
        (ANY, VMEM),
        [pltpu.VMEM((edge_c + rank, cols), BF16), pltpu.SemaphoreType.DMA((CHILD // 2,))],
        8,
        cost(leaves * slots * product_flops, 4 << 20),
        input_output_aliases={8: 0, 5: 1},
    )(work, far_index, in_vmem(tiles2), other, bulk2, in_vmem(acc2), leaf_coupling, turned, out)
    return product


def solution(mesh):


    return jax.shard_map(
        shards,
        mesh=mesh,
        in_specs=(
            P("leaf", "col"),
            P("leaf", "col", None, None),
            P("leaf", None),
            P("leaf"),
            P("leaf", None, None),
            P("leaf", None, None),
            P("leaf", None),
            P("leaf", None, None),
            P("leaf", None, None),
            P("leaf", None),
            P("leaf", None, None),
            P(),
        ),
        out_specs=P("leaf", "col"),
        check_vma=False,
    )
```

time: 57.2 us -> 55.8 us (0.976); the launches traced: 57 us -> 54.9 us
  Pallas kernels: 22.2 us -> 18.9 us
  waiting for transfers between devices: 16 us -> 18.3 us
  starting transfers between devices: 18.4 us -> 17.5 us
    pallas_call x6 -> x5, Pallas kernels: 22.2 us -> 18.9 us  [run(): pl.pallas_call(kernel, out_shape=out_shape, in_specs=in_specs, out_specs=...]
    ppermute x9 -> x10, waiting for transfers between devices: 16 us -> 18.3 us  [send(): return lax.ppermute(x, axis, pairs)]
    ppermute x9 -> x10, starting transfers between devices: 18.4 us -> 17.5 us  [send(): return lax.ppermute(x, axis, pairs)]
  transfers between devices with their start and end apart: 9 -> 10, of which waited for: 2 -> 3; matrix products, arithmetic and copies ran while one was open for 0% -> 0% of each run, Pallas kernels for 36% -> 30%
where the time goes in v2:
time: 55.8 us; the launch traced here: 54.9 us
  Pallas kernels  18.9 us (34%)
  waiting for transfers between devices  18.3 us (33%)
  starting transfers between devices  17.5 us (31%)
    pallas_call x5, Pallas kernels, run(): pl.pallas_call(kernel, out_shape=out_shape, in_specs=in_specs, out_specs=...  18.9 us
    ppermute x10, waiting for transfers between devices, send(): return lax.ppermute(x, axis, pairs)  18.3 us
    ppermute x10, starting transfers between devices, send(): return lax.ppermute(x, axis, pairs)  17.5 us
  transfers between devices with their start and end apart: 10, of which 3 were waited for; matrix products, arithmetic and copies ran while one was open for 0% of the time, Pallas kernels for 30%

profile of v2, /device:TPU:0, one launch (start us, length us, event | category | flops | bytes accessed | tf_op | source)
XLA Modules:
  0.0 54.9 jit_solution(7753173785585574701)
XLA Ops:
  0.0 0.5 collective-permute-start
  0.5 2.2 %shard_map.118 = (bf16[192,128]{1,0:T(8,128)(2,1)S(1)}, bf16[2560,128]{1,0:T(8,128)(2,1)S(1)}, bf16[1024,128]{1,0:T(8,128)(2,1)S(1)}, bf16[4352,128]{1,0:T(8,128)(2,1)S(1)}) custom-call(bf16[4096,128]{1,0:T(8,128)(2,1)} %src_hbm.1, bf16[16,64,256]{2,1,0:T(8,128)(2,1)} %basis.1, bf16[2,64,512]{2,1,0:T(8,128)(2,1)} %up_leaf.1, bf16[2,64,64]{2,1,0:T(8,128)(2,1)} %up_mid.1), custom_call_target="tpu_custom_call" | custom-call | flops 67108864 | bytes 4194304 | tf_op jit(solution)/shard_map/pallas_call | solution.py:364
  2.7 2.5 %collective-permute-start.3 = (bf16[192,128]{1,0:T(8,128)(2,1)S(1)}, bf16[192,128]{1,0:T(8,128)(2,1)S(1)}, u32[]{:S(2)}, u32[]{:S(2)}) collective-permute-start(bf16[192,128]{1,0:T(8,128)(2,1)S(1)} %get-tuple-element.26), channel_id=1, source_target_pairs={{0,2},{2,0},{4,6},{6,4},{8,10},{10,8},{12,14},{14,12},{16,18},{18,... | collective-permute-start | bytes 147464 | tf_op jit(solution)/shard_map/ppermute | solution.py:360
  5.3 0.1 collective-permute-start.1
  5.4 2.3 %collective-permute-done.3 = bf16[192,128]{1,0:T(8,128)(2,1)S(1)} collective-permute-done((bf16[192,128]{1,0:T(8,128)(2,1)S(1)}, bf16[192,128]{1,0:T(8,128)(2,1)S(1)}, u32[]{:S(2)}, u32[]{:S(2)}) %collective-permute-start.3) | collective-permute-done | bytes 49184 | tf_op jit(solution)/shard_map/ppermute | solution.py:360
  7.7 1.8 %collective-permute-start.4 = (bf16[320,128]{1,0:T(8,128)(2,1)S(1)}, bf16[320,128]{1,0:T(8,128)(2,1)S(1)}, u32[]{:S(2)}, u32[]{:S(2)}) collective-permute-start(bf16[320,128]{1,0:T(8,128)(2,1)S(1)} %pad_maximum_fusion.1), channel_id=1, source_target_pairs={{0,4},{2,6},{4,0},{6,2},{8,12},{10,14},{12,8},{14,10},{16,20},{18,... | collective-permute-start | bytes 245768 | tf_op jit(solution)/shard_map/ppermute | solution.py:360
  9.6 2.0 %shard_map.119 = (s32[7,36]{1,0:T(8,128)S(1)}, bf16[2560,128]{1,0:T(8,128)(2,1)S(1)}) custom-call(s32[8,16]{1,0:T(8,128)} %bitcast.2, s32[16]{0:T(128)} %count.3, bf16[1024,128]{1,0:T(8,128)(2,1)S(1)} %get-tuple-element.18.coef, bf16[4352,128]{1,0:T(8,128)(2,1)S(1)} %get-tuple-element.19.src), custom_call_target="tpu_custom_call" | custom-call | bytes 4194304 | tf_op jit(solution)/shard_map/pallas_call | solution.py:364
  11.5 0.7 %collective-permute-start.2 = (bf16[2560,128]{1,0:T(8,128)(2,1)S(1)}, bf16[2560,128]{1,0:T(8,128)(2,1)S(1)}, u32[]{:S(2)}, u32[]{:S(2)}) collective-permute-start(bf16[2560,128]{1,0:T(8,128)(2,1)S(1)} %get-tuple-element.23), channel_id=1, source_target_pairs={{2,4},{6,8},{10,12},{14,16},{18,20},{22,24},{26,28},{4,2},{8,6},{1... | collective-permute-start | bytes 1966088 | tf_op jit(solution)/shard_map/ppermute | solution.py:360
  12.2 0.0 collective-permute-done.4
  12.3 6.7 %collective-permute-start.9 = (bf16[64,128]{1,0:T(8,128)(2,1)S(1)}, bf16[64,128]{1,0:T(8,128)(2,1)S(1)}, u32[]{:S(2)}, u32[]{:S(2)}) collective-permute-start(bf16[64,128]{1,0:T(8,128)(2,1)S(1)} %add_convert_fusion), channel_id=1, source_target_pairs={{0,24},{2,26},{4,28},{6,30},{8,16},{10,18},{12,20},{14,22},{16,8},... | collective-permute-start | bytes 49160 | tf_op jit(solution)/shard_map/ppermute | solution.py:360
  19.0 0.0 collective-permute-start.8
  19.0 0.0 copy-start
  19.0 0.0 copy-start.1
  19.0 0.0 copy-start.2
  19.1 0.0 copy-start.3
  19.1 0.0 copy-start.4
  19.1 0.0 copy-start.5
  19.1 14.1 %collective-permute-done.9.refs_2_ = bf16[64,128]{1,0:T(8,128)(2,1)S(1)} collective-permute-done((bf16[64,128]{1,0:T(8,128)(2,1)S(1)}, bf16[64,128]{1,0:T(8,128)(2,1)S(1)}, u32[]{:S(2)}, u32[]{:S(2)}) %collective-permute-start.9) | collective-permute-done | bytes 16416 | tf_op jit(solution)/shard_map/ppermute | solution.py:360
  33.1 0.0 collective-permute-start.7
  33.2 1.9 %collective-permute-done.1.bulk1 = bf16[2560,128]{1,0:T(8,128)(2,1)S(1)} collective-permute-done((bf16[2560,128]{1,0:T(8,128)(2,1)S(1)}, bf16[2560,128]{1,0:T(8,128)(2,1)S(1)}, u32[]{:S(2)}, u32[]{:S(2)}) %collective-permute-start.1) | collective-permute-done | bytes 655392 | tf_op jit(solution)/shard_map/ppermute | solution.py:360
  35.0 0.7 %collective-permute-start.6 = (bf16[512,128]{1,0:T(8,128)(2,1)S(1)}, bf16[512,128]{1,0:T(8,128)(2,1)S(1)}, u32[]{:S(2)}, u32[]{:S(2)}) collective-permute-start(bf16[512,128]{1,0:T(8,128)(2,1)S(1)} %pad_maximum_fusion.plane), channel_id=1, source_target_pairs={{8,16},{10,18},{12,20},{14,22},{16,8},{18,10},{20,12},{22,14},{9,1... | collective-permute-start | bytes 393224 | tf_op jit(solution)/shard_map/ppermute | solution.py:360
  35.7 0.0 collective-permute-done.other
  35.7 4.5 %collective-permute-start.5 = (bf16[512,128]{1,0:T(8,128)(2,1)S(1)}, bf16[512,128]{1,0:T(8,128)(2,1)S(1)}, u32[]{:S(2)}, u32[]{:S(2)}) collective-permute-start(bf16[512,128]{1,0:T(8,128)(2,1)S(1)} %pad_maximum_fusion.plane), channel_id=1, source_target_pairs={{0,8},{2,10},{4,12},{6,14},{8,0},{10,2},{12,4},{14,6},{16,24},{18,... | collective-permute-start | bytes 393224 | tf_op jit(solution)/shard_map/ppermute | solution.py:360
  40.2 8.4 %shard_map.120 = (f32[2048,128]{1,0:T(8,128)S(1)}, f32[2048,128]{1,0:T(8,128)S(1)}, bf16[8,4,256,256]{3,2,1,0:T(8,128)(2,1)S(1)}) custom-call(s32[8,16]{1,0:T(8,128)} %bitcast.3, s32[16]{0:T(128)} %count.3, bf16[16,4,256,256]{3,2,1,0:T(8,128)(2,1)} %tiles_hbm.1, bf16[16,4,256,256]{3,2,1,0:T(8,128)(2,1)S(1)} %collective-permute-done.other, ...), custom_call_target="tpu_custom_call" | custom-call | flops 2147483648 | bytes 16777216 | tf_op jit(solution)/shard_map/pallas_call | solution.py:364
  48.5 0.0 collective-permute-done.8.refs_1_
  48.5 0.0 collective-permute-done.7.refs_0_
  48.5 0.0 collective-permute-done.6.next_b
  48.6 0.0 collective-permute-done.5.next_a
  48.6 0.0 copy-done
  48.6 3.7 %shard_map.121 = (f32[4096,128]{1,0:T(8,128)}, f32[2304,128]{1,0:T(8,128)S(1)}, bf16[8,256,64]{2,1,0:T(8,128)(2,1)S(1)}) custom-call(s32[4,16]{1,0:T(4,128)} %bitcast.4, s32[2,4]{1,0:T(2,128)} %mid_far.1, f32[2048,128]{1,0:T(8,128)S(1)} %get-tuple-element.24.near1, f32[2048,128]{1,0:T(8,128)S(1)} %get-tuple-element.25.near2, ...), custom_call_target="tpu_custom_call" | custom-call | flops 1073741824 | bytes 12582912 | tf_op jit(solution)/shard_map/pallas_call | solution.py:364
  52.3 0.0 collective-permute-done.2.bulk2
  52.3 2.6 %shard_map.122 = (f32[4096,128]{1,0:T(8,128)}, f32[2304,128]{1,0:T(8,128)S(1)}) custom-call(s32[7,36]{1,0:T(8,128)S(1)} %get-tuple-element.20.work, s32[4,16]{1,0:T(4,128)} %bitcast.5, bf16[8,4,256,256]{3,2,1,0:T(8,128)(2,1)S(1)} %get-tuple-element.22.tiles, ...), custom_call_target="tpu_custom_call", output_to_operand_aliasing={{0}: (8, {}), {1}: (5, {})} | custom-call | flops 1073741824 | bytes 4194304 | tf_op jit(solution)/shard_map/pallas_call | solution.py:364
  (12 shorter events, 0.1 us)
Async XLA Ops:
  0.0 35.7 %collective-permute-start = (bf16[16,4,256,256]{3,2,1,0:T(8,128)(2,1)}, bf16[16,4,256,256]{3,2,1,0:T(8,128)(2,1)S(1)}, u32[]{:S(2)}, u32[]{:S(2)}) collective-permute-start(bf16[16,4,256,256]{3,2,1,0:T(8,128)(2,1)} %tiles_hbm.1), channel_id=1, source_target_pairs={{0,1},{1,0},{2,3},{3,2},{4,5},{5,4},{6,7},{7,6},{8,9},{9,8},{10,11... | collective-permute-start | bytes 25165832 | tf_op jit(solution)/shard_map/ppermute | solution.py:360
  2.7 4.9 %collective-permute-start.3 = (bf16[192,128]{1,0:T(8,128)(2,1)S(1)}, bf16[192,128]{1,0:T(8,128)(2,1)S(1)}, u32[]{:S(2)}, u32[]{:S(2)}) collective-permute-start(bf16[192,128]{1,0:T(8,128)(2,1)S(1)} %get-tuple-element.26), channel_id=1, source_target_pairs={{0,2},{2,0},{4,6},{6,4},{8,10},{10,8},{12,14},{14,12},{16,18},{18,... | collective-permute-start | bytes 147464 | tf_op jit(solution)/shard_map/ppermute | solution.py:360
  5.3 29.8 %collective-permute-start.1 = (bf16[2560,128]{1,0:T(8,128)(2,1)S(1)}, bf16[2560,128]{1,0:T(8,128)(2,1)S(1)}, u32[]{:S(2)}, u32[]{:S(2)}) collective-permute-start(bf16[2560,128]{1,0:T(8,128)(2,1)S(1)} %get-tuple-element.21), channel_id=1, source_target_pairs={{0,2},{2,0},{4,6},{6,4},{8,10},{10,8},{12,14},{14,12},{16,18},{18,... | collective-permute-start | bytes 1966088 | tf_op jit(solution)/shard_map/ppermute | solution.py:360
  7.7 4.5 %collective-permute-start.4 = (bf16[320,128]{1,0:T(8,128)(2,1)S(1)}, bf16[320,128]{1,0:T(8,128)(2,1)S(1)}, u32[]{:S(2)}, u32[]{:S(2)}) collective-permute-start(bf16[320,128]{1,0:T(8,128)(2,1)S(1)} %pad_maximum_fusion.1), channel_id=1, source_target_pairs={{0,4},{2,6},{4,0},{6,2},{8,12},{10,14},{12,8},{14,10},{16,20},{18,... | collective-permute-start | bytes 245768 | tf_op jit(solution)/shard_map/ppermute | solution.py:360
  11.5 40.8 %collective-permute-start.2 = (bf16[2560,128]{1,0:T(8,128)(2,1)S(1)}, bf16[2560,128]{1,0:T(8,128)(2,1)S(1)}, u32[]{:S(2)}, u32[]{:S(2)}) collective-permute-start(bf16[2560,128]{1,0:T(8,128)(2,1)S(1)} %get-tuple-element.23), channel_id=1, source_target_pairs={{2,4},{6,8},{10,12},{14,16},{18,20},{22,24},{26,28},{4,2},{8,6},{1... | collective-permute-start | bytes 1966088 | tf_op jit(solution)/shard_map/ppermute | solution.py:360
  12.3 20.9 %collective-permute-start.9 = (bf16[64,128]{1,0:T(8,128)(2,1)S(1)}, bf16[64,128]{1,0:T(8,128)(2,1)S(1)}, u32[]{:S(2)}, u32[]{:S(2)}) collective-permute-start(bf16[64,128]{1,0:T(8,128)(2,1)S(1)} %add_convert_fusion), channel_id=1, source_target_pairs={{0,24},{2,26},{4,28},{6,30},{8,16},{10,18},{12,20},{14,22},{16,8},... | collective-permute-start | bytes 49160 | tf_op jit(solution)/shard_map/ppermute | solution.py:360
  19.0 29.5 %collective-permute-start.8 = (bf16[64,128]{1,0:T(8,128)(2,1)S(1)}, bf16[64,128]{1,0:T(8,128)(2,1)S(1)}, u32[]{:S(2)}, u32[]{:S(2)}) collective-permute-start(bf16[64,128]{1,0:T(8,128)(2,1)S(1)} %add_convert_fusion), channel_id=1, source_target_pairs={{0,16},{2,18},{4,20},{6,22},{8,24},{10,26},{12,28},{14,30},{16,0},... | collective-permute-start | bytes 49160 | tf_op jit(solution)/shard_map/ppermute | solution.py:360
  19.0 29.5 %copy-start = (bf16[16,64,256]{2,1,0:T(8,128)(2,1)S(1)}, bf16[16,64,256]{2,1,0:T(8,128)(2,1)}, u32[]{:S(2)}) copy-start(bf16[16,64,256]{2,1,0:T(8,128)(2,1)} %leaf_coupling.3) | copy-start | bytes 1572868
  19.0 29.5 %copy-start.1 = (bf16[16,64,256]{2,1,0:T(8,128)(2,1)S(1)}, bf16[16,64,256]{2,1,0:T(8,128)(2,1)}, u32[]{:S(2)}) copy-start(bf16[16,64,256]{2,1,0:T(8,128)(2,1)} %basis.1) | copy-start | bytes 1572868
  19.0 29.5 %copy-start.2 = (bf16[2,64,512]{2,1,0:T(8,128)(2,1)S(1)}, bf16[2,64,512]{2,1,0:T(8,128)(2,1)}, u32[]{:S(2)}) copy-start(bf16[2,64,512]{2,1,0:T(8,128)(2,1)} %up_leaf.1) | copy-start | bytes 393220
  19.1 29.5 %copy-start.3 = (bf16[2,64,64]{2,1,0:T(8,128)(2,1)S(1)}, bf16[2,64,64]{2,1,0:T(8,128)(2,1)}, u32[]{:S(2)}) copy-start(bf16[2,64,64]{2,1,0:T(8,128)(2,1)} %up_mid.1) | copy-start | bytes 49156
  19.1 29.5 %copy-start.4 = (bf16[4,64,256]{2,1,0:T(8,128)(2,1)S(1)}, bf16[4,64,256]{2,1,0:T(8,128)(2,1)}, u32[]{:S(2)}) copy-start(bf16[4,64,256]{2,1,0:T(8,128)(2,1)} %top_coupling.1) | copy-start | bytes 393220
  19.1 29.5 %copy-start.5 = (bf16[2,64,256]{2,1,0:T(8,128)(2,1)S(1)}, bf16[2,64,256]{2,1,0:T(8,128)(2,1)}, u32[]{:S(2)}) copy-start(bf16[2,64,256]{2,1,0:T(8,128)(2,1)} %mid_coupling.1) | copy-start | bytes 196612
  33.1 15.4 %collective-permute-start.7 = (bf16[64,128]{1,0:T(8,128)(2,1)S(1)}, bf16[64,128]{1,0:T(8,128)(2,1)S(1)}, u32[]{:S(2)}, u32[]{:S(2)}) collective-permute-start(bf16[64,128]{1,0:T(8,128)(2,1)S(1)} %add_convert_fusion), channel_id=1, source_target_pairs={{0,8},{2,10},{4,12},{6,14},{8,0},{10,2},{12,4},{14,6},{16,24},{18,... | collective-permute-start | bytes 49160 | tf_op jit(solution)/shard_map/ppermute | solution.py:360
  35.0 13.5 %collective-permute-start.6 = (bf16[512,128]{1,0:T(8,128)(2,1)S(1)}, bf16[512,128]{1,0:T(8,128)(2,1)S(1)}, u32[]{:S(2)}, u32[]{:S(2)}) collective-permute-start(bf16[512,128]{1,0:T(8,128)(2,1)S(1)} %pad_maximum_fusion.plane), channel_id=1, source_target_pairs={{8,16},{10,18},{12,20},{14,22},{16,8},{18,10},{20,12},{22,14},{9,1... | collective-permute-start | bytes 393224 | tf_op jit(solution)/shard_map/ppermute | solution.py:360
  35.7 12.9 %collective-permute-start.5 = (bf16[512,128]{1,0:T(8,128)(2,1)S(1)}, bf16[512,128]{1,0:T(8,128)(2,1)S(1)}, u32[]{:S(2)}, u32[]{:S(2)}) collective-permute-start(bf16[512,128]{1,0:T(8,128)(2,1)S(1)} %pad_maximum_fusion.plane), channel_id=1, source_target_pairs={{0,8},{2,10},{4,12},{6,14},{8,0},{10,2},{12,4},{14,6},{16,24},{18,... | collective-permute-start | bytes 393224 | tf_op jit(solution)/shard_map/ppermute | solution.py:360

commit v3 on v2

--- a/solution.py
+++ b/solution.py
@@ -86,7 +86,7 @@
     pack[pl.ds(mids * rank, rank), :] = total.astype(BF16)
 
 
-def prepare(index, count, coef, src, work, bulk2):
+def prepare(index, count, leaf_far, coef, src, work, bulk2):
     leaves = index.shape[1]
     slots = index.shape[0] // 2
     rank = coef.shape[0] // leaves
@@ -99,35 +99,84 @@
     bulk2[pl.ds(CHILD * rank, CHILD * leaf), :] = src[blocks(base, CHILD, leaf), :]
     lowest = jnp.where(odd == 1, leaves, -CHILD) + device * leaves
 
-    def row(n, found):
-        live = count[base + n]
-        out = []
-        for r, owner in ((0, core), (1, 1 - core)):
-            at = found[r]
-            for k in range(slots):
-                slot = owner * slots + k
-                outside = index[slot, base + n] - lowest
-                work[3 * r, at] = n * slots + k
-                work[3 * r + 1, at] = outside
-                work[3 * r + 2, at] = n
-                use = (slot < live) & (outside >= 0) & (outside < CHILD)
-                at = at + use.astype(jnp.int32)
-            out.append(at)
-        return tuple(out)
-
-    found = lax.fori_loop(0, CHILD, row, (jnp.int32(0), jnp.int32(0)))
-    longest = jnp.maximum(found[0], found[1])
-    rounds = (longest + BATCH - 1) // BATCH
-    work[6, 0] = rounds
-    for r in range(2):
-
-        def fill(n, _):
-            work[3 * r, n] = 0
-            work[3 * r + 1, n] = 0
-            work[3 * r + 2, n] = CHILD
-            return 0
-
-        lax.fori_loop(found[r], rounds * BATCH, fill, 0)
+    room = work.shape[1] // 2
+    for part in range(2):
+        start = jnp.bitwise_xor(part, odd) * (CHILD // 2)
+
+        def row(t, found):
+            n = start + t
+            live = count[base + n]
+            for f in range(FAR):
+                at = leaf_far[f, base + n] - lowest
+                work[7 + f, n] = jnp.where((at >= 0) & (at < CHILD), at, CHILD)
+            out = []
+            for r, owner in ((0, core), (1, 1 - core)):
+                at = found[r]
+                for k in range(slots):
+                    slot = owner * slots + k
+                    outside = index[slot, base + n] - lowest
+                    work[3 * r, at] = n * slots + k
+                    work[3 * r + 1, at] = outside
+                    work[3 * r + 2, at] = n
+                    use = (slot < live) & (outside >= 0) & (outside < CHILD)
+                    at = at + use.astype(jnp.int32)
+                out.append(at)
+            return tuple(out)
+
+        begin = jnp.int32(part * room)
+        found = lax.fori_loop(0, CHILD // 2, row, (begin, begin))
+        rounds = (jnp.maximum(found[0], found[1]) - begin + BATCH - 1) // BATCH
+        work[6, part] = rounds
+        for r in range(2):
+
+            def fill(n, _):
+                work[3 * r, n] = 0
+                work[3 * r + 1, n] = 0
+                work[3 * r + 2, n] = CHILD
+                return 0
+
+            lax.fori_loop(found[r], begin + rounds * BATCH, fill, 0)
+
+
+def fold(basis_hbm, coupling_hbm, folded, basis, coupling, sems):
+    leaves = basis_hbm.shape[0]
+    base = lax.rem(lax.axis_index("leaf"), 2) * (leaves - CHILD)
+    loads = [
+        pltpu.make_async_copy(a.at[pl.ds(base, CHILD)], b, sems.at[k])
+        for k, (a, b) in enumerate(((basis_hbm, basis), (coupling_hbm, coupling)))
+    ]
+    for load in loads:
+        load.start()
+    for load in loads:
+        load.wait()
+    for n in range(CHILD):
+        folded[n] = mm_t(basis[n], coupling[n]).astype(BF16)
+
+
+def join(pack, pack1, pair, part):
+    held = part.shape[0]
+    mids = pack.shape[0] - held
+    total = pack[pl.ds(mids, held), :].astype(F32) + pack1[pl.ds(mids, held), :].astype(F32)
+    pair[pl.ds(0, mids), :] = pack[pl.ds(0, mids), :]
+    pair[pl.ds(mids, mids), :] = pack1[pl.ds(0, mids), :]
+    pair[pl.ds(2 * mids, held), :] = total.astype(BF16)
+    part[...] = total.astype(BF16)
+
+
+def cluster(pair, pair1, plane):
+    mids = plane.shape[0] - pair.shape[0]
+    held = pair.shape[0] - mids
+    plane[pl.ds(0, mids), :] = pair[pl.ds(0, mids), :]
+    plane[pl.ds(mids, mids), :] = pair1[pl.ds(0, mids), :]
+    total = pair[pl.ds(mids, held), :].astype(F32) + pair1[pl.ds(mids, held), :].astype(F32)
+    plane[pl.ds(2 * mids, held), :] = total.astype(BF16)
+
+
+def stacked(*refs):
+    out = refs[-1]
+    held = refs[0].shape[0]
+    for k, part in enumerate(refs[:-1]):
+        out[pl.ds(k * held, held), :] = part[...]
 
 
 def load_tiles(tiles_hbm, tiles, sems, base):
@@ -200,13 +249,12 @@
 
 def downward(
     leaf_far, mid_far,
-    near1, near2, coef, bulk1, plane, next_a, next_b,
+    near1, near2, coef, bulk1, plane, next_a, next_b, beyond0, beyond1,
     basis, leaf_coupling, up_leaf, mid_coupling, up_mid, top_coupling,
-    *refs,
+    out, acc2,
+    full, down, window, chosen, stack, sems,
 ):
     total_top = top_coupling.shape[0]
-    tops = refs[: total_top - 1]
-    out, acc2, turned, full, down, window, chosen, stack, sems = refs[total_top - 1 :]
     leaves, rank, leaf = basis.shape
     mids = up_leaf.shape[0]
     group = CHILD // mids
@@ -216,8 +264,11 @@
     member = lax.rem(device, group)
 
     stack[blocks(parent, 1, rank), :] = jnp.zeros((rank, full.shape[1]), BF16)
-    for p in range(1, total_top):
-        stack[blocks(jnp.bitwise_xor(parent, p), 1, rank), :] = tops[p - 1][...]
+    stack[blocks(jnp.bitwise_xor(parent, 1), 1, rank), :] = next_a[pl.ds(CHILD * rank, rank), :]
+    for p in range(2, total_top):
+        rows = pl.ds((p - 2) * rank, rank)
+        top = beyond0[rows, :].astype(F32) + beyond1[rows, :].astype(F32)
+        stack[blocks(jnp.bitwise_xor(parent, p), 1, rank), :] = top.astype(BF16)
     top_field = mm(top_coupling[parent], stack[...]).astype(BF16)
 
     total = leaves + CHILD
@@ -271,8 +322,7 @@
             stores[-1].start()
     for n in range(CHILD):
         rows = pl.ds(n * leaf, leaf)
-        turned[n] = basis[base2 + n].T
-        acc2[rows, :] = near2[rows, :] + mm(turned[n], field_of(base2 + n))
+        acc2[rows, :] = near2[rows, :] + mm_t(basis[base2 + n], field_of(base2 + n))
     for store in stores:
         store.wait()
 
@@ -287,35 +337,37 @@
     return mm(leaf_coupling[i], jnp.concatenate(picked, axis=0))
 
 
-def near_last(work, leaf_far, tiles, other, bulk2, acc_in, leaf_coupling, turned, out_in, out, acc, window, sems):
+def near_last(work, tiles, other, bulk2, acc_in, folded, out_in, out, acc, window, sems):
     leaves, slots, leaf, _ = other.shape
-    rank = leaf_coupling.shape[1]
-    device = lax.axis_index("leaf")
-    odd = lax.rem(device, 2)
+    rank = window.shape[0] // (CHILD + 1)
+    odd = lax.rem(lax.axis_index("leaf"), 2)
     base = odd * (leaves - CHILD)
     window[pl.ds(0, CHILD * rank), :] = bulk2[pl.ds(0, CHILD * rank), :]
     window[pl.ds(CHILD * rank, rank), :] = jnp.zeros((rank, bulk2.shape[1]), BF16)
-    lowest = device * leaves + jnp.where(odd == 1, leaves, -CHILD)
-    for n in range(CHILD):
-        field = far_sum(leaf_far, leaf_coupling, window, base + n, lowest, CHILD)
-        acc[pl.ds(n * leaf, leaf), :] += mm(turned[n], field.astype(BF16))
     skip = CHILD * rank
-
-    def step(t, _):
-        for b in range(BATCH):
-            n = t * BATCH + b
-            for r, held, low in ((0, tiles, 0), (1, other, base)):
-                tile = work[3 * r, n]
-                at = pl.multiple_of(skip + work[3 * r + 1, n] * leaf, rank)
-                part = mm(held[low + tile // slots, lax.rem(tile, slots)], bulk2[pl.ds(at, leaf), :])
-                acc[blocks(work[3 * r + 2, n], 1, leaf), :] += part
-        return 0
-
-    lax.fori_loop(0, work[6, 0], step, 0)
+    room = work.shape[1] // 2
+    count = CHILD // 2
     stores = []
-    for n in range(0, CHILD, 2):
+    for half in range(2):
+        start = jnp.bitwise_xor(half, odd) * count
+        for t in range(count):
+            n = start + t
+            picked = [window[blocks(work[7 + f, n], 1, rank), :] for f in range(FAR)]
+            acc[blocks(n, 1, leaf), :] += mm(folded[n], jnp.concatenate(picked, axis=0))
+
+        def step(t, _):
+            for b in range(BATCH):
+                n = half * room + t * BATCH + b
+                for r, held, low in ((0, tiles, 0), (1, other, base)):
+                    tile = work[3 * r, n]
+                    at = pl.multiple_of(skip + work[3 * r + 1, n] * leaf, rank)
+                    part = mm(held[low + tile // slots, lax.rem(tile, slots)], bulk2[pl.ds(at, leaf), :])
+                    acc[blocks(work[3 * r + 2, n], 1, leaf), :] += part
+            return 0
+
+        lax.fori_loop(0, work[6, half], step, 0)
         stores.append(
-            pltpu.make_async_copy(acc.at[pl.ds(n * leaf, 2 * leaf)], out.at[blocks(base + n, 2, leaf)], sems.at[n // 2])
+            pltpu.make_async_copy(acc.at[blocks(start, count, leaf)], out.at[blocks(base + start, count, leaf)], sems.at[half])
         )
         stores[-1].start()
     for store in stores:
@@ -347,7 +399,7 @@
     edge = CHILD * leaf
     edge_c = CHILD * rank
     rows = leaves * leaf
-    assert leaves == 2 * CHILD and group >= 2 and total_top >= 4
+    assert leaves == 2 * CHILD and group == 4 and total_top >= 4
     product_flops = 2 * leaf * leaf * cols
 
     rest = [(i, i + 1) for i in range(1, devices - 1, 2)]
@@ -404,31 +456,64 @@
 
     work, bulk2 = call(
         prepare,
-        (sds((7, CHILD * slots + BATCH), jnp.int32), sds((edge_c + edge, cols), BF16)),
-        [SMEM, SMEM, VMEM, VMEM],
+        (sds((7 + FAR, CHILD * slots + 2 * BATCH), jnp.int32), sds((edge_c + edge, cols), BF16)),
+        [SMEM, SMEM, SMEM, VMEM, VMEM],
         (SMEM, VMEM),
         [],
         8,
         cost(0, 4 << 20),
-    )(index, count, coef, src)
+    )(index, count, far_index, coef, src)
 
     held = mids * rank
-    plane = jnp.concatenate([pack[:held], pack1[:held]], axis=0)
-    total = pack[held : held + rank].astype(F32) + pack1[held : held + rank].astype(F32)
-    total = total.astype(BF16)
-    k = 2
-    while k < group:
-        got = send(jnp.concatenate([plane, total], axis=0), swap(k))
-        held = plane.shape[0]
-        plane = jnp.concatenate([plane, got[:held]], axis=0)
-        total = (total.astype(F32) + got[held:].astype(F32)).astype(BF16)
-        k *= 2
-
-    tops = [send(total, swap(k * group)) for k in range(1, total_top)]
-    beyond = [(i, i + group) for i in range(group, devices - group) if i % (2 * group) >= group]
+    pair, part = call(
+        join,
+        (sds((2 * held + rank, cols), BF16), sds((rank, cols), BF16)),
+        [VMEM] * 2,
+        (VMEM,) * 2,
+        [],
+        4,
+        cost(0, 1 << 18),
+    )(pack, pack1)
+
+    pair1 = send(pair, swap(2))
+    parts = [send(part, swap(k * group)) for k in range(2, total_top)]
+    plane = call(
+        cluster,
+        sds((4 * held + rank, cols), BF16),
+        [VMEM] * 2,
+        VMEM,
+        [],
+        4,
+        cost(0, 1 << 18),
+    )(pair, pair1)
+    beyond = call(
+        stacked,
+        sds(((total_top - 2) * rank, cols), BF16),
+        [VMEM] * len(parts),
+        VMEM,
+        [],
+        4,
+        cost(0, 1 << 18),
+    )(*parts)
+    next_pairs = [(i, i + group) for i in range(group, devices - group) if i % (2 * group) >= group]
     next_a = send(plane, swap(group))
-    next_b = send(plane, beyond + [(j, i) for i, j in beyond])
+    next_b = send(plane, next_pairs + [(j, i) for i, j in next_pairs])
+    beyond1 = send(beyond, swap(2))
     bulk2 = send(bulk2, rest)
+
+    folded = call(
+        fold,
+        sds((CHILD, leaf, leaf_coupling.shape[2]), BF16),
+        [HBM] * 2,
+        VMEM,
+        [
+            pltpu.VMEM((CHILD,) + leaf_basis.shape[1:], BF16),
+            pltpu.VMEM((CHILD,) + leaf_coupling.shape[1:], BF16),
+            pltpu.SemaphoreType.DMA((2,)),
+        ],
+        6,
+        cost(CHILD * 2 * leaf * leaf * rank, 2 << 20),
+    )(in_hbm(leaf_basis), in_hbm(leaf_coupling))
 
     half_tiles = (CHILD,) + near_tiles.shape[1:]
     near1, near2, tiles2 = call(
@@ -446,11 +531,11 @@
         cost(leaves * 2 * slots * product_flops, 16 << 20),
     )(index, count, own_tiles, other, src, bulk1)
 
-    out, acc2, turned = call(
+    out, acc2 = call(
         downward,
-        (sds((rows, cols), F32), sds((edge + leaf, cols), F32), sds((CHILD, leaf, rank), BF16)),
-        [SMEM] * 2 + [VMEM] * (12 + total_top),
-        (ANY, VMEM, VMEM),
+        (sds((rows, cols), F32), sds((edge + leaf, cols), F32)),
+        [SMEM] * 2 + [VMEM] * 15,
+        (ANY, VMEM),
         [
             pltpu.VMEM((edge, cols), F32),
             pltpu.VMEM((leaves * rank, cols), F32),
@@ -463,20 +548,20 @@
         cost(leaves * 4 * product_flops, 12 << 20),
     )(
         far_index, mid_index,
-        near1, near2, coef, bulk1, plane, next_a, next_b,
-        leaf_basis, leaf_coupling, up_leaf, mid_coupling, up_mid, top_coupling, *tops,
+        near1, near2, coef, bulk1, plane, next_a, next_b, beyond, beyond1,
+        leaf_basis, leaf_coupling, up_leaf, mid_coupling, up_mid, top_coupling,
     )
 
     product, _ = call(
         near_last,
         (sds((rows, cols), F32), sds((edge + leaf, cols), F32)),
-        [SMEM] * 2 + [VMEM] * 6 + [ANY],
+        [SMEM] + [VMEM] * 5 + [ANY],
         (ANY, VMEM),
-        [pltpu.VMEM((edge_c + rank, cols), BF16), pltpu.SemaphoreType.DMA((CHILD // 2,))],
+        [pltpu.VMEM((edge_c + rank, cols), BF16), pltpu.SemaphoreType.DMA((2,))],
         8,
         cost(leaves * slots * product_flops, 4 << 20),
-        input_output_aliases={8: 0, 5: 1},
-    )(work, far_index, in_vmem(tiles2), other, bulk2, in_vmem(acc2), leaf_coupling, turned, out)
+        input_output_aliases={6: 0, 4: 1},
+    )(work, in_vmem(tiles2), other, bulk2, in_vmem(acc2), folded, out)
     return product
 
 

time: 55.8 us -> 67.8 us (1.22)
  the two profiles are of different devices: /device:TPU:0 before, /device:TPU:12 now
where the time goes in v3:
time: 67.8 us; the launch traced here: 67.6 us
  waiting for transfers between devices  26.2 us (39%)
  Pallas kernels  21.1 us (31%)
  starting transfers between devices  20 us (29%)
    ppermute x10, waiting for transfers between devices, send(): return lax.ppermute(x, axis, pairs)  26.2 us
    pallas_call x9, Pallas kernels, run(): pl.pallas_call(kernel, out_shape=out_shape, in_specs=in_specs, out_specs=...  21.1 us
    ppermute x10, starting transfers between devices, send(): return lax.ppermute(x, axis, pairs)  20 us
  transfers between devices with their start and end apart: 10, of which 3 were waited for; matrix products, arithmetic and copies ran while one was open for 0% of the time, Pallas kernels for 26%

profile of v3, /device:TPU:12, one launch (start us, length us, event | category | flops | bytes accessed | tf_op | source)
XLA Modules:
  0.0 67.6 jit_solution(4011012863881181377)
XLA Ops:
  0.0 0.0 collective-permute-start
  0.0 2.2 %shard_map.118 = (bf16[192,128]{1,0:T(8,128)(2,1)S(1)}, bf16[2560,128]{1,0:T(8,128)(2,1)S(1)}, bf16[1024,128]{1,0:T(8,128)(2,1)S(1)}, bf16[4352,128]{1,0:T(8,128)(2,1)S(1)}) custom-call(bf16[4096,128]{1,0:T(8,128)(2,1)} %src_hbm.1, bf16[16,64,256]{2,1,0:T(8,128)(2,1)} %basis_hbm.3, bf16[2,64,512]{2,1,0:T(8,128)(2,1)} %up_leaf.1, bf16[2,64,64]{2,1,0:T(8,128)(2,1)} %up_mid.1), custom_call_target="tpu_custom_call" | custom-call | flops 67108864 | bytes 4194304 | tf_op jit(solution)/shard_map/pallas_call | solution.py:416
  2.3 1.5 %collective-permute-start.1 = (bf16[2560,128]{1,0:T(8,128)(2,1)S(1)}, bf16[2560,128]{1,0:T(8,128)(2,1)S(1)}, u32[]{:S(2)}, u32[]{:S(2)}) collective-permute-start(bf16[2560,128]{1,0:T(8,128)(2,1)S(1)} %get-tuple-element.22), channel_id=1, source_target_pairs={{0,2},{2,0},{4,6},{6,4},{8,10},{10,8},{12,14},{14,12},{16,18},{18,... | collective-permute-start | bytes 1966088 | tf_op jit(solution)/shard_map/ppermute | solution.py:412
  3.8 2.2 %shard_map.119 = (s32[11,40]{1,0:T(8,128)S(1)}, bf16[2560,128]{1,0:T(8,128)(2,1)S(1)}) custom-call(s32[8,16]{1,0:T(8,128)} %bitcast.2, s32[16]{0:T(128)} %count.3, s32[4,16]{1,0:T(4,128)} %bitcast.4, bf16[1024,128]{1,0:T(8,128)(2,1)S(1)} %get-tuple-element.19.coef, bf16[4352,128]{1,0:T(8,128)(2,1)S(1)} %get-tuple-element.20.src), custom_call_target="tpu_custom_call" | custom-call | bytes 4194304 | tf_op jit(solution)/shard_map/pallas_call | solution.py:416
  6.0 2.4 %collective-permute-start.2 = (bf16[2560,128]{1,0:T(8,128)(2,1)S(1)}, bf16[2560,128]{1,0:T(8,128)(2,1)S(1)}, u32[]{:S(2)}, u32[]{:S(2)}) collective-permute-start(bf16[2560,128]{1,0:T(8,128)(2,1)S(1)} %get-tuple-element.24), channel_id=1, source_target_pairs={{2,4},{6,8},{10,12},{14,16},{18,20},{22,24},{26,28},{4,2},{8,6},{1... | collective-permute-start | bytes 1966088 | tf_op jit(solution)/shard_map/ppermute | solution.py:412
  8.4 2.6 %collective-permute-start.3 = (bf16[192,128]{1,0:T(8,128)(2,1)S(1)}, bf16[192,128]{1,0:T(8,128)(2,1)S(1)}, u32[]{:S(2)}, u32[]{:S(2)}) collective-permute-start(bf16[192,128]{1,0:T(8,128)(2,1)S(1)} %get-tuple-element.27.pack), channel_id=1, source_target_pairs={{0,2},{2,0},{4,6},{6,4},{8,10},{10,8},{12,14},{14,12},{16,18},{18,... | collective-permute-start | bytes 147464 | tf_op jit(solution)/shard_map/ppermute | solution.py:412
  11.1 23.5 %collective-permute-done.3.pack1 = bf16[192,128]{1,0:T(8,128)(2,1)S(1)} collective-permute-done((bf16[192,128]{1,0:T(8,128)(2,1)S(1)}, bf16[192,128]{1,0:T(8,128)(2,1)S(1)}, u32[]{:S(2)}, u32[]{:S(2)}) %collective-permute-start.3) | collective-permute-done | bytes 49184 | tf_op jit(solution)/shard_map/ppermute | solution.py:412
  34.6 0.6 collective-permute-start.4
  35.2 2.6 %collective-permute-start.7 = (bf16[64,128]{1,0:T(8,128)(2,1)S(1)}, bf16[64,128]{1,0:T(8,128)(2,1)S(1)}, u32[]{:S(2)}, u32[]{:S(2)}) collective-permute-start(bf16[64,128]{1,0:T(8,128)(2,1)S(1)} %get-tuple-element.29), channel_id=1, source_target_pairs={{0,16},{2,18},{4,20},{6,22},{8,24},{10,26},{12,28},{14,30},{16,0},... | collective-permute-start | bytes 49160 | tf_op jit(solution)/shard_map/ppermute | solution.py:412
  37.7 2.0 %collective-permute-done.7.refs_0_ = bf16[64,128]{1,0:T(8,128)(2,1)S(1)} collective-permute-done((bf16[64,128]{1,0:T(8,128)(2,1)S(1)}, bf16[64,128]{1,0:T(8,128)(2,1)S(1)}, u32[]{:S(2)}, u32[]{:S(2)}) %collective-permute-start.7) | collective-permute-done | bytes 16416 | tf_op jit(solution)/shard_map/ppermute | solution.py:412
  39.8 1.6 %collective-permute-start.8 = (bf16[64,128]{1,0:T(8,128)(2,1)S(1)}, bf16[64,128]{1,0:T(8,128)(2,1)S(1)}, u32[]{:S(2)}, u32[]{:S(2)}) collective-permute-start(bf16[64,128]{1,0:T(8,128)(2,1)S(1)} %get-tuple-element.29), channel_id=1, source_target_pairs={{0,24},{2,26},{4,28},{6,30},{8,16},{10,18},{12,20},{14,22},{16,8},... | collective-permute-start | bytes 49160 | tf_op jit(solution)/shard_map/ppermute | solution.py:412
  41.4 1.5 %shard_map.125.folded = bf16[8,256,256]{2,1,0:T(8,128)(2,1)S(1)} custom-call(bf16[16,64,256]{2,1,0:T(8,128)(2,1)} %basis_hbm.3, bf16[16,64,256]{2,1,0:T(8,128)(2,1)} %coupling_hbm.1), custom_call_target="tpu_custom_call" | custom-call | flops 67108864 | bytes 2097152 | tf_op jit(solution)/shard_map/pallas_call | solution.py:416
  42.9 0.6 collective-permute-done.8.refs_1_
  43.5 1.5 %collective-permute-start.9 = (bf16[128,128]{1,0:T(8,128)(2,1)S(1)}, bf16[128,128]{1,0:T(8,128)(2,1)S(1)}, u32[]{:S(2)}, u32[]{:S(2)}) collective-permute-start(bf16[128,128]{1,0:T(8,128)(2,1)S(1)} %shard_map.123.beyond0), channel_id=1, source_target_pairs={{0,4},{2,6},{4,0},{6,2},{8,12},{10,14},{12,8},{14,10},{16,20},{18,... | collective-permute-start | bytes 98312 | tf_op jit(solution)/shard_map/ppermute | solution.py:412
  45.1 0.0 collective-permute-done.4.pair1
  45.1 0.0 copy-start
  45.1 0.0 copy-start.1
  45.1 0.0 copy-start.2
  45.1 0.0 copy-start.3
  45.1 0.0 copy-start.4
  45.1 0.0 copy-start.5
  45.1 2.2 %collective-permute-start.5 = (bf16[576,128]{1,0:T(8,128)(2,1)S(1)}, bf16[576,128]{1,0:T(8,128)(2,1)S(1)}, u32[]{:S(2)}, u32[]{:S(2)}) collective-permute-start(bf16[576,128]{1,0:T(8,128)(2,1)S(1)} %shard_map.122.plane), channel_id=1, source_target_pairs={{0,8},{2,10},{4,12},{6,14},{8,0},{10,2},{12,4},{14,6},{16,24},{18,... | collective-permute-start | bytes 442376 | tf_op jit(solution)/shard_map/ppermute | solution.py:412
  47.3 0.0 collective-permute-done.1.bulk1
  47.3 5.0 %collective-permute-start.6 = (bf16[576,128]{1,0:T(8,128)(2,1)S(1)}, bf16[576,128]{1,0:T(8,128)(2,1)S(1)}, u32[]{:S(2)}, u32[]{:S(2)}) collective-permute-start(bf16[576,128]{1,0:T(8,128)(2,1)S(1)} %shard_map.122.plane), channel_id=1, source_target_pairs={{8,16},{10,18},{12,20},{14,22},{16,8},{18,10},{20,12},{22,14},{9,1... | collective-permute-start | bytes 442376 | tf_op jit(solution)/shard_map/ppermute | solution.py:412
  52.3 0.0 collective-permute-done.other
  52.3 8.4 %shard_map.120 = (f32[2048,128]{1,0:T(8,128)S(1)}, f32[2048,128]{1,0:T(8,128)S(1)}, bf16[8,4,256,256]{3,2,1,0:T(8,128)(2,1)S(1)}) custom-call(s32[8,16]{1,0:T(8,128)} %bitcast.3, s32[16]{0:T(128)} %count.3, bf16[16,4,256,256]{3,2,1,0:T(8,128)(2,1)} %tiles_hbm.1, bf16[16,4,256,256]{3,2,1,0:T(8,128)(2,1)S(1)} %collective-permute-done.other, ...), custom_call_target="tpu_custom_call" | custom-call | flops 2147483648 | bytes 16777216 | tf_op jit(solution)/shard_map/pallas_call | solution.py:416
  60.7 0.0 collective-permute-done.9.beyond1
  60.7 0.0 collective-permute-done.5.next_a
  60.7 0.0 collective-permute-done.6.next_b
  60.8 3.4 %shard_map.124 = (f32[4096,128]{1,0:T(8,128)}, f32[2304,128]{1,0:T(8,128)S(1)}) custom-call(s32[4,16]{1,0:T(4,128)} %bitcast.5, s32[2,4]{1,0:T(2,128)} %mid_far.1, f32[2048,128]{1,0:T(8,128)S(1)} %get-tuple-element.25.near1, f32[2048,128]{1,0:T(8,128)S(1)} %get-tuple-element.26.near2, bf16[1024,128]{1,0:T(8,128)(2,1)S(1)} %get-tuple-element.19.coef, ...), custom_call_target="tpu_custom_call" | custom-call | flops 1073741824 | bytes 12582912 | tf_op jit(solution)/shard_map/pallas_call | solution.py:416
  64.1 0.0 collective-permute-done.2.bulk2
  64.2 3.4 %shard_map.126 = (f32[4096,128]{1,0:T(8,128)}, f32[2304,128]{1,0:T(8,128)S(1)}) custom-call(s32[11,40]{1,0:T(8,128)S(1)} %get-tuple-element.21.work, bf16[8,4,256,256]{3,2,1,0:T(8,128)(2,1)S(1)} %get-tuple-element.23.tiles, bf16[16,4,256,256]{3,2,1,0:T(8,128)(2,1)S(1)} %collective-permute-done.other, ...), custom_call_target="tpu_custom_call", output_to_operand_aliasing={{0}: (6, {}), {1}: (4, {})} | custom-call | flops 1073741824 | bytes 4194304 | tf_op jit(solution)/shard_map/pallas_call | solution.py:416
  (9 shorter events, 0.0 us)
Async XLA Ops:
  0.0 52.3 %collective-permute-start = (bf16[16,4,256,256]{3,2,1,0:T(8,128)(2,1)}, bf16[16,4,256,256]{3,2,1,0:T(8,128)(2,1)S(1)}, u32[]{:S(2)}, u32[]{:S(2)}) collective-permute-start(bf16[16,4,256,256]{3,2,1,0:T(8,128)(2,1)} %tiles_hbm.1), channel_id=1, source_target_pairs={{0,1},{1,0},{2,3},{3,2},{4,5},{5,4},{6,7},{7,6},{8,9},{9,8},{10,11... | collective-permute-start | bytes 25165832 | tf_op jit(solution)/shard_map/ppermute | solution.py:412
  2.3 45.1 %collective-permute-start.1 = (bf16[2560,128]{1,0:T(8,128)(2,1)S(1)}, bf16[2560,128]{1,0:T(8,128)(2,1)S(1)}, u32[]{:S(2)}, u32[]{:S(2)}) collective-permute-start(bf16[2560,128]{1,0:T(8,128)(2,1)S(1)} %get-tuple-element.22), channel_id=1, source_target_pairs={{0,2},{2,0},{4,6},{6,4},{8,10},{10,8},{12,14},{14,12},{16,18},{18,... | collective-permute-start | bytes 1966088 | tf_op jit(solution)/shard_map/ppermute | solution.py:412
  6.0 58.1 %collective-permute-start.2 = (bf16[2560,128]{1,0:T(8,128)(2,1)S(1)}, bf16[2560,128]{1,0:T(8,128)(2,1)S(1)}, u32[]{:S(2)}, u32[]{:S(2)}) collective-permute-start(bf16[2560,128]{1,0:T(8,128)(2,1)S(1)} %get-tuple-element.24), channel_id=1, source_target_pairs={{2,4},{6,8},{10,12},{14,16},{18,20},{22,24},{26,28},{4,2},{8,6},{1... | collective-permute-start | bytes 1966088 | tf_op jit(solution)/shard_map/ppermute | solution.py:412
  8.4 26.1 %collective-permute-start.3 = (bf16[192,128]{1,0:T(8,128)(2,1)S(1)}, bf16[192,128]{1,0:T(8,128)(2,1)S(1)}, u32[]{:S(2)}, u32[]{:S(2)}) collective-permute-start(bf16[192,128]{1,0:T(8,128)(2,1)S(1)} %get-tuple-element.27.pack), channel_id=1, source_target_pairs={{0,2},{2,0},{4,6},{6,4},{8,10},{10,8},{12,14},{14,12},{16,18},{18,... | collective-permute-start | bytes 147464 | tf_op jit(solution)/shard_map/ppermute | solution.py:412
  34.6 10.5 %collective-permute-start.4 = (bf16[320,128]{1,0:T(8,128)(2,1)S(1)}, bf16[320,128]{1,0:T(8,128)(2,1)S(1)}, u32[]{:S(2)}, u32[]{:S(2)}) collective-permute-start(bf16[320,128]{1,0:T(8,128)(2,1)S(1)} %get-tuple-element.28.pair), channel_id=1, source_target_pairs={{0,4},{2,6},{4,0},{6,2},{8,12},{10,14},{12,8},{14,10},{16,20},{18,... | collective-permute-start | bytes 245768 | tf_op jit(solution)/shard_map/ppermute | solution.py:412
  35.2 4.6 %collective-permute-start.7 = (bf16[64,128]{1,0:T(8,128)(2,1)S(1)}, bf16[64,128]{1,0:T(8,128)(2,1)S(1)}, u32[]{:S(2)}, u32[]{:S(2)}) collective-permute-start(bf16[64,128]{1,0:T(8,128)(2,1)S(1)} %get-tuple-element.29), channel_id=1, source_target_pairs={{0,16},{2,18},{4,20},{6,22},{8,24},{10,26},{12,28},{14,30},{16,0},... | collective-permute-start | bytes 49160 | tf_op jit(solution)/shard_map/ppermute | solution.py:412
  39.8 3.7 %collective-permute-start.8 = (bf16[64,128]{1,0:T(8,128)(2,1)S(1)}, bf16[64,128]{1,0:T(8,128)(2,1)S(1)}, u32[]{:S(2)}, u32[]{:S(2)}) collective-permute-start(bf16[64,128]{1,0:T(8,128)(2,1)S(1)} %get-tuple-element.29), channel_id=1, source_target_pairs={{0,24},{2,26},{4,28},{6,30},{8,16},{10,18},{12,20},{14,22},{16,8},... | collective-permute-start | bytes 49160 | tf_op jit(solution)/shard_map/ppermute | solution.py:412
  43.5 17.2 %collective-permute-start.9 = (bf16[128,128]{1,0:T(8,128)(2,1)S(1)}, bf16[128,128]{1,0:T(8,128)(2,1)S(1)}, u32[]{:S(2)}, u32[]{:S(2)}) collective-permute-start(bf16[128,128]{1,0:T(8,128)(2,1)S(1)} %shard_map.123.beyond0), channel_id=1, source_target_pairs={{0,4},{2,6},{4,0},{6,2},{8,12},{10,14},{12,8},{14,10},{16,20},{18,... | collective-permute-start | bytes 98312 | tf_op jit(solution)/shard_map/ppermute | solution.py:412
  45.1 15.6 %copy-start = (bf16[16,64,256]{2,1,0:T(8,128)(2,1)S(1)}, bf16[16,64,256]{2,1,0:T(8,128)(2,1)}, u32[]{:S(2)}) copy-start(bf16[16,64,256]{2,1,0:T(8,128)(2,1)} %basis_hbm.3) | copy-start | bytes 1572868
  45.1 15.6 %copy-start.1 = (bf16[16,64,256]{2,1,0:T(8,128)(2,1)S(1)}, bf16[16,64,256]{2,1,0:T(8,128)(2,1)}, u32[]{:S(2)}) copy-start(bf16[16,64,256]{2,1,0:T(8,128)(2,1)} %coupling_hbm.1) | copy-start | bytes 1572868
  45.1 15.6 %copy-start.2 = (bf16[2,64,512]{2,1,0:T(8,128)(2,1)S(1)}, bf16[2,64,512]{2,1,0:T(8,128)(2,1)}, u32[]{:S(2)}) copy-start(bf16[2,64,512]{2,1,0:T(8,128)(2,1)} %up_leaf.1) | copy-start | bytes 393220
  45.1 15.6 %copy-start.3 = (bf16[2,64,64]{2,1,0:T(8,128)(2,1)S(1)}, bf16[2,64,64]{2,1,0:T(8,128)(2,1)}, u32[]{:S(2)}) copy-start(bf16[2,64,64]{2,1,0:T(8,128)(2,1)} %up_mid.1) | copy-start | bytes 49156
  45.1 15.6 %copy-start.4 = (bf16[4,64,256]{2,1,0:T(8,128)(2,1)S(1)}, bf16[4,64,256]{2,1,0:T(8,128)(2,1)}, u32[]{:S(2)}) copy-start(bf16[4,64,256]{2,1,0:T(8,128)(2,1)} %top_coupling.1) | copy-start | bytes 393220
  45.1 15.6 %copy-start.5 = (bf16[2,64,256]{2,1,0:T(8,128)(2,1)S(1)}, bf16[2,64,256]{2,1,0:T(8,128)(2,1)}, u32[]{:S(2)}) copy-start(bf16[2,64,256]{2,1,0:T(8,128)(2,1)} %mid_coupling.1) | copy-start | bytes 196612
  45.1 15.6 %collective-permute-start.5 = (bf16[576,128]{1,0:T(8,128)(2,1)S(1)}, bf16[576,128]{1,0:T(8,128)(2,1)S(1)}, u32[]{:S(2)}, u32[]{:S(2)}) collective-permute-start(bf16[576,128]{1,0:T(8,128)(2,1)S(1)} %shard_map.122.plane), channel_id=1, source_target_pairs={{0,8},{2,10},{4,12},{6,14},{8,0},{10,2},{12,4},{14,6},{16,24},{18,... | collective-permute-start | bytes 442376 | tf_op jit(solution)/shard_map/ppermute | solution.py:412
  47.3 13.4 %collective-permute-start.6 = (bf16[576,128]{1,0:T(8,128)(2,1)S(1)}, bf16[576,128]{1,0:T(8,128)(2,1)S(1)}, u32[]{:S(2)}, u32[]{:S(2)}) collective-permute-start(bf16[576,128]{1,0:T(8,128)(2,1)S(1)} %shard_map.122.plane), channel_id=1, source_target_pairs={{8,16},{10,18},{12,20},{14,22},{16,8},{18,10},{20,12},{22,14},{9,1... | collective-permute-start | bytes 442376 | tf_op jit(solution)/shard_map/ppermute | solution.py:412

commit v4 on v3

--- a/solution.py
+++ b/solution.py
@@ -1,3 +1,5 @@
+import functools
+
 import jax
 import jax.numpy as jnp
 from jax import lax
@@ -9,7 +11,7 @@
 CHILD = 8
 FAR = 4
 BATCH = 4
-PARTS = 4
+PARTS = 2
 
 F32 = jnp.float32
 BF16 = jnp.bfloat16
@@ -138,19 +140,24 @@
             lax.fori_loop(found[r], begin + rounds * BATCH, fill, 0)
 
 
-def fold(basis_hbm, coupling_hbm, folded, basis, coupling, sems):
-    leaves = basis_hbm.shape[0]
-    base = lax.rem(lax.axis_index("leaf"), 2) * (leaves - CHILD)
-    loads = [
-        pltpu.make_async_copy(a.at[pl.ds(base, CHILD)], b, sems.at[k])
-        for k, (a, b) in enumerate(((basis_hbm, basis), (coupling_hbm, coupling)))
-    ]
-    for load in loads:
-        load.start()
-    for load in loads:
-        load.wait()
-    for n in range(CHILD):
-        folded[n] = mm_t(basis[n], coupling[n]).astype(BF16)
+def fold(late, last, basis_hbm, coupling_hbm, *refs):
+    folded, basis, coupling, sems = refs[-4:]
+    leaves, _, _ = basis_hbm.shape
+    device = lax.axis_index("leaf")
+    base = lax.rem(device, 2) * (leaves - CHILD)
+
+    @pl.when((device >= last) == late)
+    def _():
+        loads = [
+            pltpu.make_async_copy(a.at[pl.ds(base, CHILD)], b, sems.at[k])
+            for k, (a, b) in enumerate(((basis_hbm, basis), (coupling_hbm, coupling)))
+        ]
+        for load in loads:
+            load.start()
+        for load in loads:
+            load.wait()
+        for n in range(CHILD):
+            folded[n] = mm_t(basis[n], coupling[n]).astype(BF16)
 
 
 def join(pack, pack1, pair, part):
@@ -501,19 +508,23 @@
     beyond1 = send(beyond, swap(2))
     bulk2 = send(bulk2, rest)
 
-    folded = call(
-        fold,
-        sds((CHILD, leaf, leaf_coupling.shape[2]), BF16),
-        [HBM] * 2,
-        VMEM,
-        [
-            pltpu.VMEM((CHILD,) + leaf_basis.shape[1:], BF16),
-            pltpu.VMEM((CHILD,) + leaf_coupling.shape[1:], BF16),
-            pltpu.SemaphoreType.DMA((2,)),
-        ],
-        6,
-        cost(CHILD * 2 * leaf * leaf * rank, 2 << 20),
-    )(in_hbm(leaf_basis), in_hbm(leaf_coupling))
+    folded = None
+    for late in (False, True):
+        held = [] if folded is None else [in_vmem(folded)]
+        folded = call(
+            functools.partial(fold, late, devices - group),
+            sds((CHILD, leaf, leaf_coupling.shape[2]), BF16),
+            [HBM] * 2 + [VMEM] * len(held),
+            VMEM,
+            [
+                pltpu.VMEM((CHILD,) + leaf_basis.shape[1:], BF16),
+                pltpu.VMEM((CHILD,) + leaf_coupling.shape[1:], BF16),
+                pltpu.SemaphoreType.DMA((2,)),
+            ],
+            6,
+            cost(CHILD * 2 * leaf * leaf * rank, 2 << 20),
+            **({"input_output_aliases": {2: 0}} if held else {}),
+        )(in_hbm(leaf_basis), in_hbm(leaf_coupling), *held)
 
     half_tiles = (CHILD,) + near_tiles.shape[1:]
     near1, near2, tiles2 = call(

time: 67.8 us -> 67.8 us (level)
    pallas_call x9 -> x10, Pallas kernels: 21.1 us -> 21.1 us  [run(): pl.pallas_call(kernel, out_shape=out_shape, in_specs=in_specs, out_specs=...]
where the time goes in v4:
time: 67.8 us; the launch traced here: 67.5 us
  waiting for transfers between devices  26.2 us (39%)
  Pallas kernels  21.1 us (31%)
  starting transfers between devices  20 us (29%)
    ppermute x10, waiting for transfers between devices, send(): return lax.ppermute(x, axis, pairs)  26.2 us
    pallas_call x10, Pallas kernels, run(): pl.pallas_call(kernel, out_shape=out_shape, in_specs=in_specs, out_specs=...  21.1 us
    ppermute x10, starting transfers between devices, send(): return lax.ppermute(x, axis, pairs)  20 us
  transfers between devices with their start and end apart: 10, of which 3 were waited for; matrix products, arithmetic and copies ran while one was open for 0% of the time, Pallas kernels for 26%

profile of v4, /device:TPU:12, one launch (start us, length us, event | category | flops | bytes accessed | tf_op | source)
XLA Modules:
  0.0 67.5 jit_solution(11281714205158573049)
XLA Ops:
  0.0 0.0 collective-permute-start
  0.0 2.1 %shard_map.118 = (bf16[192,128]{1,0:T(8,128)(2,1)S(1)}, bf16[2560,128]{1,0:T(8,128)(2,1)S(1)}, bf16[1024,128]{1,0:T(8,128)(2,1)S(1)}, bf16[4352,128]{1,0:T(8,128)(2,1)S(1)}) custom-call(bf16[4096,128]{1,0:T(8,128)(2,1)} %src_hbm.1, bf16[16,64,256]{2,1,0:T(8,128)(2,1)} %basis_hbm.5, bf16[2,64,512]{2,1,0:T(8,128)(2,1)} %up_leaf.1, bf16[2,64,64]{2,1,0:T(8,128)(2,1)} %up_mid.1), custom_call_target="tpu_custom_call" | custom-call | flops 67108864 | bytes 4194304 | tf_op jit(solution)/shard_map/pallas_call | solution.py:423
  2.1 1.5 %collective-permute-start.1 = (bf16[2560,128]{1,0:T(8,128)(2,1)S(1)}, bf16[2560,128]{1,0:T(8,128)(2,1)S(1)}, u32[]{:S(2)}, u32[]{:S(2)}) collective-permute-start(bf16[2560,128]{1,0:T(8,128)(2,1)S(1)} %get-tuple-element.22), channel_id=1, source_target_pairs={{0,2},{2,0},{4,6},{6,4},{8,10},{10,8},{12,14},{14,12},{16,18},{18,... | collective-permute-start | bytes 1966088 | tf_op jit(solution)/shard_map/ppermute | solution.py:419
  3.7 2.2 %shard_map.119 = (s32[11,40]{1,0:T(8,128)S(1)}, bf16[2560,128]{1,0:T(8,128)(2,1)S(1)}) custom-call(s32[8,16]{1,0:T(8,128)} %bitcast.2, s32[16]{0:T(128)} %count.3, s32[4,16]{1,0:T(4,128)} %bitcast.4, bf16[1024,128]{1,0:T(8,128)(2,1)S(1)} %get-tuple-element.19.coef, bf16[4352,128]{1,0:T(8,128)(2,1)S(1)} %get-tuple-element.20.src), custom_call_target="tpu_custom_call" | custom-call | bytes 4194304 | tf_op jit(solution)/shard_map/pallas_call | solution.py:423
  5.9 2.4 %collective-permute-start.2 = (bf16[2560,128]{1,0:T(8,128)(2,1)S(1)}, bf16[2560,128]{1,0:T(8,128)(2,1)S(1)}, u32[]{:S(2)}, u32[]{:S(2)}) collective-permute-start(bf16[2560,128]{1,0:T(8,128)(2,1)S(1)} %get-tuple-element.24), channel_id=1, source_target_pairs={{2,4},{6,8},{10,12},{14,16},{18,20},{22,24},{26,28},{4,2},{8,6},{1... | collective-permute-start | bytes 1966088 | tf_op jit(solution)/shard_map/ppermute | solution.py:419
  8.3 2.6 %collective-permute-start.3 = (bf16[192,128]{1,0:T(8,128)(2,1)S(1)}, bf16[192,128]{1,0:T(8,128)(2,1)S(1)}, u32[]{:S(2)}, u32[]{:S(2)}) collective-permute-start(bf16[192,128]{1,0:T(8,128)(2,1)S(1)} %get-tuple-element.27.pack), channel_id=1, source_target_pairs={{0,2},{2,0},{4,6},{6,4},{8,10},{10,8},{12,14},{14,12},{16,18},{18,... | collective-permute-start | bytes 147464 | tf_op jit(solution)/shard_map/ppermute | solution.py:419
  10.9 23.5 %collective-permute-done.3.pack1 = bf16[192,128]{1,0:T(8,128)(2,1)S(1)} collective-permute-done((bf16[192,128]{1,0:T(8,128)(2,1)S(1)}, bf16[192,128]{1,0:T(8,128)(2,1)S(1)}, u32[]{:S(2)}, u32[]{:S(2)}) %collective-permute-start.3) | collective-permute-done | bytes 49184 | tf_op jit(solution)/shard_map/ppermute | solution.py:419
  34.4 0.6 collective-permute-start.4
  35.0 2.6 %collective-permute-start.7 = (bf16[64,128]{1,0:T(8,128)(2,1)S(1)}, bf16[64,128]{1,0:T(8,128)(2,1)S(1)}, u32[]{:S(2)}, u32[]{:S(2)}) collective-permute-start(bf16[64,128]{1,0:T(8,128)(2,1)S(1)} %get-tuple-element.29), channel_id=1, source_target_pairs={{0,16},{2,18},{4,20},{6,22},{8,24},{10,26},{12,28},{14,30},{16,0},... | collective-permute-start | bytes 49160 | tf_op jit(solution)/shard_map/ppermute | solution.py:419
  37.6 2.1 %collective-permute-done.7.refs_0_ = bf16[64,128]{1,0:T(8,128)(2,1)S(1)} collective-permute-done((bf16[64,128]{1,0:T(8,128)(2,1)S(1)}, bf16[64,128]{1,0:T(8,128)(2,1)S(1)}, u32[]{:S(2)}, u32[]{:S(2)}) %collective-permute-start.7) | collective-permute-done | bytes 16416 | tf_op jit(solution)/shard_map/ppermute | solution.py:419
  39.7 1.6 %collective-permute-start.8 = (bf16[64,128]{1,0:T(8,128)(2,1)S(1)}, bf16[64,128]{1,0:T(8,128)(2,1)S(1)}, u32[]{:S(2)}, u32[]{:S(2)}) collective-permute-start(bf16[64,128]{1,0:T(8,128)(2,1)S(1)} %get-tuple-element.29), channel_id=1, source_target_pairs={{0,24},{2,26},{4,28},{6,30},{8,16},{10,18},{12,20},{14,22},{16,8},... | collective-permute-start | bytes 49160 | tf_op jit(solution)/shard_map/ppermute | solution.py:419
  41.2 1.5 %shard_map.125.refs_0_ = bf16[8,256,256]{2,1,0:T(8,128)(2,1)S(1)} custom-call(bf16[16,64,256]{2,1,0:T(8,128)(2,1)} %basis_hbm.5, bf16[16,64,256]{2,1,0:T(8,128)(2,1)} %coupling_hbm.3), custom_call_target="tpu_custom_call" | custom-call | flops 67108864 | bytes 2097152 | tf_op jit(solution)/shard_map/pallas_call | solution.py:423
  42.8 0.6 collective-permute-done.8.refs_1_
  43.4 1.5 %collective-permute-start.9 = (bf16[128,128]{1,0:T(8,128)(2,1)S(1)}, bf16[128,128]{1,0:T(8,128)(2,1)S(1)}, u32[]{:S(2)}, u32[]{:S(2)}) collective-permute-start(bf16[128,128]{1,0:T(8,128)(2,1)S(1)} %shard_map.123.beyond0), channel_id=1, source_target_pairs={{0,4},{2,6},{4,0},{6,2},{8,12},{10,14},{12,8},{14,10},{16,20},{18,... | collective-permute-start | bytes 98312 | tf_op jit(solution)/shard_map/ppermute | solution.py:419
  44.9 0.0 collective-permute-done.4.pair1
  44.9 0.0 copy-start
  44.9 0.0 copy-start.1
  45.0 0.0 copy-start.2
  45.0 0.0 copy-start.3
  45.0 0.0 copy-start.4
  45.0 0.0 copy-start.5
  45.0 2.2 %collective-permute-start.5 = (bf16[576,128]{1,0:T(8,128)(2,1)S(1)}, bf16[576,128]{1,0:T(8,128)(2,1)S(1)}, u32[]{:S(2)}, u32[]{:S(2)}) collective-permute-start(bf16[576,128]{1,0:T(8,128)(2,1)S(1)} %shard_map.122.plane), channel_id=1, source_target_pairs={{0,8},{2,10},{4,12},{6,14},{8,0},{10,2},{12,4},{14,6},{16,24},{18,... | collective-permute-start | bytes 442376 | tf_op jit(solution)/shard_map/ppermute | solution.py:419
  47.2 0.0 collective-permute-done.1.bulk1
  47.2 5.0 %collective-permute-start.6 = (bf16[576,128]{1,0:T(8,128)(2,1)S(1)}, bf16[576,128]{1,0:T(8,128)(2,1)S(1)}, u32[]{:S(2)}, u32[]{:S(2)}) collective-permute-start(bf16[576,128]{1,0:T(8,128)(2,1)S(1)} %shard_map.122.plane), channel_id=1, source_target_pairs={{8,16},{10,18},{12,20},{14,22},{16,8},{18,10},{20,12},{22,14},{9,1... | collective-permute-start | bytes 442376 | tf_op jit(solution)/shard_map/ppermute | solution.py:419
  52.2 0.0 collective-permute-done.other
  52.2 8.4 %shard_map.120 = (f32[2048,128]{1,0:T(8,128)S(1)}, f32[2048,128]{1,0:T(8,128)S(1)}, bf16[8,4,256,256]{3,2,1,0:T(8,128)(2,1)S(1)}) custom-call(s32[8,16]{1,0:T(8,128)} %bitcast.3, s32[16]{0:T(128)} %count.3, bf16[16,4,256,256]{3,2,1,0:T(8,128)(2,1)} %tiles_hbm.1, bf16[16,4,256,256]{3,2,1,0:T(8,128)(2,1)S(1)} %collective-permute-done.other, ...), custom_call_target="tpu_custom_call" | custom-call | flops 2147483648 | bytes 16777216 | tf_op jit(solution)/shard_map/pallas_call | solution.py:423
  60.6 0.0 collective-permute-done.9.beyond1
  60.6 0.0 collective-permute-done.5.next_a
  60.6 0.0 collective-permute-done.6.next_b
  60.7 3.4 %shard_map.124 = (f32[4096,128]{1,0:T(8,128)}, f32[2304,128]{1,0:T(8,128)S(1)}) custom-call(s32[4,16]{1,0:T(4,128)} %bitcast.5, s32[2,4]{1,0:T(2,128)} %mid_far.1, f32[2048,128]{1,0:T(8,128)S(1)} %get-tuple-element.25.near1, f32[2048,128]{1,0:T(8,128)S(1)} %get-tuple-element.26.near2, bf16[1024,128]{1,0:T(8,128)(2,1)S(1)} %get-tuple-element.19.coef, ...), custom_call_target="tpu_custom_call" | custom-call | flops 1073741824 | bytes 12582912 | tf_op jit(solution)/shard_map/pallas_call | solution.py:423
  64.1 0.0 collective-permute-done.2.bulk2
  64.1 3.4 %shard_map.127 = (f32[4096,128]{1,0:T(8,128)}, f32[2304,128]{1,0:T(8,128)S(1)}) custom-call(s32[11,40]{1,0:T(8,128)S(1)} %get-tuple-element.21.work, bf16[8,4,256,256]{3,2,1,0:T(8,128)(2,1)S(1)} %get-tuple-element.23.tiles, bf16[16,4,256,256]{3,2,1,0:T(8,128)(2,1)S(1)} %collective-permute-done.other, ...), custom_call_target="tpu_custom_call", output_to_operand_aliasing={{0}: (6, {}), {1}: (4, {})} | custom-call | flops 1073741824 | bytes 4194304 | tf_op jit(solution)/shard_map/pallas_call | solution.py:423
  (10 shorter events, 0.1 us)
Async XLA Ops:
  0.0 52.2 %collective-permute-start = (bf16[16,4,256,256]{3,2,1,0:T(8,128)(2,1)}, bf16[16,4,256,256]{3,2,1,0:T(8,128)(2,1)S(1)}, u32[]{:S(2)}, u32[]{:S(2)}) collective-permute-start(bf16[16,4,256,256]{3,2,1,0:T(8,128)(2,1)} %tiles_hbm.1), channel_id=1, source_target_pairs={{0,1},{1,0},{2,3},{3,2},{4,5},{5,4},{6,7},{7,6},{8,9},{9,8},{10,11... | collective-permute-start | bytes 25165832 | tf_op jit(solution)/shard_map/ppermute | solution.py:419
  2.1 45.1 %collective-permute-start.1 = (bf16[2560,128]{1,0:T(8,128)(2,1)S(1)}, bf16[2560,128]{1,0:T(8,128)(2,1)S(1)}, u32[]{:S(2)}, u32[]{:S(2)}) collective-permute-start(bf16[2560,128]{1,0:T(8,128)(2,1)S(1)} %get-tuple-element.22), channel_id=1, source_target_pairs={{0,2},{2,0},{4,6},{6,4},{8,10},{10,8},{12,14},{14,12},{16,18},{18,... | collective-permute-start | bytes 1966088 | tf_op jit(solution)/shard_map/ppermute | solution.py:419
  5.9 58.2 %collective-permute-start.2 = (bf16[2560,128]{1,0:T(8,128)(2,1)S(1)}, bf16[2560,128]{1,0:T(8,128)(2,1)S(1)}, u32[]{:S(2)}, u32[]{:S(2)}) collective-permute-start(bf16[2560,128]{1,0:T(8,128)(2,1)S(1)} %get-tuple-element.24), channel_id=1, source_target_pairs={{2,4},{6,8},{10,12},{14,16},{18,20},{22,24},{26,28},{4,2},{8,6},{1... | collective-permute-start | bytes 1966088 | tf_op jit(solution)/shard_map/ppermute | solution.py:419
  8.3 26.1 %collective-permute-start.3 = (bf16[192,128]{1,0:T(8,128)(2,1)S(1)}, bf16[192,128]{1,0:T(8,128)(2,1)S(1)}, u32[]{:S(2)}, u32[]{:S(2)}) collective-permute-start(bf16[192,128]{1,0:T(8,128)(2,1)S(1)} %get-tuple-element.27.pack), channel_id=1, source_target_pairs={{0,2},{2,0},{4,6},{6,4},{8,10},{10,8},{12,14},{14,12},{16,18},{18,... | collective-permute-start | bytes 147464 | tf_op jit(solution)/shard_map/ppermute | solution.py:419
  34.4 10.5 %collective-permute-start.4 = (bf16[320,128]{1,0:T(8,128)(2,1)S(1)}, bf16[320,128]{1,0:T(8,128)(2,1)S(1)}, u32[]{:S(2)}, u32[]{:S(2)}) collective-permute-start(bf16[320,128]{1,0:T(8,128)(2,1)S(1)} %get-tuple-element.28.pair), channel_id=1, source_target_pairs={{0,4},{2,6},{4,0},{6,2},{8,12},{10,14},{12,8},{14,10},{16,20},{18,... | collective-permute-start | bytes 245768 | tf_op jit(solution)/shard_map/ppermute | solution.py:419
  35.0 4.6 %collective-permute-start.7 = (bf16[64,128]{1,0:T(8,128)(2,1)S(1)}, bf16[64,128]{1,0:T(8,128)(2,1)S(1)}, u32[]{:S(2)}, u32[]{:S(2)}) collective-permute-start(bf16[64,128]{1,0:T(8,128)(2,1)S(1)} %get-tuple-element.29), channel_id=1, source_target_pairs={{0,16},{2,18},{4,20},{6,22},{8,24},{10,26},{12,28},{14,30},{16,0},... | collective-permute-start | bytes 49160 | tf_op jit(solution)/shard_map/ppermute | solution.py:419
  39.7 3.7 %collective-permute-start.8 = (bf16[64,128]{1,0:T(8,128)(2,1)S(1)}, bf16[64,128]{1,0:T(8,128)(2,1)S(1)}, u32[]{:S(2)}, u32[]{:S(2)}) collective-permute-start(bf16[64,128]{1,0:T(8,128)(2,1)S(1)} %get-tuple-element.29), channel_id=1, source_target_pairs={{0,24},{2,26},{4,28},{6,30},{8,16},{10,18},{12,20},{14,22},{16,8},... | collective-permute-start | bytes 49160 | tf_op jit(solution)/shard_map/ppermute | solution.py:419
  43.4 17.2 %collective-permute-start.9 = (bf16[128,128]{1,0:T(8,128)(2,1)S(1)}, bf16[128,128]{1,0:T(8,128)(2,1)S(1)}, u32[]{:S(2)}, u32[]{:S(2)}) collective-permute-start(bf16[128,128]{1,0:T(8,128)(2,1)S(1)} %shard_map.123.beyond0), channel_id=1, source_target_pairs={{0,4},{2,6},{4,0},{6,2},{8,12},{10,14},{12,8},{14,10},{16,20},{18,... | collective-permute-start | bytes 98312 | tf_op jit(solution)/shard_map/ppermute | solution.py:419
  44.9 15.7 %copy-start = (bf16[16,64,256]{2,1,0:T(8,128)(2,1)S(1)}, bf16[16,64,256]{2,1,0:T(8,128)(2,1)}, u32[]{:S(2)}) copy-start(bf16[16,64,256]{2,1,0:T(8,128)(2,1)} %basis_hbm.5) | copy-start | bytes 1572868
  44.9 15.7 %copy-start.1 = (bf16[16,64,256]{2,1,0:T(8,128)(2,1)S(1)}, bf16[16,64,256]{2,1,0:T(8,128)(2,1)}, u32[]{:S(2)}) copy-start(bf16[16,64,256]{2,1,0:T(8,128)(2,1)} %coupling_hbm.3) | copy-start | bytes 1572868
  45.0 15.7 %copy-start.2 = (bf16[2,64,512]{2,1,0:T(8,128)(2,1)S(1)}, bf16[2,64,512]{2,1,0:T(8,128)(2,1)}, u32[]{:S(2)}) copy-start(bf16[2,64,512]{2,1,0:T(8,128)(2,1)} %up_leaf.1) | copy-start | bytes 393220
  45.0 15.7 %copy-start.3 = (bf16[2,64,64]{2,1,0:T(8,128)(2,1)S(1)}, bf16[2,64,64]{2,1,0:T(8,128)(2,1)}, u32[]{:S(2)}) copy-start(bf16[2,64,64]{2,1,0:T(8,128)(2,1)} %up_mid.1) | copy-start | bytes 49156
  45.0 15.7 %copy-start.4 = (bf16[4,64,256]{2,1,0:T(8,128)(2,1)S(1)}, bf16[4,64,256]{2,1,0:T(8,128)(2,1)}, u32[]{:S(2)}) copy-start(bf16[4,64,256]{2,1,0:T(8,128)(2,1)} %top_coupling.1) | copy-start | bytes 393220
  45.0 15.7 %copy-start.5 = (bf16[2,64,256]{2,1,0:T(8,128)(2,1)S(1)}, bf16[2,64,256]{2,1,0:T(8,128)(2,1)}, u32[]{:S(2)}) copy-start(bf16[2,64,256]{2,1,0:T(8,128)(2,1)} %mid_coupling.1) | copy-start | bytes 196612
  45.0 15.6 %collective-permute-start.5 = (bf16[576,128]{1,0:T(8,128)(2,1)S(1)}, bf16[576,128]{1,0:T(8,128)(2,1)S(1)}, u32[]{:S(2)}, u32[]{:S(2)}) collective-permute-start(bf16[576,128]{1,0:T(8,128)(2,1)S(1)} %shard_map.122.plane), channel_id=1, source_target_pairs={{0,8},{2,10},{4,12},{6,14},{8,0},{10,2},{12,4},{14,6},{16,24},{18,... | collective-permute-start | bytes 442376 | tf_op jit(solution)/shard_map/ppermute | solution.py:419
  47.2 13.4 %collective-permute-start.6 = (bf16[576,128]{1,0:T(8,128)(2,1)S(1)}, bf16[576,128]{1,0:T(8,128)(2,1)S(1)}, u32[]{:S(2)}, u32[]{:S(2)}) collective-permute-start(bf16[576,128]{1,0:T(8,128)(2,1)S(1)} %shard_map.122.plane), channel_id=1, source_target_pairs={{8,16},{10,18},{12,20},{14,22},{16,8},{18,10},{20,12},{22,14},{9,1... | collective-permute-start | bytes 442376 | tf_op jit(solution)/shard_map/ppermute | solution.py:419

commit v5 on v4

--- a/solution.py
+++ b/solution.py
@@ -140,13 +140,17 @@
             lax.fori_loop(found[r], begin + rounds * BATCH, fill, 0)
 
 
-def fold(late, last, basis_hbm, coupling_hbm, *refs):
+def fold(group, after, basis_hbm, coupling_hbm, *refs):
     folded, basis, coupling, sems = refs[-4:]
     leaves, _, _ = basis_hbm.shape
     device = lax.axis_index("leaf")
     base = lax.rem(device, 2) * (leaves - CHILD)
-
-    @pl.when((device >= last) == late)
+    parent = device // group
+    member = lax.rem(device, group)
+    inner = (member > 0) & (member < group - 1)
+    early = (parent >= 2) | ((parent == 1) & inner)
+
+    @pl.when(early != after)
     def _():
         loads = [
             pltpu.make_async_copy(a.at[pl.ds(base, CHILD)], b, sems.at[k])
@@ -509,10 +513,10 @@
     bulk2 = send(bulk2, rest)
 
     folded = None
-    for late in (False, True):
+    for after in (False, True):
         held = [] if folded is None else [in_vmem(folded)]
         folded = call(
-            functools.partial(fold, late, devices - group),
+            functools.partial(fold, group, after),
             sds((CHILD, leaf, leaf_coupling.shape[2]), BF16),
             [HBM] * 2 + [VMEM] * len(held),
             VMEM,

time: 67.8 us -> 67.8 us (level)
  no operation moved by 1% of the time
where the time goes in v5:
time: 67.8 us; the launch traced here: 67.5 us
  waiting for transfers between devices  26.2 us (39%)
  Pallas kernels  21.1 us (31%)
  starting transfers between devices  20 us (29%)
    ppermute x10, waiting for transfers between devices, send(): return lax.ppermute(x, axis, pairs)  26.2 us
    pallas_call x10, Pallas kernels, run(): pl.pallas_call(kernel, out_shape=out_shape, in_specs=in_specs, out_specs=...  21.1 us
    ppermute x10, starting transfers between devices, send(): return lax.ppermute(x, axis, pairs)  20 us
  transfers between devices with their start and end apart: 10, of which 3 were waited for; matrix products, arithmetic and copies ran while one was open for 0% of the time, Pallas kernels for 26%

profile of v5, /device:TPU:12, one launch (start us, length us, event | category | flops | bytes accessed | tf_op | source)
XLA Modules:
  0.0 67.5 jit_solution(6438828714482974337)
XLA Ops:
  0.0 0.0 collective-permute-start
  0.0 2.1 %shard_map.118 = (bf16[192,128]{1,0:T(8,128)(2,1)S(1)}, bf16[2560,128]{1,0:T(8,128)(2,1)S(1)}, bf16[1024,128]{1,0:T(8,128)(2,1)S(1)}, bf16[4352,128]{1,0:T(8,128)(2,1)S(1)}) custom-call(bf16[4096,128]{1,0:T(8,128)(2,1)} %src_hbm.1, bf16[16,64,256]{2,1,0:T(8,128)(2,1)} %basis_hbm.5, bf16[2,64,512]{2,1,0:T(8,128)(2,1)} %up_leaf.1, bf16[2,64,64]{2,1,0:T(8,128)(2,1)} %up_mid.1), custom_call_target="tpu_custom_call" | custom-call | flops 67108864 | bytes 4194304 | tf_op jit(solution)/shard_map/pallas_call | solution.py:427
  2.1 1.5 %collective-permute-start.1 = (bf16[2560,128]{1,0:T(8,128)(2,1)S(1)}, bf16[2560,128]{1,0:T(8,128)(2,1)S(1)}, u32[]{:S(2)}, u32[]{:S(2)}) collective-permute-start(bf16[2560,128]{1,0:T(8,128)(2,1)S(1)} %get-tuple-element.22), channel_id=1, source_target_pairs={{0,2},{2,0},{4,6},{6,4},{8,10},{10,8},{12,14},{14,12},{16,18},{18,... | collective-permute-start | bytes 1966088 | tf_op jit(solution)/shard_map/ppermute | solution.py:423
  3.7 2.2 %shard_map.119 = (s32[11,40]{1,0:T(8,128)S(1)}, bf16[2560,128]{1,0:T(8,128)(2,1)S(1)}) custom-call(s32[8,16]{1,0:T(8,128)} %bitcast.2, s32[16]{0:T(128)} %count.3, s32[4,16]{1,0:T(4,128)} %bitcast.4, bf16[1024,128]{1,0:T(8,128)(2,1)S(1)} %get-tuple-element.19.coef, bf16[4352,128]{1,0:T(8,128)(2,1)S(1)} %get-tuple-element.20.src), custom_call_target="tpu_custom_call" | custom-call | bytes 4194304 | tf_op jit(solution)/shard_map/pallas_call | solution.py:427
  5.9 2.4 %collective-permute-start.2 = (bf16[2560,128]{1,0:T(8,128)(2,1)S(1)}, bf16[2560,128]{1,0:T(8,128)(2,1)S(1)}, u32[]{:S(2)}, u32[]{:S(2)}) collective-permute-start(bf16[2560,128]{1,0:T(8,128)(2,1)S(1)} %get-tuple-element.24), channel_id=1, source_target_pairs={{2,4},{6,8},{10,12},{14,16},{18,20},{22,24},{26,28},{4,2},{8,6},{1... | collective-permute-start | bytes 1966088 | tf_op jit(solution)/shard_map/ppermute | solution.py:423
  8.3 2.6 %collective-permute-start.3 = (bf16[192,128]{1,0:T(8,128)(2,1)S(1)}, bf16[192,128]{1,0:T(8,128)(2,1)S(1)}, u32[]{:S(2)}, u32[]{:S(2)}) collective-permute-start(bf16[192,128]{1,0:T(8,128)(2,1)S(1)} %get-tuple-element.27.pack), channel_id=1, source_target_pairs={{0,2},{2,0},{4,6},{6,4},{8,10},{10,8},{12,14},{14,12},{16,18},{18,... | collective-permute-start | bytes 147464 | tf_op jit(solution)/shard_map/ppermute | solution.py:423
  10.9 23.5 %collective-permute-done.3.pack1 = bf16[192,128]{1,0:T(8,128)(2,1)S(1)} collective-permute-done((bf16[192,128]{1,0:T(8,128)(2,1)S(1)}, bf16[192,128]{1,0:T(8,128)(2,1)S(1)}, u32[]{:S(2)}, u32[]{:S(2)}) %collective-permute-start.3) | collective-permute-done | bytes 49184 | tf_op jit(solution)/shard_map/ppermute | solution.py:423
  34.4 0.6 collective-permute-start.4
  35.0 2.6 %collective-permute-start.7 = (bf16[64,128]{1,0:T(8,128)(2,1)S(1)}, bf16[64,128]{1,0:T(8,128)(2,1)S(1)}, u32[]{:S(2)}, u32[]{:S(2)}) collective-permute-start(bf16[64,128]{1,0:T(8,128)(2,1)S(1)} %get-tuple-element.29), channel_id=1, source_target_pairs={{0,16},{2,18},{4,20},{6,22},{8,24},{10,26},{12,28},{14,30},{16,0},... | collective-permute-start | bytes 49160 | tf_op jit(solution)/shard_map/ppermute | solution.py:423
  37.6 2.1 %collective-permute-done.7.refs_0_ = bf16[64,128]{1,0:T(8,128)(2,1)S(1)} collective-permute-done((bf16[64,128]{1,0:T(8,128)(2,1)S(1)}, bf16[64,128]{1,0:T(8,128)(2,1)S(1)}, u32[]{:S(2)}, u32[]{:S(2)}) %collective-permute-start.7) | collective-permute-done | bytes 16416 | tf_op jit(solution)/shard_map/ppermute | solution.py:423
  39.7 1.6 %collective-permute-start.8 = (bf16[64,128]{1,0:T(8,128)(2,1)S(1)}, bf16[64,128]{1,0:T(8,128)(2,1)S(1)}, u32[]{:S(2)}, u32[]{:S(2)}) collective-permute-start(bf16[64,128]{1,0:T(8,128)(2,1)S(1)} %get-tuple-element.29), channel_id=1, source_target_pairs={{0,24},{2,26},{4,28},{6,30},{8,16},{10,18},{12,20},{14,22},{16,8},... | collective-permute-start | bytes 49160 | tf_op jit(solution)/shard_map/ppermute | solution.py:423
  41.2 1.5 %shard_map.125.refs_0_ = bf16[8,256,256]{2,1,0:T(8,128)(2,1)S(1)} custom-call(bf16[16,64,256]{2,1,0:T(8,128)(2,1)} %basis_hbm.5, bf16[16,64,256]{2,1,0:T(8,128)(2,1)} %coupling_hbm.3), custom_call_target="tpu_custom_call" | custom-call | flops 67108864 | bytes 2097152 | tf_op jit(solution)/shard_map/pallas_call | solution.py:427
  42.8 0.6 collective-permute-done.8.refs_1_
  43.4 1.5 %collective-permute-start.9 = (bf16[128,128]{1,0:T(8,128)(2,1)S(1)}, bf16[128,128]{1,0:T(8,128)(2,1)S(1)}, u32[]{:S(2)}, u32[]{:S(2)}) collective-permute-start(bf16[128,128]{1,0:T(8,128)(2,1)S(1)} %shard_map.123.beyond0), channel_id=1, source_target_pairs={{0,4},{2,6},{4,0},{6,2},{8,12},{10,14},{12,8},{14,10},{16,20},{18,... | collective-permute-start | bytes 98312 | tf_op jit(solution)/shard_map/ppermute | solution.py:423
  44.9 0.0 collective-permute-done.4.pair1
  44.9 0.0 copy-start
  44.9 0.0 copy-start.1
  45.0 0.0 copy-start.2
  45.0 0.0 copy-start.3
  45.0 0.0 copy-start.4
  45.0 0.0 copy-start.5
  45.0 2.2 %collective-permute-start.5 = (bf16[576,128]{1,0:T(8,128)(2,1)S(1)}, bf16[576,128]{1,0:T(8,128)(2,1)S(1)}, u32[]{:S(2)}, u32[]{:S(2)}) collective-permute-start(bf16[576,128]{1,0:T(8,128)(2,1)S(1)} %shard_map.122.plane), channel_id=1, source_target_pairs={{0,8},{2,10},{4,12},{6,14},{8,0},{10,2},{12,4},{14,6},{16,24},{18,... | collective-permute-start | bytes 442376 | tf_op jit(solution)/shard_map/ppermute | solution.py:423
  47.2 0.0 collective-permute-done.1.bulk1
  47.2 5.0 %collective-permute-start.6 = (bf16[576,128]{1,0:T(8,128)(2,1)S(1)}, bf16[576,128]{1,0:T(8,128)(2,1)S(1)}, u32[]{:S(2)}, u32[]{:S(2)}) collective-permute-start(bf16[576,128]{1,0:T(8,128)(2,1)S(1)} %shard_map.122.plane), channel_id=1, source_target_pairs={{8,16},{10,18},{12,20},{14,22},{16,8},{18,10},{20,12},{22,14},{9,1... | collective-permute-start | bytes 442376 | tf_op jit(solution)/shard_map/ppermute | solution.py:423
  52.2 0.0 collective-permute-done.other
  52.2 8.4 %shard_map.120 = (f32[2048,128]{1,0:T(8,128)S(1)}, f32[2048,128]{1,0:T(8,128)S(1)}, bf16[8,4,256,256]{3,2,1,0:T(8,128)(2,1)S(1)}) custom-call(s32[8,16]{1,0:T(8,128)} %bitcast.3, s32[16]{0:T(128)} %count.3, bf16[16,4,256,256]{3,2,1,0:T(8,128)(2,1)} %tiles_hbm.1, bf16[16,4,256,256]{3,2,1,0:T(8,128)(2,1)S(1)} %collective-permute-done.other, ...), custom_call_target="tpu_custom_call" | custom-call | flops 2147483648 | bytes 16777216 | tf_op jit(solution)/shard_map/pallas_call | solution.py:427
  60.6 0.0 collective-permute-done.9.beyond1
  60.6 0.0 collective-permute-done.5.next_a
  60.6 0.0 collective-permute-done.6.next_b
  60.7 3.4 %shard_map.124 = (f32[4096,128]{1,0:T(8,128)}, f32[2304,128]{1,0:T(8,128)S(1)}) custom-call(s32[4,16]{1,0:T(4,128)} %bitcast.5, s32[2,4]{1,0:T(2,128)} %mid_far.1, f32[2048,128]{1,0:T(8,128)S(1)} %get-tuple-element.25.near1, f32[2048,128]{1,0:T(8,128)S(1)} %get-tuple-element.26.near2, bf16[1024,128]{1,0:T(8,128)(2,1)S(1)} %get-tuple-element.19.coef, ...), custom_call_target="tpu_custom_call" | custom-call | flops 1073741824 | bytes 12582912 | tf_op jit(solution)/shard_map/pallas_call | solution.py:427
  64.1 0.0 collective-permute-done.2.bulk2
  64.1 3.4 %shard_map.127 = (f32[4096,128]{1,0:T(8,128)}, f32[2304,128]{1,0:T(8,128)S(1)}) custom-call(s32[11,40]{1,0:T(8,128)S(1)} %get-tuple-element.21.work, bf16[8,4,256,256]{3,2,1,0:T(8,128)(2,1)S(1)} %get-tuple-element.23.tiles, bf16[16,4,256,256]{3,2,1,0:T(8,128)(2,1)S(1)} %collective-permute-done.other, ...), custom_call_target="tpu_custom_call", output_to_operand_aliasing={{0}: (6, {}), {1}: (4, {})} | custom-call | flops 1073741824 | bytes 4194304 | tf_op jit(solution)/shard_map/pallas_call | solution.py:427
  (10 shorter events, 0.1 us)
Async XLA Ops:
  0.0 52.2 %collective-permute-start = (bf16[16,4,256,256]{3,2,1,0:T(8,128)(2,1)}, bf16[16,4,256,256]{3,2,1,0:T(8,128)(2,1)S(1)}, u32[]{:S(2)}, u32[]{:S(2)}) collective-permute-start(bf16[16,4,256,256]{3,2,1,0:T(8,128)(2,1)} %tiles_hbm.1), channel_id=1, source_target_pairs={{0,1},{1,0},{2,3},{3,2},{4,5},{5,4},{6,7},{7,6},{8,9},{9,8},{10,11... | collective-permute-start | bytes 25165832 | tf_op jit(solution)/shard_map/ppermute | solution.py:423
  2.1 45.1 %collective-permute-start.1 = (bf16[2560,128]{1,0:T(8,128)(2,1)S(1)}, bf16[2560,128]{1,0:T(8,128)(2,1)S(1)}, u32[]{:S(2)}, u32[]{:S(2)}) collective-permute-start(bf16[2560,128]{1,0:T(8,128)(2,1)S(1)} %get-tuple-element.22), channel_id=1, source_target_pairs={{0,2},{2,0},{4,6},{6,4},{8,10},{10,8},{12,14},{14,12},{16,18},{18,... | collective-permute-start | bytes 1966088 | tf_op jit(solution)/shard_map/ppermute | solution.py:423
  5.9 58.2 %collective-permute-start.2 = (bf16[2560,128]{1,0:T(8,128)(2,1)S(1)}, bf16[2560,128]{1,0:T(8,128)(2,1)S(1)}, u32[]{:S(2)}, u32[]{:S(2)}) collective-permute-start(bf16[2560,128]{1,0:T(8,128)(2,1)S(1)} %get-tuple-element.24), channel_id=1, source_target_pairs={{2,4},{6,8},{10,12},{14,16},{18,20},{22,24},{26,28},{4,2},{8,6},{1... | collective-permute-start | bytes 1966088 | tf_op jit(solution)/shard_map/ppermute | solution.py:423
  8.3 26.1 %collective-permute-start.3 = (bf16[192,128]{1,0:T(8,128)(2,1)S(1)}, bf16[192,128]{1,0:T(8,128)(2,1)S(1)}, u32[]{:S(2)}, u32[]{:S(2)}) collective-permute-start(bf16[192,128]{1,0:T(8,128)(2,1)S(1)} %get-tuple-element.27.pack), channel_id=1, source_target_pairs={{0,2},{2,0},{4,6},{6,4},{8,10},{10,8},{12,14},{14,12},{16,18},{18,... | collective-permute-start | bytes 147464 | tf_op jit(solution)/shard_map/ppermute | solution.py:423
  34.4 10.5 %collective-permute-start.4 = (bf16[320,128]{1,0:T(8,128)(2,1)S(1)}, bf16[320,128]{1,0:T(8,128)(2,1)S(1)}, u32[]{:S(2)}, u32[]{:S(2)}) collective-permute-start(bf16[320,128]{1,0:T(8,128)(2,1)S(1)} %get-tuple-element.28.pair), channel_id=1, source_target_pairs={{0,4},{2,6},{4,0},{6,2},{8,12},{10,14},{12,8},{14,10},{16,20},{18,... | collective-permute-start | bytes 245768 | tf_op jit(solution)/shard_map/ppermute | solution.py:423
  35.0 4.6 %collective-permute-start.7 = (bf16[64,128]{1,0:T(8,128)(2,1)S(1)}, bf16[64,128]{1,0:T(8,128)(2,1)S(1)}, u32[]{:S(2)}, u32[]{:S(2)}) collective-permute-start(bf16[64,128]{1,0:T(8,128)(2,1)S(1)} %get-tuple-element.29), channel_id=1, source_target_pairs={{0,16},{2,18},{4,20},{6,22},{8,24},{10,26},{12,28},{14,30},{16,0},... | collective-permute-start | bytes 49160 | tf_op jit(solution)/shard_map/ppermute | solution.py:423
  39.7 3.7 %collective-permute-start.8 = (bf16[64,128]{1,0:T(8,128)(2,1)S(1)}, bf16[64,128]{1,0:T(8,128)(2,1)S(1)}, u32[]{:S(2)}, u32[]{:S(2)}) collective-permute-start(bf16[64,128]{1,0:T(8,128)(2,1)S(1)} %get-tuple-element.29), channel_id=1, source_target_pairs={{0,24},{2,26},{4,28},{6,30},{8,16},{10,18},{12,20},{14,22},{16,8},... | collective-permute-start | bytes 49160 | tf_op jit(solution)/shard_map/ppermute | solution.py:423
  43.4 17.2 %collective-permute-start.9 = (bf16[128,128]{1,0:T(8,128)(2,1)S(1)}, bf16[128,128]{1,0:T(8,128)(2,1)S(1)}, u32[]{:S(2)}, u32[]{:S(2)}) collective-permute-start(bf16[128,128]{1,0:T(8,128)(2,1)S(1)} %shard_map.123.beyond0), channel_id=1, source_target_pairs={{0,4},{2,6},{4,0},{6,2},{8,12},{10,14},{12,8},{14,10},{16,20},{18,... | collective-permute-start | bytes 98312 | tf_op jit(solution)/shard_map/ppermute | solution.py:423
  44.9 15.7 %copy-start = (bf16[16,64,256]{2,1,0:T(8,128)(2,1)S(1)}, bf16[16,64,256]{2,1,0:T(8,128)(2,1)}, u32[]{:S(2)}) copy-start(bf16[16,64,256]{2,1,0:T(8,128)(2,1)} %basis_hbm.5) | copy-start | bytes 1572868
  44.9 15.7 %copy-start.1 = (bf16[16,64,256]{2,1,0:T(8,128)(2,1)S(1)}, bf16[16,64,256]{2,1,0:T(8,128)(2,1)}, u32[]{:S(2)}) copy-start(bf16[16,64,256]{2,1,0:T(8,128)(2,1)} %coupling_hbm.3) | copy-start | bytes 1572868
  45.0 15.7 %copy-start.2 = (bf16[2,64,512]{2,1,0:T(8,128)(2,1)S(1)}, bf16[2,64,512]{2,1,0:T(8,128)(2,1)}, u32[]{:S(2)}) copy-start(bf16[2,64,512]{2,1,0:T(8,128)(2,1)} %up_leaf.1) | copy-start | bytes 393220
  45.0 15.7 %copy-start.3 = (bf16[2,64,64]{2,1,0:T(8,128)(2,1)S(1)}, bf16[2,64,64]{2,1,0:T(8,128)(2,1)}, u32[]{:S(2)}) copy-start(bf16[2,64,64]{2,1,0:T(8,128)(2,1)} %up_mid.1) | copy-start | bytes 49156
  45.0 15.7 %copy-start.4 = (bf16[4,64,256]{2,1,0:T(8,128)(2,1)S(1)}, bf16[4,64,256]{2,1,0:T(8,128)(2,1)}, u32[]{:S(2)}) copy-start(bf16[4,64,256]{2,1,0:T(8,128)(2,1)} %top_coupling.1) | copy-start | bytes 393220
  45.0 15.7 %copy-start.5 = (bf16[2,64,256]{2,1,0:T(8,128)(2,1)S(1)}, bf16[2,64,256]{2,1,0:T(8,128)(2,1)}, u32[]{:S(2)}) copy-start(bf16[2,64,256]{2,1,0:T(8,128)(2,1)} %mid_coupling.1) | copy-start | bytes 196612
  45.0 15.6 %collective-permute-start.5 = (bf16[576,128]{1,0:T(8,128)(2,1)S(1)}, bf16[576,128]{1,0:T(8,128)(2,1)S(1)}, u32[]{:S(2)}, u32[]{:S(2)}) collective-permute-start(bf16[576,128]{1,0:T(8,128)(2,1)S(1)} %shard_map.122.plane), channel_id=1, source_target_pairs={{0,8},{2,10},{4,12},{6,14},{8,0},{10,2},{12,4},{14,6},{16,24},{18,... | collective-permute-start | bytes 442376 | tf_op jit(solution)/shard_map/ppermute | solution.py:423
  47.2 13.4 %collective-permute-start.6 = (bf16[576,128]{1,0:T(8,128)(2,1)S(1)}, bf16[576,128]{1,0:T(8,128)(2,1)S(1)}, u32[]{:S(2)}, u32[]{:S(2)}) collective-permute-start(bf16[576,128]{1,0:T(8,128)(2,1)S(1)} %shard_map.122.plane), channel_id=1, source_target_pairs={{8,16},{10,18},{12,20},{14,22},{16,8},{18,10},{20,12},{22,14},{9,1... | collective-permute-start | bytes 442376 | tf_op jit(solution)/shard_map/ppermute | solution.py:423

commit v6 on v5

--- a/solution.py
+++ b/solution.py
@@ -101,43 +101,38 @@
     bulk2[pl.ds(CHILD * rank, CHILD * leaf), :] = src[blocks(base, CHILD, leaf), :]
     lowest = jnp.where(odd == 1, leaves, -CHILD) + device * leaves
 
-    room = work.shape[1] // 2
-    for part in range(2):
-        start = jnp.bitwise_xor(part, odd) * (CHILD // 2)
-
-        def row(t, found):
-            n = start + t
-            live = count[base + n]
-            for f in range(FAR):
-                at = leaf_far[f, base + n] - lowest
-                work[7 + f, n] = jnp.where((at >= 0) & (at < CHILD), at, CHILD)
-            out = []
-            for r, owner in ((0, core), (1, 1 - core)):
-                at = found[r]
-                for k in range(slots):
-                    slot = owner * slots + k
-                    outside = index[slot, base + n] - lowest
-                    work[3 * r, at] = n * slots + k
-                    work[3 * r + 1, at] = outside
-                    work[3 * r + 2, at] = n
-                    use = (slot < live) & (outside >= 0) & (outside < CHILD)
-                    at = at + use.astype(jnp.int32)
-                out.append(at)
-            return tuple(out)
-
-        begin = jnp.int32(part * room)
-        found = lax.fori_loop(0, CHILD // 2, row, (begin, begin))
-        rounds = (jnp.maximum(found[0], found[1]) - begin + BATCH - 1) // BATCH
-        work[6, part] = rounds
-        for r in range(2):
-
-            def fill(n, _):
-                work[3 * r, n] = 0
-                work[3 * r + 1, n] = 0
-                work[3 * r + 2, n] = CHILD
-                return 0
-
-            lax.fori_loop(found[r], begin + rounds * BATCH, fill, 0)
+
+    def row(n, found):
+        live = count[base + n]
+        for f in range(FAR):
+            at = leaf_far[f, base + n] - lowest
+            work[7 + f, n] = jnp.where((at >= 0) & (at < CHILD), at, CHILD)
+        out = []
+        for r, owner in ((0, core), (1, 1 - core)):
+            at = found[r]
+            for k in range(slots):
+                slot = owner * slots + k
+                outside = index[slot, base + n] - lowest
+                work[3 * r, at] = n * slots + k
+                work[3 * r + 1, at] = outside
+                work[3 * r + 2, at] = n
+                use = (slot < live) & (outside >= 0) & (outside < CHILD)
+                at = at + use.astype(jnp.int32)
+            out.append(at)
+        return tuple(out)
+
+    found = lax.fori_loop(0, CHILD, row, (jnp.int32(0), jnp.int32(0)))
+    rounds = (jnp.maximum(found[0], found[1]) + BATCH - 1) // BATCH
+    work[6, 0] = rounds
+    for r in range(2):
+
+        def fill(n, _):
+            work[3 * r, n] = 0
+            work[3 * r + 1, n] = 0
+            work[3 * r + 2, n] = CHILD
+            return 0
+
+        lax.fori_loop(found[r], rounds * BATCH, fill, 0)
 
 
 def fold(group, after, basis_hbm, coupling_hbm, *refs):
@@ -356,30 +351,24 @@
     window[pl.ds(0, CHILD * rank), :] = bulk2[pl.ds(0, CHILD * rank), :]
     window[pl.ds(CHILD * rank, rank), :] = jnp.zeros((rank, bulk2.shape[1]), BF16)
     skip = CHILD * rank
-    room = work.shape[1] // 2
-    count = CHILD // 2
+
+    def step(t, _):
+        for b in range(BATCH):
+            n = t * BATCH + b
+            for r, held, low in ((0, tiles, 0), (1, other, base)):
+                tile = work[3 * r, n]
+                at = pl.multiple_of(skip + work[3 * r + 1, n] * leaf, rank)
+                part = mm(held[low + tile // slots, lax.rem(tile, slots)], bulk2[pl.ds(at, leaf), :])
+                acc[blocks(work[3 * r + 2, n], 1, leaf), :] += part
+        return 0
+
+    lax.fori_loop(0, work[6, 0], step, 0)
     stores = []
-    for half in range(2):
-        start = jnp.bitwise_xor(half, odd) * count
-        for t in range(count):
-            n = start + t
-            picked = [window[blocks(work[7 + f, n], 1, rank), :] for f in range(FAR)]
-            acc[blocks(n, 1, leaf), :] += mm(folded[n], jnp.concatenate(picked, axis=0))
-
-        def step(t, _):
-            for b in range(BATCH):
-                n = half * room + t * BATCH + b
-                for r, held, low in ((0, tiles, 0), (1, other, base)):
-                    tile = work[3 * r, n]
-                    at = pl.multiple_of(skip + work[3 * r + 1, n] * leaf, rank)
-                    part = mm(held[low + tile // slots, lax.rem(tile, slots)], bulk2[pl.ds(at, leaf), :])
-                    acc[blocks(work[3 * r + 2, n], 1, leaf), :] += part
-            return 0
-
-        lax.fori_loop(0, work[6, half], step, 0)
-        stores.append(
-            pltpu.make_async_copy(acc.at[blocks(start, count, leaf)], out.at[blocks(base + start, count, leaf)], sems.at[half])
-        )
+    for n in range(CHILD):
+        rows = pl.ds(n * leaf, leaf)
+        picked = [window[blocks(work[7 + f, n], 1, rank), :] for f in range(FAR)]
+        acc[rows, :] += mm(folded[n], jnp.concatenate(picked, axis=0))
+        stores.append(pltpu.make_async_copy(acc.at[rows], out.at[blocks(base + n, 1, leaf)], sems.at[n]))
         stores[-1].start()
     for store in stores:
         store.wait()
@@ -467,7 +456,7 @@
 
     work, bulk2 = call(
         prepare,
-        (sds((7 + FAR, CHILD * slots + 2 * BATCH), jnp.int32), sds((edge_c + edge, cols), BF16)),
+        (sds((7 + FAR, CHILD * slots + BATCH), jnp.int32), sds((edge_c + edge, cols), BF16)),
         [SMEM, SMEM, SMEM, VMEM, VMEM],
         (SMEM, VMEM),
         [],
@@ -572,7 +561,7 @@
         (sds((rows, cols), F32), sds((edge + leaf, cols), F32)),
         [SMEM] + [VMEM] * 5 + [ANY],
         (ANY, VMEM),
-        [pltpu.VMEM((edge_c + rank, cols), BF16), pltpu.SemaphoreType.DMA((2,))],
+        [pltpu.VMEM((edge_c + rank, cols), BF16), pltpu.SemaphoreType.DMA((CHILD,))],
         8,
         cost(leaves * slots * product_flops, 4 << 20),
         input_output_aliases={6: 0, 4: 1},

time: 67.8 us -> 67.6 us (level)
  no operation moved by 1% of the time
where the time goes in v6:
time: 67.6 us; the launch traced here: 67.3 us
  waiting for transfers between devices  26.2 us (39%)
  Pallas kernels  20.9 us (31%)
  starting transfers between devices  19.9 us (29%)
    ppermute x10, waiting for transfers between devices, send(): return lax.ppermute(x, axis, pairs)  26.2 us
    pallas_call x10, Pallas kernels, run(): pl.pallas_call(kernel, out_shape=out_shape, in_specs=in_specs, out_specs=...  20.9 us
    ppermute x10, starting transfers between devices, send(): return lax.ppermute(x, axis, pairs)  19.9 us
  transfers between devices with their start and end apart: 10, of which 3 were waited for; matrix products, arithmetic and copies ran while one was open for 0% of the time, Pallas kernels for 26%

profile of v6, /device:TPU:12, one launch (start us, length us, event | category | flops | bytes accessed | tf_op | source)
XLA Modules:
  0.0 67.3 jit_solution(4189441089495007292)
XLA Ops:
  0.0 0.0 collective-permute-start
  0.0 2.1 %shard_map.118 = (bf16[192,128]{1,0:T(8,128)(2,1)S(1)}, bf16[2560,128]{1,0:T(8,128)(2,1)S(1)}, bf16[1024,128]{1,0:T(8,128)(2,1)S(1)}, bf16[4352,128]{1,0:T(8,128)(2,1)S(1)}) custom-call(bf16[4096,128]{1,0:T(8,128)(2,1)} %src_hbm.1, bf16[16,64,256]{2,1,0:T(8,128)(2,1)} %basis_hbm.5, bf16[2,64,512]{2,1,0:T(8,128)(2,1)} %up_leaf.1, bf16[2,64,64]{2,1,0:T(8,128)(2,1)} %up_mid.1), custom_call_target="tpu_custom_call" | custom-call | flops 67108864 | bytes 4194304 | tf_op jit(solution)/shard_map/pallas_call | solution.py:416
  2.1 1.5 %collective-permute-start.1 = (bf16[2560,128]{1,0:T(8,128)(2,1)S(1)}, bf16[2560,128]{1,0:T(8,128)(2,1)S(1)}, u32[]{:S(2)}, u32[]{:S(2)}) collective-permute-start(bf16[2560,128]{1,0:T(8,128)(2,1)S(1)} %get-tuple-element.22), channel_id=1, source_target_pairs={{0,2},{2,0},{4,6},{6,4},{8,10},{10,8},{12,14},{14,12},{16,18},{18,... | collective-permute-start | bytes 1966088 | tf_op jit(solution)/shard_map/ppermute | solution.py:412
  3.7 2.2 %shard_map.119 = (s32[11,36]{1,0:T(8,128)S(1)}, bf16[2560,128]{1,0:T(8,128)(2,1)S(1)}) custom-call(s32[8,16]{1,0:T(8,128)} %bitcast.2, s32[16]{0:T(128)} %count.3, s32[4,16]{1,0:T(4,128)} %bitcast.4, bf16[1024,128]{1,0:T(8,128)(2,1)S(1)} %get-tuple-element.19.coef, bf16[4352,128]{1,0:T(8,128)(2,1)S(1)} %get-tuple-element.20.src), custom_call_target="tpu_custom_call" | custom-call | bytes 4194304 | tf_op jit(solution)/shard_map/pallas_call | solution.py:416
  5.9 2.4 %collective-permute-start.2 = (bf16[2560,128]{1,0:T(8,128)(2,1)S(1)}, bf16[2560,128]{1,0:T(8,128)(2,1)S(1)}, u32[]{:S(2)}, u32[]{:S(2)}) collective-permute-start(bf16[2560,128]{1,0:T(8,128)(2,1)S(1)} %get-tuple-element.24), channel_id=1, source_target_pairs={{2,4},{6,8},{10,12},{14,16},{18,20},{22,24},{26,28},{4,2},{8,6},{1... | collective-permute-start | bytes 1966088 | tf_op jit(solution)/shard_map/ppermute | solution.py:412
  8.3 2.6 %collective-permute-start.3 = (bf16[192,128]{1,0:T(8,128)(2,1)S(1)}, bf16[192,128]{1,0:T(8,128)(2,1)S(1)}, u32[]{:S(2)}, u32[]{:S(2)}) collective-permute-start(bf16[192,128]{1,0:T(8,128)(2,1)S(1)} %get-tuple-element.27.pack), channel_id=1, source_target_pairs={{0,2},{2,0},{4,6},{6,4},{8,10},{10,8},{12,14},{14,12},{16,18},{18,... | collective-permute-start | bytes 147464 | tf_op jit(solution)/shard_map/ppermute | solution.py:412
  10.9 23.6 %collective-permute-done.3.pack1 = bf16[192,128]{1,0:T(8,128)(2,1)S(1)} collective-permute-done((bf16[192,128]{1,0:T(8,128)(2,1)S(1)}, bf16[192,128]{1,0:T(8,128)(2,1)S(1)}, u32[]{:S(2)}, u32[]{:S(2)}) %collective-permute-start.3) | collective-permute-done | bytes 49184 | tf_op jit(solution)/shard_map/ppermute | solution.py:412
  34.4 0.6 collective-permute-start.4
  35.0 2.6 %collective-permute-start.7 = (bf16[64,128]{1,0:T(8,128)(2,1)S(1)}, bf16[64,128]{1,0:T(8,128)(2,1)S(1)}, u32[]{:S(2)}, u32[]{:S(2)}) collective-permute-start(bf16[64,128]{1,0:T(8,128)(2,1)S(1)} %get-tuple-element.29), channel_id=1, source_target_pairs={{0,16},{2,18},{4,20},{6,22},{8,24},{10,26},{12,28},{14,30},{16,0},... | collective-permute-start | bytes 49160 | tf_op jit(solution)/shard_map/ppermute | solution.py:412
  37.6 2.1 %collective-permute-done.7.refs_0_ = bf16[64,128]{1,0:T(8,128)(2,1)S(1)} collective-permute-done((bf16[64,128]{1,0:T(8,128)(2,1)S(1)}, bf16[64,128]{1,0:T(8,128)(2,1)S(1)}, u32[]{:S(2)}, u32[]{:S(2)}) %collective-permute-start.7) | collective-permute-done | bytes 16416 | tf_op jit(solution)/shard_map/ppermute | solution.py:412
  39.7 1.6 %collective-permute-start.8 = (bf16[64,128]{1,0:T(8,128)(2,1)S(1)}, bf16[64,128]{1,0:T(8,128)(2,1)S(1)}, u32[]{:S(2)}, u32[]{:S(2)}) collective-permute-start(bf16[64,128]{1,0:T(8,128)(2,1)S(1)} %get-tuple-element.29), channel_id=1, source_target_pairs={{0,24},{2,26},{4,28},{6,30},{8,16},{10,18},{12,20},{14,22},{16,8},... | collective-permute-start | bytes 49160 | tf_op jit(solution)/shard_map/ppermute | solution.py:412
  41.2 1.5 %shard_map.125.refs_0_ = bf16[8,256,256]{2,1,0:T(8,128)(2,1)S(1)} custom-call(bf16[16,64,256]{2,1,0:T(8,128)(2,1)} %basis_hbm.5, bf16[16,64,256]{2,1,0:T(8,128)(2,1)} %coupling_hbm.3), custom_call_target="tpu_custom_call" | custom-call | flops 67108864 | bytes 2097152 | tf_op jit(solution)/shard_map/pallas_call | solution.py:416
  42.8 0.6 collective-permute-done.8.refs_1_
  43.4 1.5 %collective-permute-start.9 = (bf16[128,128]{1,0:T(8,128)(2,1)S(1)}, bf16[128,128]{1,0:T(8,128)(2,1)S(1)}, u32[]{:S(2)}, u32[]{:S(2)}) collective-permute-start(bf16[128,128]{1,0:T(8,128)(2,1)S(1)} %shard_map.123.beyond0), channel_id=1, source_target_pairs={{0,4},{2,6},{4,0},{6,2},{8,12},{10,14},{12,8},{14,10},{16,20},{18,... | collective-permute-start | bytes 98312 | tf_op jit(solution)/shard_map/ppermute | solution.py:412
  44.9 0.0 collective-permute-done.4.pair1
  44.9 0.0 copy-start
  44.9 0.0 copy-start.1
  45.0 0.0 copy-start.2
  45.0 0.0 copy-start.3
  45.0 0.0 copy-start.4
  45.0 0.0 copy-start.5
  45.0 2.2 %collective-permute-start.5 = (bf16[576,128]{1,0:T(8,128)(2,1)S(1)}, bf16[576,128]{1,0:T(8,128)(2,1)S(1)}, u32[]{:S(2)}, u32[]{:S(2)}) collective-permute-start(bf16[576,128]{1,0:T(8,128)(2,1)S(1)} %shard_map.122.plane), channel_id=1, source_target_pairs={{0,8},{2,10},{4,12},{6,14},{8,0},{10,2},{12,4},{14,6},{16,24},{18,... | collective-permute-start | bytes 442376 | tf_op jit(solution)/shard_map/ppermute | solution.py:412
  47.2 0.0 collective-permute-done.1.bulk1
  47.2 5.0 %collective-permute-start.6 = (bf16[576,128]{1,0:T(8,128)(2,1)S(1)}, bf16[576,128]{1,0:T(8,128)(2,1)S(1)}, u32[]{:S(2)}, u32[]{:S(2)}) collective-permute-start(bf16[576,128]{1,0:T(8,128)(2,1)S(1)} %shard_map.122.plane), channel_id=1, source_target_pairs={{8,16},{10,18},{12,20},{14,22},{16,8},{18,10},{20,12},{22,14},{9,1... | collective-permute-start | bytes 442376 | tf_op jit(solution)/shard_map/ppermute | solution.py:412
  52.2 0.0 collective-permute-done.other
  52.2 8.4 %shard_map.120 = (f32[2048,128]{1,0:T(8,128)S(1)}, f32[2048,128]{1,0:T(8,128)S(1)}, bf16[8,4,256,256]{3,2,1,0:T(8,128)(2,1)S(1)}) custom-call(s32[8,16]{1,0:T(8,128)} %bitcast.3, s32[16]{0:T(128)} %count.3, bf16[16,4,256,256]{3,2,1,0:T(8,128)(2,1)} %tiles_hbm.1, bf16[16,4,256,256]{3,2,1,0:T(8,128)(2,1)S(1)} %collective-permute-done.other, ...), custom_call_target="tpu_custom_call" | custom-call | flops 2147483648 | bytes 16777216 | tf_op jit(solution)/shard_map/pallas_call | solution.py:416
  60.6 0.0 collective-permute-done.9.beyond1
  60.6 0.0 collective-permute-done.5.next_a
  60.6 0.0 collective-permute-done.6.next_b
  60.7 3.4 %shard_map.124 = (f32[4096,128]{1,0:T(8,128)}, f32[2304,128]{1,0:T(8,128)S(1)}) custom-call(s32[4,16]{1,0:T(4,128)} %bitcast.5, s32[2,4]{1,0:T(2,128)} %mid_far.1, f32[2048,128]{1,0:T(8,128)S(1)} %get-tuple-element.25.near1, f32[2048,128]{1,0:T(8,128)S(1)} %get-tuple-element.26.near2, bf16[1024,128]{1,0:T(8,128)(2,1)S(1)} %get-tuple-element.19.coef, ...), custom_call_target="tpu_custom_call" | custom-call | flops 1073741824 | bytes 12582912 | tf_op jit(solution)/shard_map/pallas_call | solution.py:416
  64.1 0.0 collective-permute-done.2.bulk2
  64.1 3.3 %shard_map.127 = (f32[4096,128]{1,0:T(8,128)}, f32[2304,128]{1,0:T(8,128)S(1)}) custom-call(s32[11,36]{1,0:T(8,128)S(1)} %get-tuple-element.21.work, bf16[8,4,256,256]{3,2,1,0:T(8,128)(2,1)S(1)} %get-tuple-element.23.tiles, bf16[16,4,256,256]{3,2,1,0:T(8,128)(2,1)S(1)} %collective-permute-done.other, ...), custom_call_target="tpu_custom_call", output_to_operand_aliasing={{0}: (6, {}), {1}: (4, {})} | custom-call | flops 1073741824 | bytes 4194304 | tf_op jit(solution)/shard_map/pallas_call | solution.py:416
  (10 shorter events, 0.1 us)
Async XLA Ops:
  0.0 52.2 %collective-permute-start = (bf16[16,4,256,256]{3,2,1,0:T(8,128)(2,1)}, bf16[16,4,256,256]{3,2,1,0:T(8,128)(2,1)S(1)}, u32[]{:S(2)}, u32[]{:S(2)}) collective-permute-start(bf16[16,4,256,256]{3,2,1,0:T(8,128)(2,1)} %tiles_hbm.1), channel_id=1, source_target_pairs={{0,1},{1,0},{2,3},{3,2},{4,5},{5,4},{6,7},{7,6},{8,9},{9,8},{10,11... | collective-permute-start | bytes 25165832 | tf_op jit(solution)/shard_map/ppermute | solution.py:412
  2.1 45.1 %collective-permute-start.1 = (bf16[2560,128]{1,0:T(8,128)(2,1)S(1)}, bf16[2560,128]{1,0:T(8,128)(2,1)S(1)}, u32[]{:S(2)}, u32[]{:S(2)}) collective-permute-start(bf16[2560,128]{1,0:T(8,128)(2,1)S(1)} %get-tuple-element.22), channel_id=1, source_target_pairs={{0,2},{2,0},{4,6},{6,4},{8,10},{10,8},{12,14},{14,12},{16,18},{18,... | collective-permute-start | bytes 1966088 | tf_op jit(solution)/shard_map/ppermute | solution.py:412
  5.9 58.2 %collective-permute-start.2 = (bf16[2560,128]{1,0:T(8,128)(2,1)S(1)}, bf16[2560,128]{1,0:T(8,128)(2,1)S(1)}, u32[]{:S(2)}, u32[]{:S(2)}) collective-permute-start(bf16[2560,128]{1,0:T(8,128)(2,1)S(1)} %get-tuple-element.24), channel_id=1, source_target_pairs={{2,4},{6,8},{10,12},{14,16},{18,20},{22,24},{26,28},{4,2},{8,6},{1... | collective-permute-start | bytes 1966088 | tf_op jit(solution)/shard_map/ppermute | solution.py:412
  8.3 26.2 %collective-permute-start.3 = (bf16[192,128]{1,0:T(8,128)(2,1)S(1)}, bf16[192,128]{1,0:T(8,128)(2,1)S(1)}, u32[]{:S(2)}, u32[]{:S(2)}) collective-permute-start(bf16[192,128]{1,0:T(8,128)(2,1)S(1)} %get-tuple-element.27.pack), channel_id=1, source_target_pairs={{0,2},{2,0},{4,6},{6,4},{8,10},{10,8},{12,14},{14,12},{16,18},{18,... | collective-permute-start | bytes 147464 | tf_op jit(solution)/shard_map/ppermute | solution.py:412
  34.4 10.5 %collective-permute-start.4 = (bf16[320,128]{1,0:T(8,128)(2,1)S(1)}, bf16[320,128]{1,0:T(8,128)(2,1)S(1)}, u32[]{:S(2)}, u32[]{:S(2)}) collective-permute-start(bf16[320,128]{1,0:T(8,128)(2,1)S(1)} %get-tuple-element.28.pair), channel_id=1, source_target_pairs={{0,4},{2,6},{4,0},{6,2},{8,12},{10,14},{12,8},{14,10},{16,20},{18,... | collective-permute-start | bytes 245768 | tf_op jit(solution)/shard_map/ppermute | solution.py:412
  35.0 4.6 %collective-permute-start.7 = (bf16[64,128]{1,0:T(8,128)(2,1)S(1)}, bf16[64,128]{1,0:T(8,128)(2,1)S(1)}, u32[]{:S(2)}, u32[]{:S(2)}) collective-permute-start(bf16[64,128]{1,0:T(8,128)(2,1)S(1)} %get-tuple-element.29), channel_id=1, source_target_pairs={{0,16},{2,18},{4,20},{6,22},{8,24},{10,26},{12,28},{14,30},{16,0},... | collective-permute-start | bytes 49160 | tf_op jit(solution)/shard_map/ppermute | solution.py:412
  39.7 3.7 %collective-permute-start.8 = (bf16[64,128]{1,0:T(8,128)(2,1)S(1)}, bf16[64,128]{1,0:T(8,128)(2,1)S(1)}, u32[]{:S(2)}, u32[]{:S(2)}) collective-permute-start(bf16[64,128]{1,0:T(8,128)(2,1)S(1)} %get-tuple-element.29), channel_id=1, source_target_pairs={{0,24},{2,26},{4,28},{6,30},{8,16},{10,18},{12,20},{14,22},{16,8},... | collective-permute-start | bytes 49160 | tf_op jit(solution)/shard_map/ppermute | solution.py:412
  43.4 17.2 %collective-permute-start.9 = (bf16[128,128]{1,0:T(8,128)(2,1)S(1)}, bf16[128,128]{1,0:T(8,128)(2,1)S(1)}, u32[]{:S(2)}, u32[]{:S(2)}) collective-permute-start(bf16[128,128]{1,0:T(8,128)(2,1)S(1)} %shard_map.123.beyond0), channel_id=1, source_target_pairs={{0,4},{2,6},{4,0},{6,2},{8,12},{10,14},{12,8},{14,10},{16,20},{18,... | collective-permute-start | bytes 98312 | tf_op jit(solution)/shard_map/ppermute | solution.py:412
  44.9 15.7 %copy-start = (bf16[16,64,256]{2,1,0:T(8,128)(2,1)S(1)}, bf16[16,64,256]{2,1,0:T(8,128)(2,1)}, u32[]{:S(2)}) copy-start(bf16[16,64,256]{2,1,0:T(8,128)(2,1)} %basis_hbm.5) | copy-start | bytes 1572868
  44.9 15.7 %copy-start.1 = (bf16[16,64,256]{2,1,0:T(8,128)(2,1)S(1)}, bf16[16,64,256]{2,1,0:T(8,128)(2,1)}, u32[]{:S(2)}) copy-start(bf16[16,64,256]{2,1,0:T(8,128)(2,1)} %coupling_hbm.3) | copy-start | bytes 1572868
  45.0 15.7 %copy-start.2 = (bf16[2,64,512]{2,1,0:T(8,128)(2,1)S(1)}, bf16[2,64,512]{2,1,0:T(8,128)(2,1)}, u32[]{:S(2)}) copy-start(bf16[2,64,512]{2,1,0:T(8,128)(2,1)} %up_leaf.1) | copy-start | bytes 393220
  45.0 15.7 %copy-start.3 = (bf16[2,64,64]{2,1,0:T(8,128)(2,1)S(1)}, bf16[2,64,64]{2,1,0:T(8,128)(2,1)}, u32[]{:S(2)}) copy-start(bf16[2,64,64]{2,1,0:T(8,128)(2,1)} %up_mid.1) | copy-start | bytes 49156
  45.0 15.7 %copy-start.4 = (bf16[4,64,256]{2,1,0:T(8,128)(2,1)S(1)}, bf16[4,64,256]{2,1,0:T(8,128)(2,1)}, u32[]{:S(2)}) copy-start(bf16[4,64,256]{2,1,0:T(8,128)(2,1)} %top_coupling.1) | copy-start | bytes 393220
  45.0 15.7 %copy-start.5 = (bf16[2,64,256]{2,1,0:T(8,128)(2,1)S(1)}, bf16[2,64,256]{2,1,0:T(8,128)(2,1)}, u32[]{:S(2)}) copy-start(bf16[2,64,256]{2,1,0:T(8,128)(2,1)} %mid_coupling.1) | copy-start | bytes 196612
  45.0 15.6 %collective-permute-start.5 = (bf16[576,128]{1,0:T(8,128)(2,1)S(1)}, bf16[576,128]{1,0:T(8,128)(2,1)S(1)}, u32[]{:S(2)}, u32[]{:S(2)}) collective-permute-start(bf16[576,128]{1,0:T(8,128)(2,1)S(1)} %shard_map.122.plane), channel_id=1, source_target_pairs={{0,8},{2,10},{4,12},{6,14},{8,0},{10,2},{12,4},{14,6},{16,24},{18,... | collective-permute-start | bytes 442376 | tf_op jit(solution)/shard_map/ppermute | solution.py:412
  47.2 13.4 %collective-permute-start.6 = (bf16[576,128]{1,0:T(8,128)(2,1)S(1)}, bf16[576,128]{1,0:T(8,128)(2,1)S(1)}, u32[]{:S(2)}, u32[]{:S(2)}) collective-permute-start(bf16[576,128]{1,0:T(8,128)(2,1)S(1)} %shard_map.122.plane), channel_id=1, source_target_pairs={{8,16},{10,18},{12,20},{14,22},{16,8},{18,10},{20,12},{22,14},{9,1... | collective-permute-start | bytes 442376 | tf_op jit(solution)/shard_map/ppermute | solution.py:412

commit v7 on v6

--- a/solution.py
+++ b/solution.py
@@ -143,7 +143,8 @@
     parent = device // group
     member = lax.rem(device, group)
     inner = (member > 0) & (member < group - 1)
-    early = (parent >= 2) | ((parent == 1) & inner)
+    core = lax.axis_index("col")
+    early = ((parent >= 2) | ((parent == 1) & inner)) & ((core == 0) | (parent >= 2))
 
     @pl.when(early != after)
     def _():
@@ -250,7 +251,7 @@
         )
         return 0
 
-    lax.fori_loop(0, CHILD, all1, 0, unroll=2)
+    lax.fori_loop(0, CHILD, all1, 0, unroll=4)
 
 
 def downward(

time: 67.6 us -> 67.3 us (level)
  no operation moved by 1% of the time
where the time goes in v7:
time: 67.3 us; the launch traced here: 67 us
  waiting for transfers between devices  26.2 us (39%)
  Pallas kernels  20.6 us (31%)
  starting transfers between devices  19.9 us (30%)
    ppermute x10, waiting for transfers between devices, send(): return lax.ppermute(x, axis, pairs)  26.2 us
    pallas_call x10, Pallas kernels, run(): pl.pallas_call(kernel, out_shape=out_shape, in_specs=in_specs, out_specs=...  20.6 us
    ppermute x10, starting transfers between devices, send(): return lax.ppermute(x, axis, pairs)  19.9 us
  transfers between devices with their start and end apart: 10, of which 3 were waited for; matrix products, arithmetic and copies ran while one was open for 0% of the time, Pallas kernels for 26%

profile of v7, /device:TPU:12, one launch (start us, length us, event | category | flops | bytes accessed | tf_op | source)
XLA Modules:
  0.0 67.0 jit_solution(4099848792957393252)
XLA Ops:
  0.0 0.0 collective-permute-start
  0.0 2.1 %shard_map.118 = (bf16[192,128]{1,0:T(8,128)(2,1)S(1)}, bf16[2560,128]{1,0:T(8,128)(2,1)S(1)}, bf16[1024,128]{1,0:T(8,128)(2,1)S(1)}, bf16[4352,128]{1,0:T(8,128)(2,1)S(1)}) custom-call(bf16[4096,128]{1,0:T(8,128)(2,1)} %src_hbm.1, bf16[16,64,256]{2,1,0:T(8,128)(2,1)} %basis_hbm.5, bf16[2,64,512]{2,1,0:T(8,128)(2,1)} %up_leaf.1, bf16[2,64,64]{2,1,0:T(8,128)(2,1)} %up_mid.1), custom_call_target="tpu_custom_call" | custom-call | flops 67108864 | bytes 4194304 | tf_op jit(solution)/shard_map/pallas_call | solution.py:417
  2.1 1.5 %collective-permute-start.1 = (bf16[2560,128]{1,0:T(8,128)(2,1)S(1)}, bf16[2560,128]{1,0:T(8,128)(2,1)S(1)}, u32[]{:S(2)}, u32[]{:S(2)}) collective-permute-start(bf16[2560,128]{1,0:T(8,128)(2,1)S(1)} %get-tuple-element.22), channel_id=1, source_target_pairs={{0,2},{2,0},{4,6},{6,4},{8,10},{10,8},{12,14},{14,12},{16,18},{18,... | collective-permute-start | bytes 1966088 | tf_op jit(solution)/shard_map/ppermute | solution.py:413
  3.7 2.2 %shard_map.119 = (s32[11,36]{1,0:T(8,128)S(1)}, bf16[2560,128]{1,0:T(8,128)(2,1)S(1)}) custom-call(s32[8,16]{1,0:T(8,128)} %bitcast.2, s32[16]{0:T(128)} %count.3, s32[4,16]{1,0:T(4,128)} %bitcast.4, bf16[1024,128]{1,0:T(8,128)(2,1)S(1)} %get-tuple-element.19.coef, bf16[4352,128]{1,0:T(8,128)(2,1)S(1)} %get-tuple-element.20.src), custom_call_target="tpu_custom_call" | custom-call | bytes 4194304 | tf_op jit(solution)/shard_map/pallas_call | solution.py:417
  5.9 2.4 %collective-permute-start.2 = (bf16[2560,128]{1,0:T(8,128)(2,1)S(1)}, bf16[2560,128]{1,0:T(8,128)(2,1)S(1)}, u32[]{:S(2)}, u32[]{:S(2)}) collective-permute-start(bf16[2560,128]{1,0:T(8,128)(2,1)S(1)} %get-tuple-element.24), channel_id=1, source_target_pairs={{2,4},{6,8},{10,12},{14,16},{18,20},{22,24},{26,28},{4,2},{8,6},{1... | collective-permute-start | bytes 1966088 | tf_op jit(solution)/shard_map/ppermute | solution.py:413
  8.3 2.6 %collective-permute-start.3 = (bf16[192,128]{1,0:T(8,128)(2,1)S(1)}, bf16[192,128]{1,0:T(8,128)(2,1)S(1)}, u32[]{:S(2)}, u32[]{:S(2)}) collective-permute-start(bf16[192,128]{1,0:T(8,128)(2,1)S(1)} %get-tuple-element.27.pack), channel_id=1, source_target_pairs={{0,2},{2,0},{4,6},{6,4},{8,10},{10,8},{12,14},{14,12},{16,18},{18,... | collective-permute-start | bytes 147464 | tf_op jit(solution)/shard_map/ppermute | solution.py:413
  10.9 23.6 %collective-permute-done.3.pack1 = bf16[192,128]{1,0:T(8,128)(2,1)S(1)} collective-permute-done((bf16[192,128]{1,0:T(8,128)(2,1)S(1)}, bf16[192,128]{1,0:T(8,128)(2,1)S(1)}, u32[]{:S(2)}, u32[]{:S(2)}) %collective-permute-start.3) | collective-permute-done | bytes 49184 | tf_op jit(solution)/shard_map/ppermute | solution.py:413
  34.4 0.6 collective-permute-start.4
  35.0 2.6 %collective-permute-start.7 = (bf16[64,128]{1,0:T(8,128)(2,1)S(1)}, bf16[64,128]{1,0:T(8,128)(2,1)S(1)}, u32[]{:S(2)}, u32[]{:S(2)}) collective-permute-start(bf16[64,128]{1,0:T(8,128)(2,1)S(1)} %get-tuple-element.29), channel_id=1, source_target_pairs={{0,16},{2,18},{4,20},{6,22},{8,24},{10,26},{12,28},{14,30},{16,0},... | collective-permute-start | bytes 49160 | tf_op jit(solution)/shard_map/ppermute | solution.py:413
  37.6 2.1 %collective-permute-done.7.refs_0_ = bf16[64,128]{1,0:T(8,128)(2,1)S(1)} collective-permute-done((bf16[64,128]{1,0:T(8,128)(2,1)S(1)}, bf16[64,128]{1,0:T(8,128)(2,1)S(1)}, u32[]{:S(2)}, u32[]{:S(2)}) %collective-permute-start.7) | collective-permute-done | bytes 16416 | tf_op jit(solution)/shard_map/ppermute | solution.py:413
  39.7 1.6 %collective-permute-start.8 = (bf16[64,128]{1,0:T(8,128)(2,1)S(1)}, bf16[64,128]{1,0:T(8,128)(2,1)S(1)}, u32[]{:S(2)}, u32[]{:S(2)}) collective-permute-start(bf16[64,128]{1,0:T(8,128)(2,1)S(1)} %get-tuple-element.29), channel_id=1, source_target_pairs={{0,24},{2,26},{4,28},{6,30},{8,16},{10,18},{12,20},{14,22},{16,8},... | collective-permute-start | bytes 49160 | tf_op jit(solution)/shard_map/ppermute | solution.py:413
  41.2 1.5 %shard_map.125.refs_0_ = bf16[8,256,256]{2,1,0:T(8,128)(2,1)S(1)} custom-call(bf16[16,64,256]{2,1,0:T(8,128)(2,1)} %basis_hbm.5, bf16[16,64,256]{2,1,0:T(8,128)(2,1)} %coupling_hbm.3), custom_call_target="tpu_custom_call" | custom-call | flops 67108864 | bytes 2097152 | tf_op jit(solution)/shard_map/pallas_call | solution.py:417
  42.8 0.6 collective-permute-done.8.refs_1_
  43.4 1.5 %collective-permute-start.9 = (bf16[128,128]{1,0:T(8,128)(2,1)S(1)}, bf16[128,128]{1,0:T(8,128)(2,1)S(1)}, u32[]{:S(2)}, u32[]{:S(2)}) collective-permute-start(bf16[128,128]{1,0:T(8,128)(2,1)S(1)} %shard_map.123.beyond0), channel_id=1, source_target_pairs={{0,4},{2,6},{4,0},{6,2},{8,12},{10,14},{12,8},{14,10},{16,20},{18,... | collective-permute-start | bytes 98312 | tf_op jit(solution)/shard_map/ppermute | solution.py:413
  44.9 0.0 collective-permute-done.4.pair1
  44.9 0.0 copy-start
  44.9 0.0 copy-start.1
  45.0 0.0 copy-start.2
  45.0 0.0 copy-start.3
  45.0 0.0 copy-start.4
  45.0 0.0 copy-start.5
  45.0 2.2 %collective-permute-start.5 = (bf16[576,128]{1,0:T(8,128)(2,1)S(1)}, bf16[576,128]{1,0:T(8,128)(2,1)S(1)}, u32[]{:S(2)}, u32[]{:S(2)}) collective-permute-start(bf16[576,128]{1,0:T(8,128)(2,1)S(1)} %shard_map.122.plane), channel_id=1, source_target_pairs={{0,8},{2,10},{4,12},{6,14},{8,0},{10,2},{12,4},{14,6},{16,24},{18,... | collective-permute-start | bytes 442376 | tf_op jit(solution)/shard_map/ppermute | solution.py:413
  47.2 0.0 collective-permute-done.1.bulk1
  47.2 5.0 %collective-permute-start.6 = (bf16[576,128]{1,0:T(8,128)(2,1)S(1)}, bf16[576,128]{1,0:T(8,128)(2,1)S(1)}, u32[]{:S(2)}, u32[]{:S(2)}) collective-permute-start(bf16[576,128]{1,0:T(8,128)(2,1)S(1)} %shard_map.122.plane), channel_id=1, source_target_pairs={{8,16},{10,18},{12,20},{14,22},{16,8},{18,10},{20,12},{22,14},{9,1... | collective-permute-start | bytes 442376 | tf_op jit(solution)/shard_map/ppermute | solution.py:413
  52.2 0.0 collective-permute-done.other
  52.2 8.1 %shard_map.120 = (f32[2048,128]{1,0:T(8,128)S(1)}, f32[2048,128]{1,0:T(8,128)S(1)}, bf16[8,4,256,256]{3,2,1,0:T(8,128)(2,1)S(1)}) custom-call(s32[8,16]{1,0:T(8,128)} %bitcast.3, s32[16]{0:T(128)} %count.3, bf16[16,4,256,256]{3,2,1,0:T(8,128)(2,1)} %tiles_hbm.1, bf16[16,4,256,256]{3,2,1,0:T(8,128)(2,1)S(1)} %collective-permute-done.other, ...), custom_call_target="tpu_custom_call" | custom-call | flops 2147483648 | bytes 16777216 | tf_op jit(solution)/shard_map/pallas_call | solution.py:417
  60.3 0.0 collective-permute-done.9.beyond1
  60.3 0.0 collective-permute-done.5.next_a
  60.3 0.0 collective-permute-done.6.next_b
  60.4 3.4 %shard_map.124 = (f32[4096,128]{1,0:T(8,128)}, f32[2304,128]{1,0:T(8,128)S(1)}) custom-call(s32[4,16]{1,0:T(4,128)} %bitcast.5, s32[2,4]{1,0:T(2,128)} %mid_far.1, f32[2048,128]{1,0:T(8,128)S(1)} %get-tuple-element.25.near1, f32[2048,128]{1,0:T(8,128)S(1)} %get-tuple-element.26.near2, bf16[1024,128]{1,0:T(8,128)(2,1)S(1)} %get-tuple-element.19.coef, ...), custom_call_target="tpu_custom_call" | custom-call | flops 1073741824 | bytes 12582912 | tf_op jit(solution)/shard_map/pallas_call | solution.py:417
  63.7 0.0 collective-permute-done.2.bulk2
  63.7 3.3 %shard_map.127 = (f32[4096,128]{1,0:T(8,128)}, f32[2304,128]{1,0:T(8,128)S(1)}) custom-call(s32[11,36]{1,0:T(8,128)S(1)} %get-tuple-element.21.work, bf16[8,4,256,256]{3,2,1,0:T(8,128)(2,1)S(1)} %get-tuple-element.23.tiles, bf16[16,4,256,256]{3,2,1,0:T(8,128)(2,1)S(1)} %collective-permute-done.other, ...), custom_call_target="tpu_custom_call", output_to_operand_aliasing={{0}: (6, {}), {1}: (4, {})} | custom-call | flops 1073741824 | bytes 4194304 | tf_op jit(solution)/shard_map/pallas_call | solution.py:417
  (10 shorter events, 0.1 us)
Async XLA Ops:
  0.0 52.2 %collective-permute-start = (bf16[16,4,256,256]{3,2,1,0:T(8,128)(2,1)}, bf16[16,4,256,256]{3,2,1,0:T(8,128)(2,1)S(1)}, u32[]{:S(2)}, u32[]{:S(2)}) collective-permute-start(bf16[16,4,256,256]{3,2,1,0:T(8,128)(2,1)} %tiles_hbm.1), channel_id=1, source_target_pairs={{0,1},{1,0},{2,3},{3,2},{4,5},{5,4},{6,7},{7,6},{8,9},{9,8},{10,11... | collective-permute-start | bytes 25165832 | tf_op jit(solution)/shard_map/ppermute | solution.py:413
  2.1 45.1 %collective-permute-start.1 = (bf16[2560,128]{1,0:T(8,128)(2,1)S(1)}, bf16[2560,128]{1,0:T(8,128)(2,1)S(1)}, u32[]{:S(2)}, u32[]{:S(2)}) collective-permute-start(bf16[2560,128]{1,0:T(8,128)(2,1)S(1)} %get-tuple-element.22), channel_id=1, source_target_pairs={{0,2},{2,0},{4,6},{6,4},{8,10},{10,8},{12,14},{14,12},{16,18},{18,... | collective-permute-start | bytes 1966088 | tf_op jit(solution)/shard_map/ppermute | solution.py:413
  5.9 57.9 %collective-permute-start.2 = (bf16[2560,128]{1,0:T(8,128)(2,1)S(1)}, bf16[2560,128]{1,0:T(8,128)(2,1)S(1)}, u32[]{:S(2)}, u32[]{:S(2)}) collective-permute-start(bf16[2560,128]{1,0:T(8,128)(2,1)S(1)} %get-tuple-element.24), channel_id=1, source_target_pairs={{2,4},{6,8},{10,12},{14,16},{18,20},{22,24},{26,28},{4,2},{8,6},{1... | collective-permute-start | bytes 1966088 | tf_op jit(solution)/shard_map/ppermute | solution.py:413
  8.3 26.2 %collective-permute-start.3 = (bf16[192,128]{1,0:T(8,128)(2,1)S(1)}, bf16[192,128]{1,0:T(8,128)(2,1)S(1)}, u32[]{:S(2)}, u32[]{:S(2)}) collective-permute-start(bf16[192,128]{1,0:T(8,128)(2,1)S(1)} %get-tuple-element.27.pack), channel_id=1, source_target_pairs={{0,2},{2,0},{4,6},{6,4},{8,10},{10,8},{12,14},{14,12},{16,18},{18,... | collective-permute-start | bytes 147464 | tf_op jit(solution)/shard_map/ppermute | solution.py:413
  34.4 10.5 %collective-permute-start.4 = (bf16[320,128]{1,0:T(8,128)(2,1)S(1)}, bf16[320,128]{1,0:T(8,128)(2,1)S(1)}, u32[]{:S(2)}, u32[]{:S(2)}) collective-permute-start(bf16[320,128]{1,0:T(8,128)(2,1)S(1)} %get-tuple-element.28.pair), channel_id=1, source_target_pairs={{0,4},{2,6},{4,0},{6,2},{8,12},{10,14},{12,8},{14,10},{16,20},{18,... | collective-permute-start | bytes 245768 | tf_op jit(solution)/shard_map/ppermute | solution.py:413
  35.0 4.6 %collective-permute-start.7 = (bf16[64,128]{1,0:T(8,128)(2,1)S(1)}, bf16[64,128]{1,0:T(8,128)(2,1)S(1)}, u32[]{:S(2)}, u32[]{:S(2)}) collective-permute-start(bf16[64,128]{1,0:T(8,128)(2,1)S(1)} %get-tuple-element.29), channel_id=1, source_target_pairs={{0,16},{2,18},{4,20},{6,22},{8,24},{10,26},{12,28},{14,30},{16,0},... | collective-permute-start | bytes 49160 | tf_op jit(solution)/shard_map/ppermute | solution.py:413
  39.7 3.7 %collective-permute-start.8 = (bf16[64,128]{1,0:T(8,128)(2,1)S(1)}, bf16[64,128]{1,0:T(8,128)(2,1)S(1)}, u32[]{:S(2)}, u32[]{:S(2)}) collective-permute-start(bf16[64,128]{1,0:T(8,128)(2,1)S(1)} %get-tuple-element.29), channel_id=1, source_target_pairs={{0,24},{2,26},{4,28},{6,30},{8,16},{10,18},{12,20},{14,22},{16,8},... | collective-permute-start | bytes 49160 | tf_op jit(solution)/shard_map/ppermute | solution.py:413
  43.4 16.9 %collective-permute-start.9 = (bf16[128,128]{1,0:T(8,128)(2,1)S(1)}, bf16[128,128]{1,0:T(8,128)(2,1)S(1)}, u32[]{:S(2)}, u32[]{:S(2)}) collective-permute-start(bf16[128,128]{1,0:T(8,128)(2,1)S(1)} %shard_map.123.beyond0), channel_id=1, source_target_pairs={{0,4},{2,6},{4,0},{6,2},{8,12},{10,14},{12,8},{14,10},{16,20},{18,... | collective-permute-start | bytes 98312 | tf_op jit(solution)/shard_map/ppermute | solution.py:413
  44.9 15.4 %copy-start = (bf16[16,64,256]{2,1,0:T(8,128)(2,1)S(1)}, bf16[16,64,256]{2,1,0:T(8,128)(2,1)}, u32[]{:S(2)}) copy-start(bf16[16,64,256]{2,1,0:T(8,128)(2,1)} %basis_hbm.5) | copy-start | bytes 1572868
  44.9 15.4 %copy-start.1 = (bf16[16,64,256]{2,1,0:T(8,128)(2,1)S(1)}, bf16[16,64,256]{2,1,0:T(8,128)(2,1)}, u32[]{:S(2)}) copy-start(bf16[16,64,256]{2,1,0:T(8,128)(2,1)} %coupling_hbm.3) | copy-start | bytes 1572868
  45.0 15.4 %copy-start.2 = (bf16[2,64,512]{2,1,0:T(8,128)(2,1)S(1)}, bf16[2,64,512]{2,1,0:T(8,128)(2,1)}, u32[]{:S(2)}) copy-start(bf16[2,64,512]{2,1,0:T(8,128)(2,1)} %up_leaf.1) | copy-start | bytes 393220
  45.0 15.4 %copy-start.3 = (bf16[2,64,64]{2,1,0:T(8,128)(2,1)S(1)}, bf16[2,64,64]{2,1,0:T(8,128)(2,1)}, u32[]{:S(2)}) copy-start(bf16[2,64,64]{2,1,0:T(8,128)(2,1)} %up_mid.1) | copy-start | bytes 49156
  45.0 15.4 %copy-start.4 = (bf16[4,64,256]{2,1,0:T(8,128)(2,1)S(1)}, bf16[4,64,256]{2,1,0:T(8,128)(2,1)}, u32[]{:S(2)}) copy-start(bf16[4,64,256]{2,1,0:T(8,128)(2,1)} %top_coupling.1) | copy-start | bytes 393220
  45.0 15.3 %copy-start.5 = (bf16[2,64,256]{2,1,0:T(8,128)(2,1)S(1)}, bf16[2,64,256]{2,1,0:T(8,128)(2,1)}, u32[]{:S(2)}) copy-start(bf16[2,64,256]{2,1,0:T(8,128)(2,1)} %mid_coupling.1) | copy-start | bytes 196612
  45.0 15.3 %collective-permute-start.5 = (bf16[576,128]{1,0:T(8,128)(2,1)S(1)}, bf16[576,128]{1,0:T(8,128)(2,1)S(1)}, u32[]{:S(2)}, u32[]{:S(2)}) collective-permute-start(bf16[576,128]{1,0:T(8,128)(2,1)S(1)} %shard_map.122.plane), channel_id=1, source_target_pairs={{0,8},{2,10},{4,12},{6,14},{8,0},{10,2},{12,4},{14,6},{16,24},{18,... | collective-permute-start | bytes 442376 | tf_op jit(solution)/shard_map/ppermute | solution.py:413
  47.2 13.1 %collective-permute-start.6 = (bf16[576,128]{1,0:T(8,128)(2,1)S(1)}, bf16[576,128]{1,0:T(8,128)(2,1)S(1)}, u32[]{:S(2)}, u32[]{:S(2)}) collective-permute-start(bf16[576,128]{1,0:T(8,128)(2,1)S(1)} %shard_map.122.plane), channel_id=1, source_target_pairs={{8,16},{10,18},{12,20},{14,22},{16,8},{18,10},{20,12},{22,14},{9,1... | collective-permute-start | bytes 442376 | tf_op jit(solution)/shard_map/ppermute | solution.py:413
